TPU v7x, 32 devices: a whole 2x2x4 slice. The times are simulated.
32 devices in a mesh: lon: 4 (over y, x), lat: 8 (over z, core).
Axes of the slice: x: 2, y: 2, z: 4, core: 2. Of those that a mesh axis runs over, the one named last changes fastest.
Arguments:
- state_adjoint: float32 [4, 4, 512, 1024], P(None, None, 'lat', 'lon'), may hold values from -6 to 6
- east_velocity: float32 [4, 512, 1024], P(None, 'lat', 'lon'), may hold values from -1.2 to 1.2
- north_velocity: float32 [4, 512, 1024], P(None, 'lat', 'lon'), may hold values from -1.2 to 1.2
- ocean_mask: int32 [4, 512, 1024], P(None, 'lat', 'lon'), may hold values 0 or 1
- partner: int32 [1024], P('lon'), may hold values from 0 to 1023, as said below
Outputs:
- sensitivity: float32 [4, 4, 512, 1024], P(None, None, 'lat', 'lon')
Inputs may be any that keep to these rules, and one draw needn't show every extreme that they name: partner[i] = (c - i) mod 1024 with one c for all columns, 1023 <= c <= 1278; hence partner[partner[i]] = i.
All inputs are finite; a program needn't handle non-finite values. No bound on the sum of `ocean_mask` on one device may be relied on, other than what follows from the above.
Results may differ from a plain program's by a relative error of at most 0.00002.
Values sent between devices are 32-bit elements; how exact they have to be, the bound alone decides.
No kernel may reach another device: no remote copies, remote signals or barrier semaphores. Data moves between devices by JAX's collectives and lax.ppermute only.
A program may use at most 64 MiB of HBM per device.

v0:
```python
import jax
import jax.numpy as jnp
from jax import lax
from jax.sharding import PartitionSpec as P

STEPS = 2


def shifted(shard, axis, by):
    count = lax.axis_size(axis)
    return lax.ppermute(shard, axis, [(i, (i + by) % count) for i in range(count)])


def shifted_2(shard, axis, by):
    count = lax.axis_size(axis)
    pairs = [(i, i + by) for i in range(count) if 0 <= i + by < count]
    return lax.ppermute(shard, axis, pairs)


def with_halo(block, sides, width, periodic):
    for axis, dim in sides:
        count = lax.axis_size(axis)
        forward = [(i, i + 1) for i in range(count - 1)]
        if periodic:
            forward.append((count - 1, 0))
        backward = [(target, source) for source, target in forward]
        low = lax.ppermute(
            lax.slice_in_dim(block, block.shape[dim] - width, None, axis=dim), axis, forward
        )
        high = lax.ppermute(lax.slice_in_dim(block, 0, width, axis=dim), axis, backward)
        block = jnp.concatenate([low, block, high], axis=dim)
    return block


def per_device(state_adjoint, east_velocity, north_velocity, ocean_mask, partner):
    wet_cells = ocean_mask.astype(jnp.float32)
    fold_signs = jnp.array([1.0, 1.0, -1.0, -1.0], dtype=jnp.float32).reshape(4, 1, 1)
    lat_place = lax.axis_index("lat")
    lat_count = lax.axis_size("lat")
    is_top = (lat_place == lat_count - 1).astype(jnp.float32)
    speed_west_edge = shifted(east_velocity[:, :, -1:], "lon", 1)
    speed_south_edge = shifted_2(north_velocity[:, -1:, :], "lat", 1)
    west_speed = jnp.concatenate([speed_west_edge, east_velocity[:, :, :-1]], axis=2)
    south_speed = jnp.concatenate([speed_south_edge, north_velocity[:, :-1, :]], axis=1)
    fold_weight = 1.0 + north_velocity[:, -1, :]
    current = state_adjoint
    for iteration in range(STEPS):
        masked = wet_cells * current
        lon_padded = with_halo(masked, (("lon", 3),), 1, True)
        lat_padded = with_halo(masked, (("lat", 2),), 1, False)
        west_rim = lon_padded[:, :, :, 0]
        east_rim = lon_padded[:, :, :, -1]
        south_rim = lat_padded[:, :, 0, :]
        north_rim = lat_padded[:, :, -1, :]
        east_adj = jnp.concatenate([masked[..., 1:], east_rim[..., None]], axis=3)
        west_adj = jnp.concatenate([west_rim[..., None], masked[..., :-1]], axis=3)
        north_adj = jnp.concatenate([masked[:, :, 1:, :], north_rim[:, :, None, :]], axis=2)
        south_adj = jnp.concatenate([south_rim[:, :, None, :], masked[:, :, :-1, :]], axis=2)
        transport = (
            0.5 * east_velocity * (east_adj - masked)
            + 0.5 * west_speed * (masked - west_adj)
            + 0.5 * north_velocity * (north_adj - masked)
            + 0.5 * south_speed * (masked - south_adj)
        )
        fold_flux = fold_weight * masked[:, :, -1, :]
        whole_row = lax.all_gather(fold_flux, "lon", axis=2, tiled=True)
        picked = jnp.take(whole_row, partner, axis=2)
        folded = 0.5 * fold_signs * picked
        total = masked + transport
        total = total.at[:, :, -1, :].add(is_top * folded)
        current = wet_cells * total
    return current


def solution(mesh):
    placed = (
        P(None, None, "lat", "lon"),
        P(None, "lat", "lon"),
        P(None, "lat", "lon"),
        P(None, "lat", "lon"),
        P("lon"),
    )
    return jax.shard_map(
        per_device,
        mesh=mesh,
        in_specs=placed,
        out_specs=P(None, None, "lat", "lon"),
        check_vma=False,
    )
```

profile of v0, /device:TPU:10, one launch (start us, length us, event | category | flops | bytes accessed | tf_op | source)
XLA Modules:
  0.0 109.1 jit_solution(16763126374377405692)
XLA Ops:
  0.0 0.8 broadcast_add_fusion
  0.8 1.9 %collective-permute-start.4 = (f32[4,1,256]{2,1,0:T(1,128)S(1)}, f32[4,1,256]{2,1,0:T(1,128)S(1)}, u32[]{:S(2)}, u32[]{:S(2)}) collective-permute-start(f32[4,1,256]{2,1,0:T(1,128)S(1)} %get-tuple-element.47), channel_id=1, source_target_pairs={{0,1},{1,2},{2,3},{3,4},{4,5},{5,6},{6,7},{8,9},{9,10},{10,11},{11... | collective-permute-start | bytes 12296 | tf_op jit(solution)/shard_map/ppermute | solution.py:17
  2.7 1.7 %slice.119 = f32[4,64,1]{2,1,0:T(8,128)} slice(f32[4,64,256]{2,1,0:T(8,128)} %param.13), slice={[0:4], [0:64], [255:256]} | slice | bytes 2048 | tf_op jit(solution)/shard_map/slice | solution.py:41
  4.3 1.5 %collective-permute-start.1 = (f32[4,64,1]{2,1,0:T(8,128)}, f32[4,64,1]{2,1,0:T(8,128)}, u32[]{:S(2)}, u32[]{:S(2)}) collective-permute-start(f32[4,64,1]{2,1,0:T(8,128)} %slice.119), channel_id=1, source_target_pairs={{0,8},{8,16},{16,24},{24,0},{1,9},{9,17},{17,25},{25,1},{2,10},{10... | collective-permute-start | bytes 3080 | tf_op jit(solution)/shard_map/ppermute | solution.py:11
  5.8 1.0 convert_element_type.6
  6.8 0.2 copy.78
  7.0 0.0 copy-start.8
  7.0 0.0 copy-start.4
  7.0 0.0 copy-start.5
  7.0 2.1 %copy_multiply_fusion = f32[4,4,64,256]{3,1,0,2:T(4,128)S(1)} fusion(f32[4,4,64,256]{3,2,1,0:T(8,128)} %param.12, f32[4,64,256]{2,0,1:T(4,128)S(1)} %copy.78), kind=kLoop, calls=%fused_computation.26 | loop fusion | flops 262144 | bytes 2359296 | tf_op jit(solution)/shard_map/mul | solution.py:48
  9.1 3.3 %collective-permute-start.5 = (f32[4,4,1,256]{3,1,0,2:T(4,128)S(1)}, f32[4,4,1,256]{3,1,0,2:T(4,128)S(1)}, u32[]{:S(2)}, u32[]{:S(2)}) collective-permute-start(f32[4,4,1,256]{3,1,0,2:T(4,128)S(1)} %get-tuple-element.38), channel_id=1, source_target_pairs={{0,1},{1,2},{2,3},{3,4},{4,5},{5,6},{6,7},{8,9},{9,10},{10,11},{11... | collective-permute-start | bytes 49160 | tf_op jit(solution)/shard_map/ppermute | solution.py:27
  12.4 2.3 %collective-permute-start.3 = (f32[4,4,1,256]{3,1,0,2:T(4,128)S(1)}, f32[4,4,1,256]{3,1,0,2:T(4,128)S(1)}, u32[]{:S(2)}, u32[]{:S(2)}) collective-permute-start(f32[4,4,1,256]{3,1,0,2:T(4,128)S(1)} %get-tuple-element.39), channel_id=1, source_target_pairs={{1,0},{2,1},{3,2},{4,3},{5,4},{6,5},{7,6},{9,8},{10,9},{11,10},{12... | collective-permute-start | bytes 49160 | tf_op jit(solution)/shard_map/ppermute | solution.py:30
  14.7 1.3 %fusion.26 = (f32[4,4,64,1]{3,1,0,2:T(4,128)}, f32[4,4,64,1]{3,1,0,2:T(4,128)}) fusion(f32[4,4,64,256]{3,1,0,2:T(4,128)S(1)} %copy_multiply_fusion), kind=kLoop, calls=%fused_computation.54 | loop fusion | bytes 16384 | tf_op jit(solution)/shard_map/slice | solution.py:28
  16.0 1.5 %collective-permute-start.2 = (f32[4,4,64,1]{3,1,0,2:T(4,128)}, f32[4,4,64,1]{3,1,0,2:T(4,128)}, u32[]{:S(2)}, u32[]{:S(2)}) collective-permute-start(f32[4,4,64,1]{3,1,0,2:T(4,128)} %get-tuple-element.42), channel_id=1, source_target_pairs={{0,8},{8,16},{16,24},{24,0},{1,9},{9,17},{17,25},{25,1},{2,10},{10... | collective-permute-start | bytes 12296 | tf_op jit(solution)/shard_map/ppermute | solution.py:27
  17.5 0.5 compare_and_fusion
  18.1 1.8 %fusion.25 = (f32[4,4,63,256]{3,1,0,2:T(4,128)}, f32[4,4,63,256]{3,1,0,2:T(4,128)}) fusion(f32[4,4,64,256]{3,1,0,2:T(4,128)S(1)} %copy_multiply_fusion), kind=kLoop, calls=%fused_computation.53 | loop fusion | bytes 4128768 | tf_op jit(solution)/shard_map/slice | solution.py:58
  19.9 1.7 %fusion.27 = (f32[4,4,64,255]{3,1,0,2:T(4,128)S(1)}, f32[4,4,64,255]{3,1,0,2:T(4,128)}) fusion(f32[4,4,64,256]{3,1,0,2:T(4,128)S(1)} %copy_multiply_fusion), kind=kLoop, calls=%fused_computation.55 | loop fusion | bytes 4177920 | tf_op jit(solution)/shard_map/slice | solution.py:56
  21.6 12.3 %all_gather.6 = f32[4,4,1024]{2,1,0:T(4,128)S(1)} all-gather(f32[4,4,256]{2,1,0:T(4,128)S(1)} %bitcast_multiply_fusion.3), channel_id=1, replica_groups=mesh['lon'=4,'lat'=8] {'lon'}, dimensions={2}, use_global_device_ids=true | all-gather | bytes 81920 | tf_op jit(solution)/shard_map/all_gather | solution.py:66
  33.9 0.9 copy.80
  34.8 0.9 copy.82
  35.7 1.7 %copy.84 = f32[4,4,1024]{1,0,2:T(4,128)} copy(f32[4,4,1024]{2,1,0:T(4,128)S(1)} %all_gather.6) | data formatting | bytes 131072 | tf_op jit(solution)/shard_map/all_gather | solution.py:66
  37.4 2.6 %gather_fusion = f32[256,4,4]{2,1,0:T(4,128)S(1)} fusion(f32[4,4,1024]{1,0,2:T(4,128)} %copy.84, s32[1024]{0:T(1024)S(1)} %pad_clamp_fusion), kind=kCustom, calls=%fused_computation.clone | custom fusion | bytes 33792 | tf_op jit(solution)/shard_map/jit(_take)/gather | solution.py:67
  40.0 0.2 copy.85
  40.2 0.4 collective-permute-start
  40.6 1.0 maximum_multiply_fusion
  41.6 0.2 copy.81
  41.9 0.2 copy.83
  42.1 12.2 %collective-permute-done = f32[4,4,64,1]{3,1,0,2:T(4,128)S(1)} collective-permute-done((f32[4,4,64,1]{3,1,0,2:T(4,128)}, f32[4,4,64,1]{3,1,0,2:T(4,128)S(1)}, u32[]{:S(2)}, u32[]{:S(2)}) %collective-permute-start) | collective-permute-done | bytes 4128 | tf_op jit(solution)/shard_map/ppermute | solution.py:30
  54.3 0.0 copy-start.6
  54.4 4.6 %fusion.4 = f32[4,4,64,256]{3,1,0,2:T(4,128)S(1)} fusion(f32[4,4,64,1]{3,1,0,2:T(4,128)S(1)} %collective-permute-done, f32[4,4,64,255]{3,1,0,2:T(4,128)} %get-tuple-element.45, f32[4,4,64,255]{3,1,0,2:T(4,128)S(1)} %get-tuple-element.44, f32[4,4,64,1]{3,1,0,2:T(4,128)} %collective-permute-done.2, f32[4,4,1,256]{3,1,0,2:T(4,128)S(1)} %collective-permute-done.3, ...), kind=kLoop, calls=%fused_computation.7 | loop fusion | flops 4456448 | bytes 7602176 | tf_op jit(solution)/shard_map/add | solution.py:69
  59.0 0.1 fusion.17
  59.1 0.3 multiply_multiply_fusion
  59.5 1.4 %fusion.22 = (f32[4,4,64,1]{3,1,0,2:T(4,128)}, f32[4,4,64,1]{3,1,0,2:T(4,128)}) fusion(f32[4,4,64,256]{3,1,0,2:T(4,128)S(1)} %multiply_multiply_fusion), kind=kLoop, calls=%fused_computation.50 | loop fusion | bytes 16384 | tf_op jit(solution)/shard_map/slice | solution.py:28
  60.8 1.8 %fusion.21 = (f32[4,4,63,256]{3,1,0,2:T(4,128)}, f32[4,4,63,256]{3,1,0,2:T(4,128)}) fusion(f32[4,4,64,256]{3,1,0,2:T(4,128)S(1)} %multiply_multiply_fusion), kind=kLoop, calls=%fused_computation.49 | loop fusion | bytes 4128768 | tf_op jit(solution)/shard_map/slice | solution.py:58
  62.6 0.7 fusion.23
  63.4 1.9 %collective-permute-start.9 = (f32[4,4,1,256]{3,1,0,2:T(4,128)S(1)}, f32[4,4,1,256]{3,1,0,2:T(4,128)S(1)}, u32[]{:S(2)}, u32[]{:S(2)}) collective-permute-start(f32[4,4,1,256]{3,1,0,2:T(4,128)S(1)} %get-tuple-element.30), channel_id=1, source_target_pairs={{0,1},{1,2},{2,3},{3,4},{4,5},{5,6},{6,7},{8,9},{9,10},{10,11},{11... | collective-permute-start | bytes 49160 | tf_op jit(solution)/shard_map/ppermute | solution.py:27
  65.3 3.6 %collective-permute-start.8 = (f32[4,4,1,256]{3,1,0,2:T(4,128)S(1)}, f32[4,4,1,256]{3,1,0,2:T(4,128)S(1)}, u32[]{:S(2)}, u32[]{:S(2)}) collective-permute-start(f32[4,4,1,256]{3,1,0,2:T(4,128)S(1)} %get-tuple-element.31), channel_id=1, source_target_pairs={{1,0},{2,1},{3,2},{4,3},{5,4},{6,5},{7,6},{9,8},{10,9},{11,10},{12... | collective-permute-start | bytes 49160 | tf_op jit(solution)/shard_map/ppermute | solution.py:30
  69.0 0.4 collective-permute-start.7
  69.4 1.7 %collective-permute-start.6 = (f32[4,4,64,1]{3,1,0,2:T(4,128)}, f32[4,4,64,1]{3,1,0,2:T(4,128)}, u32[]{:S(2)}, u32[]{:S(2)}) collective-permute-start(f32[4,4,64,1]{3,1,0,2:T(4,128)} %get-tuple-element.35), channel_id=1, source_target_pairs={{8,0},{16,8},{24,16},{0,24},{9,1},{17,9},{25,17},{1,25},{10,2},{18... | collective-permute-start | bytes 12296 | tf_op jit(solution)/shard_map/ppermute | solution.py:30
  71.0 25.6 %all_gather.7 = f32[4,4,1024]{2,1,0:T(4,128)S(1)} all-gather(f32[4,4,256]{2,1,0:T(4,128)S(1)} %bitcast_multiply_fusion.1), channel_id=1, replica_groups=mesh['lon'=4,'lat'=8] {'lon'}, dimensions={2}, use_global_device_ids=true | all-gather | bytes 81920 | tf_op jit(solution)/shard_map/all_gather | solution.py:66
  96.7 1.7 %copy.86 = f32[4,4,1024]{1,0,2:T(4,128)} copy(f32[4,4,1024]{2,1,0:T(4,128)S(1)} %all_gather.7) | data formatting | bytes 131072 | tf_op jit(solution)/shard_map/all_gather | solution.py:66
  98.4 3.4 %gather_fusion.1 = f32[256,4,4]{2,1,0:T(4,128)} fusion(f32[4,4,1024]{1,0,2:T(4,128)} %copy.86, s32[1024]{0:T(1024)S(1)} %pad_clamp_fusion), kind=kCustom, calls=%fused_computation.1.clone | custom fusion | bytes 33792 | tf_op jit(solution)/shard_map/jit(_take)/gather | solution.py:67
  101.7 1.2 %copy.87 = f32[256,4,4]{0,2,1:T(4,128)S(1)} copy(f32[256,4,4]{2,1,0:T(4,128)} %gather_fusion.1) | data formatting | bytes 32768 | tf_op jit(solution)/shard_map/jit(_take)/gather | solution.py:67
  103.0 0.0 collective-permute-done.9
  103.0 4.1 %fusion.12 = f32[4,4,64,256]{3,1,0,2:T(4,128)S(1)} fusion(f32[4,4,64,1]{3,1,0,2:T(4,128)} %collective-permute-done.6, f32[4,4,64,255]{3,1,0,2:T(4,128)S(1)} %get-tuple-element.37, f32[4,4,64,255]{3,1,0,2:T(4,128)S(1)} %get-tuple-element.36, f32[4,4,64,1]{3,1,0,2:T(4,128)} %collective-permute-done.7, f32[4,4,1,256]{3,1,0,2:T(4,128)S(1)} %collective-permute-done.8, ...), kind=kLoop, calls=%fused_computation.19 | loop fusion | flops 4718592 | bytes 7602176 | tf_op jit(solution)/shard_map/add | solution.py:69
  107.1 0.1 fusion.16
  107.2 0.3 broadcast_multiply_fusion
  107.5 1.6 %copy.88 = f32[4,4,64,256]{3,2,1,0:T(8,128)} copy(f32[4,4,64,256]{3,1,0,2:T(4,128)S(1)} %broadcast_multiply_fusion) | data formatting | bytes 2097152 | tf_op jit(solution)/shard_map/mul | solution.py:71
  (32 shorter events, 0.2 us)
Async XLA Ops:
  0.8 41.1 %collective-permute-start.4 = (f32[4,1,256]{2,1,0:T(1,128)S(1)}, f32[4,1,256]{2,1,0:T(1,128)S(1)}, u32[]{:S(2)}, u32[]{:S(2)}) collective-permute-start(f32[4,1,256]{2,1,0:T(1,128)S(1)} %get-tuple-element.47), channel_id=1, source_target_pairs={{0,1},{1,2},{2,3},{3,4},{4,5},{5,6},{6,7},{8,9},{9,10},{10,11},{11... | collective-permute-start | bytes 12296 | tf_op jit(solution)/shard_map/ppermute | solution.py:17
  4.3 35.8 %collective-permute-start.1 = (f32[4,64,1]{2,1,0:T(8,128)}, f32[4,64,1]{2,1,0:T(8,128)}, u32[]{:S(2)}, u32[]{:S(2)}) collective-permute-start(f32[4,64,1]{2,1,0:T(8,128)} %slice.119), channel_id=1, source_target_pairs={{0,8},{8,16},{16,24},{24,0},{1,9},{9,17},{17,25},{25,1},{2,10},{10... | collective-permute-start | bytes 3080 | tf_op jit(solution)/shard_map/ppermute | solution.py:11
  7.0 10.5 %copy-start.8 = (s32[256]{0:T(256)S(1)}, s32[256]{0:T(256)}, u32[]{:S(2)}) copy-start(s32[256]{0:T(256)} %param.16) | copy-start | bytes 3076
  7.0 11.0 %copy-start.4 = (f32[4,64,256]{2,1,0:T(8,128)S(1)}, f32[4,64,256]{2,1,0:T(8,128)}, u32[]{:S(2)}) copy-start(f32[4,64,256]{2,1,0:T(8,128)} %param.13) | copy-start | bytes 786436
  7.0 11.0 %copy-start.5 = (f32[4,64,256]{2,1,0:T(8,128)S(1)}, f32[4,64,256]{2,1,0:T(8,128)}, u32[]{:S(2)}) copy-start(f32[4,64,256]{2,1,0:T(8,128)} %param.14) | copy-start | bytes 786436
  9.1 45.2 %collective-permute-start.5 = (f32[4,4,1,256]{3,1,0,2:T(4,128)S(1)}, f32[4,4,1,256]{3,1,0,2:T(4,128)S(1)}, u32[]{:S(2)}, u32[]{:S(2)}) collective-permute-start(f32[4,4,1,256]{3,1,0,2:T(4,128)S(1)} %get-tuple-element.38), channel_id=1, source_target_pairs={{0,1},{1,2},{2,3},{3,4},{4,5},{5,6},{6,7},{8,9},{9,10},{10,11},{11... | collective-permute-start | bytes 49160 | tf_op jit(solution)/shard_map/ppermute | solution.py:27
  12.4 41.9 %collective-permute-start.3 = (f32[4,4,1,256]{3,1,0,2:T(4,128)S(1)}, f32[4,4,1,256]{3,1,0,2:T(4,128)S(1)}, u32[]{:S(2)}, u32[]{:S(2)}) collective-permute-start(f32[4,4,1,256]{3,1,0,2:T(4,128)S(1)} %get-tuple-element.39), channel_id=1, source_target_pairs={{1,0},{2,1},{3,2},{4,3},{5,4},{6,5},{7,6},{9,8},{10,9},{11,10},{12... | collective-permute-start | bytes 49160 | tf_op jit(solution)/shard_map/ppermute | solution.py:30
  16.0 26.0 %collective-permute-start.2 = (f32[4,4,64,1]{3,1,0,2:T(4,128)}, f32[4,4,64,1]{3,1,0,2:T(4,128)}, u32[]{:S(2)}, u32[]{:S(2)}) collective-permute-start(f32[4,4,64,1]{3,1,0,2:T(4,128)} %get-tuple-element.42), channel_id=1, source_target_pairs={{0,8},{8,16},{16,24},{24,0},{1,9},{9,17},{17,25},{25,1},{2,10},{10... | collective-permute-start | bytes 12296 | tf_op jit(solution)/shard_map/ppermute | solution.py:27
  35.7 18.7 %copy-start = (f32[4,4,64,256]{3,2,1,0:T(8,128)S(1)}, f32[4,4,64,256]{3,2,1,0:T(8,128)}, u32[]{:S(2)}) copy-start(f32[4,4,64,256]{3,2,1,0:T(8,128)} %param.12) | copy-start | bytes 3145732
  40.2 14.2 %copy-start.1 = (f32[4,64,256]{2,0,1:T(4,128)S(1)}, f32[4,64,256]{2,0,1:T(4,128)}, u32[]{:S(2)}) copy-start(f32[4,64,256]{2,0,1:T(4,128)} %copy.82) | copy-start | bytes 786436
  40.2 14.1 %collective-permute-start = (f32[4,4,64,1]{3,1,0,2:T(4,128)}, f32[4,4,64,1]{3,1,0,2:T(4,128)S(1)}, u32[]{:S(2)}, u32[]{:S(2)}) collective-permute-start(f32[4,4,64,1]{3,1,0,2:T(4,128)} %get-tuple-element.43), channel_id=1, source_target_pairs={{8,0},{16,8},{24,16},{0,24},{9,1},{17,9},{25,17},{1,25},{10,2},{18... | collective-permute-start | bytes 12296 | tf_op jit(solution)/shard_map/ppermute | solution.py:30
  41.8 17.2 %copy-start.2 = (f32[4,64,256]{2,0,1:T(4,128)}, f32[4,64,256]{2,0,1:T(4,128)S(1)}, u32[]{:S(2)}) copy-start(f32[4,64,256]{2,0,1:T(4,128)S(1)} %copy.81) | copy-start | bytes 786436
  42.1 17.0 %copy-start.3 = (f32[4,64,256]{2,0,1:T(4,128)}, f32[4,64,256]{2,0,1:T(4,128)S(1)}, u32[]{:S(2)}) copy-start(f32[4,64,256]{2,0,1:T(4,128)S(1)} %copy.83) | copy-start | bytes 786436
  54.3 4.7 %copy-start.6 = (f32[4]{0:T(128)S(1)}, f32[4]{0:T(128)}, u32[]{:S(2)}) copy-start(f32[4]{0:T(128)} %constant.73) | copy-start | bytes 52
  54.4 4.7 %copy-start.7 = (pred[256]{0:T(512)(128)(4,1)S(1)}, pred[256]{0:T(512)(128)(4,1)}, u32[]{:S(2)}) copy-start(pred[256]{0:T(512)(128)(4,1)} %compare_and_fusion) | copy-start | bytes 772
  63.4 39.6 %collective-permute-start.9 = (f32[4,4,1,256]{3,1,0,2:T(4,128)S(1)}, f32[4,4,1,256]{3,1,0,2:T(4,128)S(1)}, u32[]{:S(2)}, u32[]{:S(2)}) collective-permute-start(f32[4,4,1,256]{3,1,0,2:T(4,128)S(1)} %get-tuple-element.30), channel_id=1, source_target_pairs={{0,1},{1,2},{2,3},{3,4},{4,5},{5,6},{6,7},{8,9},{9,10},{10,11},{11... | collective-permute-start | bytes 49160 | tf_op jit(solution)/shard_map/ppermute | solution.py:27
  65.3 37.7 %collective-permute-start.8 = (f32[4,4,1,256]{3,1,0,2:T(4,128)S(1)}, f32[4,4,1,256]{3,1,0,2:T(4,128)S(1)}, u32[]{:S(2)}, u32[]{:S(2)}) collective-permute-start(f32[4,4,1,256]{3,1,0,2:T(4,128)S(1)} %get-tuple-element.31), channel_id=1, source_target_pairs={{1,0},{2,1},{3,2},{4,3},{5,4},{6,5},{7,6},{9,8},{10,9},{11,10},{12... | collective-permute-start | bytes 49160 | tf_op jit(solution)/shard_map/ppermute | solution.py:30
  69.0 34.0 %collective-permute-start.7 = (f32[4,4,64,1]{3,1,0,2:T(4,128)}, f32[4,4,64,1]{3,1,0,2:T(4,128)}, u32[]{:S(2)}, u32[]{:S(2)}) collective-permute-start(f32[4,4,64,1]{3,1,0,2:T(4,128)} %get-tuple-element.34), channel_id=1, source_target_pairs={{0,8},{8,16},{16,24},{24,0},{1,9},{9,17},{17,25},{25,1},{2,10},{10... | collective-permute-start | bytes 12296 | tf_op jit(solution)/shard_map/ppermute | solution.py:27
  69.4 33.6 %collective-permute-start.6 = (f32[4,4,64,1]{3,1,0,2:T(4,128)}, f32[4,4,64,1]{3,1,0,2:T(4,128)}, u32[]{:S(2)}, u32[]{:S(2)}) collective-permute-start(f32[4,4,64,1]{3,1,0,2:T(4,128)} %get-tuple-element.35), channel_id=1, source_target_pairs={{8,0},{16,8},{24,16},{0,24},{9,1},{17,9},{25,17},{1,25},{10,2},{18... | collective-permute-start | bytes 12296 | tf_op jit(solution)/shard_map/ppermute | solution.py:30
where the time goes:
time: 110 us; the launch traced here: 109 us
  blocking collectives  37.9 us (34%)
  local copies, waits for them, and re-layouts  25.1 us (23%)
  starting transfers between devices  18.5 us (17%)
  other arithmetic  14.9 us (14%)
  waiting for transfers between devices  12.3 us (11%)
    all_gather x2, blocking collectives, per_device(): whole_row = lax.all_gather(fold_flux, 'lon', axis=2, tiled=True)  37.9 us
    ppermute x4, waiting for transfers between devices, with_halo(): lax.ppermute(lax.slice_in_dim(block, 0, width, axis=dim), axis, backward)  12.2 us
    add x2, other arithmetic, per_device(): total = masked + transport  8.75 us
    ppermute x4, starting transfers between devices, with_halo(): lax.ppermute(lax.slice_in_dim(block, 0, width, axis=dim), axis, backward)  8 us
    gather x4, local copies, waits for them, and re-layouts, per_device(): picked = jnp.take(whole_row, partner, axis=2)  7.39 us
    ppermute x4, starting transfers between devices, with_halo(): lax.ppermute(lax.slice_in_dim(block, block.shape[dim] - width, None, axis...  7.11 us
    slice x2, local copies, waits for them, and re-layouts, per_device(): masked[:, :, :-1, :]  3.65 us
    all_gather x2, local copies, waits for them, and re-layouts, per_device(): whole_row = lax.all_gather(fold_flux, 'lon', axis=2, tiled=True)  3.41 us
  transfers between devices with their start and end apart: 10, of which 1 were waited for; matrix products, arithmetic and copies ran while one was open for 22% of the time, Pallas kernels for 0%

commit v1 on v0

v1 whole, which is shorter than its diff:
```python
import functools

import jax
import jax.numpy as jnp
from jax import lax
from jax.experimental import pallas as pl
from jax.experimental.pallas import tpu as pltpu
from jax.sharding import PartitionSpec as P

FIELDS = 4
QU, QV, QW, QN = 4, 5, 6, 7
LANES, SUBS = 128, 8


def iota(dim):
    return lax.broadcasted_iota(jnp.int32, (SUBS, LANES), dim)


def place():
    lon, lat = lax.axis_index("lon"), lax.axis_index("lat")
    return lon, lon % 2 == 0, lat % 2 == 0, lat == lax.axis_size("lat") - 1


def row_kernel(levels, s_lo, s_hi, u_lo, u_hi, v_lo, v_hi, m_lo, m_hi, a_ref, b_ref):
    _, _, lat_even, _ = place()
    for l in range(levels):
        lo_w = m_lo[l, 0:2, :].astype(jnp.float32)
        hi_w = m_hi[l, 6:8, :].astype(jnp.float32)
        pairs = [(s_lo[f, l, 0:2, :] * lo_w, s_hi[f, l, 6:8, :] * hi_w) for f in range(FIELDS)]
        pairs += [(u_lo[l, 0:2, :], u_hi[l, 6:8, :]), (v_lo[l, 0:2, :], v_hi[l, 6:8, :]), (lo_w, hi_w)]
        pairs += [(jnp.zeros_like(lo_w), jnp.zeros_like(lo_w))]
        for q, (lo, hi) in enumerate(pairs):
            at = pl.ds(16 * l + 2 * q, 2)
            a_ref[at, :] = jnp.where(lat_even, hi, lo)
            b_ref[at, :] = jnp.where(lat_even, lo, hi)


def column_kernel(s_ref, u_ref, v_ref, m_ref, a_ref, b_ref, p_ref, q_ref, halo):
    l = pl.program_id(0)
    _, lon_even, lat_even, top = place()
    lane, sub = iota(1), iota(0)
    tiles = s_ref.shape[2] // SUBS
    last = s_ref.shape[3] - LANES
    halo[...] = jnp.zeros_like(halo)
    for q in range(QN):
        a, b = a_ref[2 * q : 2 * q + 2, :], b_ref[2 * q : 2 * q + 2, :]
        halo[q, 0:2, :] = jnp.where(lat_even, a, b)
        halo[q, 6:8, :] = jnp.where(lat_even, b, a)
    for t in range(tiles + 1):
        east = jnp.zeros((SUBS, LANES), jnp.float32)
        west = jnp.zeros((SUBS, LANES), jnp.float32)
        rows = pl.ds(SUBS * t, SUBS)
        if t < tiles:
            w0 = m_ref[0, rows, 0:LANES].astype(jnp.float32)
            w1 = m_ref[0, rows, last : last + LANES].astype(jnp.float32)
        for q in range(QN):
            if t == tiles:
                first, end = halo[q, :, 0:LANES], halo[q, :, last : last + LANES]
                first = jnp.where(top & (sub < 2), pltpu.roll(end, 1, 1), first)
            elif q < FIELDS:
                first, end = s_ref[q, 0, rows, 0:LANES] * w0, s_ref[q, 0, rows, last : last + LANES] * w1
            elif q == QW:
                first, end = w0, w1
            else:
                ref = u_ref if q == QU else v_ref
                first, end = ref[0, rows, 0:LANES], ref[0, rows, last : last + LANES]
            here = lane // 2 == q
            west = jnp.where(here, pltpu.roll(first, 2 * q, 1) if q else first, west)
            east = jnp.where(here, pltpu.roll(end, 2 * q + 2, 1), east)
        mine = lane // 16 == l
        for ref, pack in ((p_ref, jnp.where(lon_even, east, west)), (q_ref, jnp.where(lon_even, west, east))):
            ref[rows, :] = jnp.where(mine, pltpu.roll(pack, 16 * l, 1), ref[rows, :])


def step_kernel(c_ref, s_ref, u_ref, v_ref, m_ref, a_ref, b_ref, f_ref, p_ref, q_ref, o_ref, hu, hv, wt, mir, r0, r1):
    l = pl.program_id(0)
    lon, lon_even, lat_even, top = place()
    lane, sub = iota(1), iota(0)
    tiles, width = s_ref.shape[2] // SUBS, s_ref.shape[3]
    cols = width // LANES
    ncol = lax.axis_size("lon") * width
    shift = lax.rem(c_ref[0] + lon * width + 1, ncol)

    def at(t, c):
        return pl.ds(SUBS * t, SUBS), pl.ds(LANES * c, LANES)

    @pl.when(top)
    def _():
        for c in range(cols + 1):
            i = LANES * c + lane
            if c == cols:
                i = jnp.where(lane < LANES // 2, i, lane - LANES)
            for g in range(2):
                p = shift + (width - 1) - i
                if g == 1:
                    p = jnp.where(sub < 2, p - 1, p)
                p = jnp.clip(p, 0, 2 * width - 1)
                got = jnp.zeros((SUBS, LANES), jnp.float32)
                for s in range(2 * cols):
                    src = b_ref if s < cols else f_ref
                    tile = src[pl.ds(SUBS * g, SUBS), pl.ds(LANES * (s % cols), LANES)]
                    picked = jnp.take_along_axis(tile, p % LANES, axis=1, mode="promise_in_bounds")
                    got = jnp.where(p // LANES == s, picked, got)
                mir[pl.ds(SUBS * g, SUBS), pl.ds(LANES * c, LANES)] = got

    def halo_tiles(q):
        side = []
        for t in range(tiles + 1):
            p, w = p_ref[pl.ds(SUBS * t, SUBS), :], q_ref[pl.ds(SUBS * t, SUBS), :]
            e, w = jnp.where(lon_even, p, w), jnp.where(lon_even, w, p)
            back = 16 * l + 2 * q
            e, w = pltpu.roll(e, LANES - back, 1), pltpu.roll(w, LANES + 126 - back, 1)
            side.append(jnp.where(lane < LANES // 2, e, w))
            corner = e
        out = []
        for c in range(cols + 1):
            if c < cols:
                a, b = (ref[2 * q : 2 * q + 2, LANES * c : LANES * c + LANES] for ref in (a_ref, b_ref))
                n, s = jnp.where(lat_even, a, b), jnp.where(lat_even, b, a)
                zero = jnp.zeros((4, LANES), jnp.float32)
                tile = jnp.concatenate([n, zero, s], axis=0)
            else:
                tile = side[tiles]
            second, first = (
                jnp.broadcast_to(mir[2 * q + k : 2 * q + k + 1, LANES * c : LANES * c + LANES], (SUBS, LANES))
                for k in range(2)
            )
            seam = jnp.broadcast_to(corner[1:2, 0:1], (SUBS, LANES))
            if c == cols and q != QU:
                first = jnp.where((shift == 0) & (lane == 0), seam, first)
            if c == cols - 1 and q == QU:
                first = jnp.where((shift == 0) & (lane == LANES - 1), seam, first)
            if q == QU:
                first = -first
            if q == QV:
                second, first = first, -second
            tile = jnp.where(top & (sub == 0), first, tile)
            tile = jnp.where(top & (sub == 1), second, tile)
            out.append(tile)
        return out, side[:tiles]

    own = {QU: (u_ref, hu), QV: (v_ref, hv), QW: (m_ref, wt)}
    for q in range(FIELDS):
        own[q] = (s_ref, r0.at[q])
    for q in (QW, QU, QV, 0, 1, 2, 3):
        src, dst = own[q]
        halo, side = halo_tiles(q)
        half = q in (QU, QV)
        for c in range(cols + 1):
            dst[at(tiles, c)] = 0.5 * halo[c] if half else halo[c]
        for t in range(tiles):
            dst[at(t, cols)] = 0.5 * side[t] if half else side[t]
            for c in range(cols):
                if q < FIELDS:
                    dst[at(t, c)] = src[(q, 0) + at(t, c)] * wt[at(t, c)]
                elif q == QW:
                    dst[at(t, c)] = src[(0,) + at(t, c)].astype(jnp.float32)
                else:
                    dst[at(t, c)] = 0.5 * src[(0,) + at(t, c)]

    east_edge, west_edge = lane == 0, lane == LANES - 1
    north_edge, south_edge = sub == 0, sub == SUBS - 1
    top_row, mirror_row = top & (sub == SUBS - 1), top & (sub == 0)
    ring = cols + 1

    def north_of(here, above):
        return pltpu.roll(jnp.where(north_edge, above, here), SUBS - 1, 0)

    def south_of(here, below):
        return pltpu.roll(jnp.where(south_edge, below, here), 1, 0)

    def step(field, src, row_tiles, columns, store):
        sign = 1.0 if field < 2 else -1.0
        low = [None] * ring
        for c in columns:
            r = src[at(tiles, c)]
            low[c] = hv[at(tiles, c)] * (north_of(r, src[at(0, c)]) - r)
        for t in row_tiles:
            now = [src[at(t, c)] for c in range(ring)]
            flux = []
            for c in range(ring):
                ahead = pltpu.roll(jnp.where(east_edge, now[(c + 1) % ring], now[c]), LANES - 1, 1)
                flux.append(hu[at(t, c)] * (ahead - now[c]))
            for c in columns:
                back = pltpu.roll(jnp.where(west_edge, flux[(c - 1) % ring], flux[c]), 1, 1)
                r, h = now[c], hv[at(t, c)]
                above = north_of(r, src[at((t + 1) % (tiles + 1), c)])
                up = h * (above - r)
                down = south_of(up, low[c])
                low[c] = up
                if t == tiles - 1:
                    met = pltpu.roll(hv[at(tiles, c)], SUBS - 2, 0)
                    up = jnp.where(top_row, sign * (0.5 + met) * above - h * r, up)
                if t == tiles:
                    met, edge = pltpu.roll(h, SUBS - 1, 0), pltpu.roll(hv[at(tiles - 1, c)], 1, 0)
                    below = pltpu.roll(src[at(tiles - 1, c)], 1, 0)
                    down = jnp.where(mirror_row, sign * (0.5 + edge) * below - met * r, down)
                store(t, c, wt[at(t, c)] * (r + flux[c] + back + up + down))

    for f in range(FIELDS):

        def keep(t, c, value, f=f):
            r1[(f,) + at(t, c)] = value

        def give(t, c, value, f=f):
            o_ref[(f, 0) + at(t, c)] = value

        step(f, r0.at[f], range(tiles + 1), range(ring), keep)
        step(f, r1.at[f], range(tiles), range(cols), give)


def per_device(state_adjoint, east_velocity, north_velocity, ocean_mask, partner):
    nlon, nlat = lax.axis_size("lon"), lax.axis_size("lat")
    fields, levels, rows, width = state_adjoint.shape
    axes = ("lon", "lat")

    def device(lon, lat):
        return lon % nlon * nlat + lat

    def both(a, b):
        return [(a, b), (b, a)]

    fold = [(device(nlon - 1 - i, nlat - 1), device(i, nlat - 1)) for i in range(nlon)]
    fold_next = [(device(nlon - i, nlat - 1), device(i, nlat - 1)) for i in range(nlon)]
    within = [e for i in range(nlon) for j in range(0, nlat, 2) for e in both(device(i, j), device(i, j + 1))]
    across = [e for i in range(nlon) for j in range(1, nlat - 1, 2) for e in both(device(i, j), device(i, j + 1))]
    even = [e for i in range(0, nlon, 2) for j in range(nlat) for e in both(device(i, j), device(i + 1, j))]
    odd = [e for i in range(1, nlon, 2) for j in range(nlat) for e in both(device(i, j), device(i + 1, j))]

    f32 = jnp.float32
    last = rows // SUBS - 1
    tile4 = [pl.BlockSpec((fields, levels, SUBS, width), lambda _, k=k: (0, 0, k, 0)) for k in (0, last)]
    tile3 = [pl.BlockSpec((levels, SUBS, width), lambda _, k=k: (0, k, 0)) for k in (0, last)]
    message = jax.ShapeDtypeStruct((16 * levels, width), f32)
    to_a, to_b = pl.pallas_call(
        functools.partial(row_kernel, levels),
        grid=(1,),
        out_shape=(message, message),
        in_specs=tile4 + tile3 * 3,
        name="pack_rows",
    )(
        state_adjoint, state_adjoint, east_velocity, east_velocity, north_velocity, north_velocity, ocean_mask, ocean_mask
    )
    from_a = lax.ppermute(to_a, axes, within)
    from_b = lax.ppermute(to_b, axes, across + fold)
    from_f = lax.ppermute(to_b, axes, fold_next)

    level4 = pl.BlockSpec((fields, 1, rows, width), lambda l: (0, l, 0, 0))
    level3 = pl.BlockSpec((1, rows, width), lambda l: (l, 0, 0))
    level2 = pl.BlockSpec((16, width), lambda l: (l, 0))
    column = pl.BlockSpec((rows + SUBS, LANES), lambda l: (0, 0))
    packed = jax.ShapeDtypeStruct((rows + SUBS, LANES), f32)
    to_p, to_q = pl.pallas_call(
        column_kernel,
        grid=(levels,),
        out_shape=(packed, packed),
        in_specs=[level4, level3, level3, level3, level2, level2],
        out_specs=(column, column),
        scratch_shapes=[pltpu.VMEM((QN, SUBS, width), f32)],
        name="pack_columns",
    )(state_adjoint, east_velocity, north_velocity, ocean_mask, from_a, from_b)
    from_p = lax.ppermute(to_p, axes, even)
    from_q = lax.ppermute(to_q, axes, odd)

    ext = (rows + SUBS, width + LANES)
    return pl.pallas_call(
        step_kernel,
        grid=(levels,),
        out_shape=jax.ShapeDtypeStruct(state_adjoint.shape, f32),
        in_specs=[pl.BlockSpec(memory_space=pltpu.SMEM), level4, level3, level3, level3, level2, level2, level2, column, column],
        out_specs=level4,
        scratch_shapes=[
            pltpu.VMEM(ext, f32),
            pltpu.VMEM(ext, f32),
            pltpu.VMEM(ext, f32),
            pltpu.VMEM((16, width + LANES), f32),
            pltpu.VMEM((fields,) + ext, f32),
            pltpu.VMEM((fields,) + ext, f32),
        ],
        name="both_steps",
    )(partner, state_adjoint, east_velocity, north_velocity, ocean_mask, from_a, from_b, from_f, from_p, from_q)


def solution(mesh):
    placed = (
        P(None, None, "lat", "lon"),
        P(None, "lat", "lon"),
        P(None, "lat", "lon"),
        P(None, "lat", "lon"),
        P("lon"),
    )
    return jax.shard_map(
        per_device,
        mesh=mesh,
        in_specs=placed,
        out_specs=P(None, None, "lat", "lon"),
        check_vma=False,
    )
```

time: 110 us -> 33.6 us (0.31)
  the two profiles are of different devices: /device:TPU:10 before, /device:TPU:25 now
where the time goes in v1:
time: 33.6 us; the launch traced here: 33.2 us
  Pallas kernels  20.1 us (60%)
  starting transfers between devices  8.58 us (26%)
  waiting for transfers between devices  3.24 us (10%)
  local copies, waits for them, and re-layouts  1.32 us (4%)
    pallas_call x1, Pallas kernels, per_device(): pl.pallas_call(step_kernel, grid=(levels,), out_shape=jax.ShapeDtypeStruc...  14.7 us
    ppermute x1, starting transfers between devices, per_device(): from_b = lax.ppermute(to_b, axes, across + fold)  4.06 us
    pallas_call x1, Pallas kernels, per_device(): pl.pallas_call(column_kernel, grid=(levels,), out_shape=(packed, packed),...  3.61 us
    pallas_call x1, Pallas kernels, per_device(): pl.pallas_call(functools.partial(row_kernel, levels), grid=(1,), out_shap...  1.73 us
    ppermute x1, starting transfers between devices, per_device(): from_f = lax.ppermute(to_b, axes, fold_next)  1.5 us
    ppermute x1, waiting for transfers between devices, per_device(): from_q = lax.ppermute(to_q, axes, odd)  1.4 us
    unnamed x10, local copies, waits for them, and re-layouts  1.32 us
    ppermute x1, waiting for transfers between devices, per_device(): from_p = lax.ppermute(to_p, axes, even)  1.3 us
  transfers between devices with their start and end apart: 5, of which 3 were waited for; matrix products, arithmetic and copies ran while one was open for 0% of the time, Pallas kernels for 11%

profile of v1, /device:TPU:25, one launch (start us, length us, event | category | flops | bytes accessed | tf_op | source)
XLA Modules:
  0.0 33.2 jit_solution(9664063458496446436)
XLA Ops:
  0.0 1.7 %pack_rows.1 = (f32[64,256]{1,0:T(8,128)}, f32[64,256]{1,0:T(8,128)}) custom-call(f32[4,4,64,256]{3,2,1,0:T(8,128)} %s_ref.3, f32[4,4,64,256]{3,2,1,0:T(8,128)} %s_ref.3, f32[4,64,256]{2,1,0:T(8,128)} %u_ref.3, f32[4,64,256]{2,1,0:T(8,128)} %u_ref.3, f32[4,64,256]{2,1,0:T(8,128)} %v_ref.3, f32[4,64,256]{2,1,0:T(8,128)} %v_ref.3, s32[4,64,256]{2,1,0:T(8,128)} %m_ref.3, ...), custom_call_target="tpu_custom_call" | custom-call | tf_op jit(solution)/shard_map/pack_rows/pallas_call | solution.py:235
  1.7 0.7 %collective-permute-start = (f32[64,256]{1,0:T(8,128)}, f32[64,256]{1,0:T(8,128)S(1)}, u32[]{:S(2)}, u32[]{:S(2)}) collective-permute-start(f32[64,256]{1,0:T(8,128)} %get-tuple-element.9), channel_id=1, source_target_pairs={{0,1},{1,0},{2,3},{3,2},{4,5},{5,4},{6,7},{7,6},{8,9},{9,8},{10,11... | collective-permute-start | bytes 196616 | tf_op jit(solution)/shard_map/ppermute | solution.py:244
  2.4 4.1 %collective-permute-start.1 = (f32[64,256]{1,0:T(8,128)}, f32[64,256]{1,0:T(8,128)S(1)}, u32[]{:S(2)}, u32[]{:S(2)}) collective-permute-start(f32[64,256]{1,0:T(8,128)} %get-tuple-element.10), channel_id=1, source_target_pairs={{1,2},{2,1},{3,4},{4,3},{5,6},{6,5},{9,10},{10,9},{11,12},{12,11},... | collective-permute-start | bytes 196616 | tf_op jit(solution)/shard_map/ppermute | solution.py:245
  6.5 1.5 %collective-permute-start.2 = (f32[64,256]{1,0:T(8,128)}, f32[64,256]{1,0:T(8,128)S(1)}, u32[]{:S(2)}, u32[]{:S(2)}) collective-permute-start(f32[64,256]{1,0:T(8,128)} %get-tuple-element.10), channel_id=1, source_target_pairs={{7,7},{31,15},{23,23},{15,31}} | collective-permute-start | bytes 196616 | tf_op jit(solution)/shard_map/ppermute | solution.py:246
  8.0 0.0 collective-permute-done.a_ref
  8.0 0.0 copy-start
  8.0 0.5 %collective-permute-done.1.b_ref = f32[64,256]{1,0:T(8,128)S(1)} collective-permute-done((f32[64,256]{1,0:T(8,128)}, f32[64,256]{1,0:T(8,128)S(1)}, u32[]{:S(2)}, u32[]{:S(2)}) %collective-permute-start.1) | collective-permute-done | bytes 65568 | tf_op jit(solution)/shard_map/ppermute | solution.py:245
  8.5 0.1 copy-done
  8.6 0.0 copy-start.1
  8.6 0.6 %copy-done.1 = f32[64,256]{1,0:T(8,128)} copy-done((f32[64,256]{1,0:T(8,128)}, f32[64,256]{1,0:T(8,128)S(1)}, u32[]{:S(2)}) %copy-start.1) | copy-done | bytes 65560
  9.2 3.6 %pack_columns.1 = (f32[72,128]{1,0:T(8,128)}, f32[72,128]{1,0:T(8,128)}) custom-call(f32[4,4,64,256]{3,2,1,0:T(8,128)} %s_ref.3, f32[4,64,256]{2,1,0:T(8,128)} %u_ref.3, f32[4,64,256]{2,1,0:T(8,128)} %v_ref.3, s32[4,64,256]{2,1,0:T(8,128)} %m_ref.3, f32[64,256]{1,0:T(8,128)} %copy-done, f32[64,256]{1,0:T(8,128)} %copy-done.1), custom_call_target="tpu_custom_call" | custom-call | tf_op jit(solution)/shard_map/pack_columns/pallas_call | solution.py:253
  12.8 1.1 %collective-permute-start.3 = (f32[72,128]{1,0:T(8,128)}, f32[72,128]{1,0:T(8,128)S(1)}, u32[]{:S(2)}, u32[]{:S(2)}) collective-permute-start(f32[72,128]{1,0:T(8,128)} %get-tuple-element.11), channel_id=1, source_target_pairs={{0,8},{8,0},{1,9},{9,1},{2,10},{10,2},{3,11},{11,3},{4,12},{12,4},... | collective-permute-start | bytes 110600 | tf_op jit(solution)/shard_map/ppermute | solution.py:262
  14.0 1.2 %collective-permute-start.4 = (f32[72,128]{1,0:T(8,128)}, f32[72,128]{1,0:T(8,128)S(1)}, u32[]{:S(2)}, u32[]{:S(2)}) collective-permute-start(f32[72,128]{1,0:T(8,128)} %get-tuple-element.12), channel_id=1, source_target_pairs={{8,16},{16,8},{9,17},{17,9},{10,18},{18,10},{11,19},{19,11},{12,20... | collective-permute-start | bytes 110600 | tf_op jit(solution)/shard_map/ppermute | solution.py:263
  15.2 0.0 collective-permute-done.2.f_ref
  15.2 0.0 copy-start.2
  15.2 1.3 %collective-permute-done.3.p_ref = f32[72,128]{1,0:T(8,128)S(1)} collective-permute-done((f32[72,128]{1,0:T(8,128)}, f32[72,128]{1,0:T(8,128)S(1)}, u32[]{:S(2)}, u32[]{:S(2)}) %collective-permute-start.3) | collective-permute-done | bytes 36896 | tf_op jit(solution)/shard_map/ppermute | solution.py:262
  16.5 0.0 copy-start.3
  16.5 1.4 %collective-permute-done.4.q_ref = f32[72,128]{1,0:T(8,128)S(1)} collective-permute-done((f32[72,128]{1,0:T(8,128)}, f32[72,128]{1,0:T(8,128)S(1)}, u32[]{:S(2)}, u32[]{:S(2)}) %collective-permute-start.4) | collective-permute-done | bytes 36896 | tf_op jit(solution)/shard_map/ppermute | solution.py:263
  17.9 0.0 copy-done.2
  17.9 0.0 copy-done.3
  17.9 0.0 copy-start.4
  17.9 0.6 %copy-done.4 = f32[72,128]{1,0:T(8,128)} copy-done((f32[72,128]{1,0:T(8,128)}, f32[72,128]{1,0:T(8,128)S(1)}, u32[]{:S(2)}) %copy-start.4) | copy-done | bytes 36888
  18.5 14.7 %both_steps.1 = f32[4,4,64,256]{3,2,1,0:T(8,128)} custom-call(s32[256]{0:T(256)} %c_ref.1, f32[4,4,64,256]{3,2,1,0:T(8,128)} %s_ref.3, f32[4,64,256]{2,1,0:T(8,128)} %u_ref.3, f32[4,64,256]{2,1,0:T(8,128)} %v_ref.3, s32[4,64,256]{2,1,0:T(8,128)} %m_ref.3, f32[64,256]{1,0:T(8,128)} %copy-done, f32[64,256]{1,0:T(8,128)} %copy-done.1, f32[64,256]{1,0:T(8,128)} %copy-done.2, ...), custom_call_target="tpu_custom_call" | custom-call | tf_op jit(solution)/shard_map/both_steps/pallas_call | solution.py:266
Async XLA Ops:
  1.7 6.2 %collective-permute-start = (f32[64,256]{1,0:T(8,128)}, f32[64,256]{1,0:T(8,128)S(1)}, u32[]{:S(2)}, u32[]{:S(2)}) collective-permute-start(f32[64,256]{1,0:T(8,128)} %get-tuple-element.9), channel_id=1, source_target_pairs={{0,1},{1,0},{2,3},{3,2},{4,5},{5,4},{6,7},{7,6},{8,9},{9,8},{10,11... | collective-permute-start | bytes 196616 | tf_op jit(solution)/shard_map/ppermute | solution.py:244
  2.4 6.1 %collective-permute-start.1 = (f32[64,256]{1,0:T(8,128)}, f32[64,256]{1,0:T(8,128)S(1)}, u32[]{:S(2)}, u32[]{:S(2)}) collective-permute-start(f32[64,256]{1,0:T(8,128)} %get-tuple-element.10), channel_id=1, source_target_pairs={{1,2},{2,1},{3,4},{4,3},{5,6},{6,5},{9,10},{10,9},{11,12},{12,11},... | collective-permute-start | bytes 196616 | tf_op jit(solution)/shard_map/ppermute | solution.py:245
  6.5 8.7 %collective-permute-start.2 = (f32[64,256]{1,0:T(8,128)}, f32[64,256]{1,0:T(8,128)S(1)}, u32[]{:S(2)}, u32[]{:S(2)}) collective-permute-start(f32[64,256]{1,0:T(8,128)} %get-tuple-element.10), channel_id=1, source_target_pairs={{7,7},{31,15},{23,23},{15,31}} | collective-permute-start | bytes 196616 | tf_op jit(solution)/shard_map/ppermute | solution.py:246
  8.0 0.6 %copy-start = (f32[64,256]{1,0:T(8,128)}, f32[64,256]{1,0:T(8,128)S(1)}, u32[]{:S(2)}) copy-start(f32[64,256]{1,0:T(8,128)S(1)} %collective-permute-done.a_ref) | copy-start | bytes 196612
  8.6 0.6 %copy-start.1 = (f32[64,256]{1,0:T(8,128)}, f32[64,256]{1,0:T(8,128)S(1)}, u32[]{:S(2)}) copy-start(f32[64,256]{1,0:T(8,128)S(1)} %collective-permute-done.1.b_ref) | copy-start | bytes 196612
  12.8 3.6 %collective-permute-start.3 = (f32[72,128]{1,0:T(8,128)}, f32[72,128]{1,0:T(8,128)S(1)}, u32[]{:S(2)}, u32[]{:S(2)}) collective-permute-start(f32[72,128]{1,0:T(8,128)} %get-tuple-element.11), channel_id=1, source_target_pairs={{0,8},{8,0},{1,9},{9,1},{2,10},{10,2},{3,11},{11,3},{4,12},{12,4},... | collective-permute-start | bytes 110600 | tf_op jit(solution)/shard_map/ppermute | solution.py:262
  14.0 3.9 %collective-permute-start.4 = (f32[72,128]{1,0:T(8,128)}, f32[72,128]{1,0:T(8,128)S(1)}, u32[]{:S(2)}, u32[]{:S(2)}) collective-permute-start(f32[72,128]{1,0:T(8,128)} %get-tuple-element.12), channel_id=1, source_target_pairs={{8,16},{16,8},{9,17},{17,9},{10,18},{18,10},{11,19},{19,11},{12,20... | collective-permute-start | bytes 110600 | tf_op jit(solution)/shard_map/ppermute | solution.py:263
  15.2 2.7 %copy-start.2 = (f32[64,256]{1,0:T(8,128)}, f32[64,256]{1,0:T(8,128)S(1)}, u32[]{:S(2)}) copy-start(f32[64,256]{1,0:T(8,128)S(1)} %collective-permute-done.2.f_ref) | copy-start | bytes 196612
  16.5 1.4 %copy-start.3 = (f32[72,128]{1,0:T(8,128)}, f32[72,128]{1,0:T(8,128)S(1)}, u32[]{:S(2)}) copy-start(f32[72,128]{1,0:T(8,128)S(1)} %collective-permute-done.3.p_ref) | copy-start | bytes 110596
  17.9 0.6 %copy-start.4 = (f32[72,128]{1,0:T(8,128)}, f32[72,128]{1,0:T(8,128)S(1)}, u32[]{:S(2)}) copy-start(f32[72,128]{1,0:T(8,128)S(1)} %collective-permute-done.4.q_ref) | copy-start | bytes 110596

commit v2 on v0

v2 whole, which is shorter than its diff:
```python
import jax
import jax.numpy as jnp
from jax import lax
from jax.experimental import pallas as pl
from jax.experimental.pallas import tpu as pltpu
from jax.sharding import PartitionSpec as P

FIELDS, LEVELS = 4, 4
QN = FIELDS + 3
LANES, SUBS = 128, 8
SOUTH, OWN = 1, 2
VMEM = pl.BlockSpec(memory_space=pltpu.VMEM)
SCOPED = 4 << 20
UNROLL1, UNROLL2 = 5, 4


def iota(dim):
    return lax.broadcasted_iota(jnp.int32, (SUBS, LANES), dim)


def rows(t, by=0):
    start = SUBS * t
    if not isinstance(start, int):
        start = pl.multiple_of(start, SUBS)
    return pl.ds(start + by, SUBS)


def cols(c):
    return pl.ds(LANES * c, LANES)


def lat_place():
    lat = lax.axis_index("lat")
    return lat % 2 == 0, lat == lax.axis_size("lat") - 1


def sign_of(field):
    return 1.0 if field < 2 else -1.0


def row_kernel(s_in, u_in, v_in, m_in, a_ref, b_ref, s_ref, u_ref, v_ref, m_ref, sems):
    copies = []
    for i, (src, dst) in enumerate(((u_in, u_ref), (v_in, v_ref), (m_in, m_ref))):
        copies.append(pltpu.make_async_copy(src, dst, sems.at[i]))
    for f in range(FIELDS):
        copies.append(pltpu.make_async_copy(s_in.at[f], s_ref.at[f], sems.at[3 + f]))
    for copy in copies:
        copy.start()
    for copy in copies:
        copy.wait()
    lat_even, _ = lat_place()
    sub = iota(0)
    last = s_ref.shape[2] // SUBS - 1

    @pl.loop(0, LEVELS)
    def _(l):
        for c in range(2):
            both = []
            for t in (0, last):
                w = m_ref[l, rows(t), cols(c)].astype(jnp.float32)
                values = [s_ref[f, l, rows(t), cols(c)] * w for f in range(FIELDS)]
                both.append(values + [0.5 * u_ref[l, rows(t), cols(c)], 0.5 * v_ref[l, rows(t), cols(c)], w, w])
            for g in range(2):
                low, high = both[0][4 * g], pltpu.roll(both[1][4 * g], 2, 0)
                for k in range(1, 4):
                    low = jnp.where(sub // 2 == k, pltpu.roll(both[0][4 * g + k], 2 * k, 0), low)
                    high = jnp.where(sub // 2 == k, pltpu.roll(both[1][4 * g + k], (2 * k + 2) % SUBS, 0), high)
                a_ref[rows(2 * l + g), cols(c)] = jnp.where(lat_even, high, low)
                b_ref[rows(2 * l + g), cols(c)] = jnp.where(lat_even, low, high)


def insert(packs, quarter, l, q, side, tile):
    seg = LEVELS * (q % 2) + l if q < FIELDS else l
    g = q // 2 if q < FIELDS else q - 2
    moved = pltpu.roll(tile, (16 * seg + (12 if side else 4)) % LANES, 1)
    packs[g] = jnp.where(quarter == 4 * seg + 1 + side, moved, packs[g])


def finish(packs, lane):
    for g in range(2, 5):
        packs[g] = jnp.where(lane < LANES // 2, packs[g], pltpu.roll(packs[g], LANES // 2, 1))


def outgoing(packs, lane, lon_even):
    east = jnp.zeros((SUBS, LANES), jnp.float32)
    west = jnp.zeros((SUBS, LANES), jnp.float32)
    pair = lane // 2 % 8
    for g, tile in enumerate(packs):
        east = jnp.where(pair == 1 + g, pltpu.roll(tile, LANES - 8 + 2 * g, 1), east)
        west = jnp.where(pair == (6 + g) % 8, pltpu.roll(tile, 8 + 2 * g, 1), west)
    return jnp.where(lon_even, east, west), jnp.where(lon_even, west, east)


def prepare_kernel(s_ref, u_ref, v_ref, m_ref, r_ref, u2_ref, v2_ref, w_ref, k_ref, p_ref, q_ref):
    lane = iota(1)
    quarter = lane // 4
    lon_even = lax.axis_index("lon") % 2 == 0

    @pl.loop(0, s_ref.shape[2] // SUBS, unroll=2)
    def _(t):
        src, dst = rows(t), rows(t + OWN)
        packs = [jnp.zeros((SUBS, LANES), jnp.float32)] * 5
        for l in range(LEVELS):
            for c in range(2):
                w = m_ref[l, src, cols(c)].astype(jnp.float32)
                values = [s_ref[f, l, src, cols(c)] * w for f in range(FIELDS)]
                values += [0.5 * u_ref[l, src, cols(c)], 0.5 * v_ref[l, src, cols(c)], w]
                for q, value in enumerate(values):
                    ref = (u2_ref, v2_ref, w_ref)[q - FIELDS] if q >= FIELDS else r_ref
                    ref[LEVELS * q + l if q < FIELDS else l, c, dst, :] = value
                    insert(packs, quarter, l, q, c, value)
        finish(packs, lane)
        for g in range(5):
            k_ref[g, src, :] = packs[g]
        p_ref[src, :], q_ref[src, :] = outgoing(packs, lane, lon_even)


def halo_kernel(
    c_ref, a_ref, b_ref, f_ref, r_in, u2_in, v2_in, w_in, k_in, p_in, q_in,
    r_ref, u2_ref, v2_ref, w_ref, k_ref, p_ref, q_ref, north, south,
):
    lane, sub = iota(1), iota(0)
    quarter = lane // 4
    lat_even, top = lat_place()
    lon = lax.axis_index("lon")
    lon_even = lon % 2 == 0
    width = a_ref.shape[1]
    tiles = k_ref.shape[1] // SUBS - 1

    @pl.loop(0, 2 * LEVELS)
    def _(i):
        for c in range(2):
            a, b = a_ref[rows(i), cols(c)], b_ref[rows(i), cols(c)]
            north[c, rows(i + 1), :] = jnp.where(lat_even, a, b)
            south[c, rows(i + 1), :] = jnp.where(lat_even, b, a)

    @pl.when(top)
    def _():
        ncol = lax.axis_size("lon") * width
        shift = jnp.clip(lax.rem(c_ref[0] + lon * width + 1, ncol), 0, width - 1)

        @pl.loop(0, LEVELS)
        def _(l):
            for g in range(2):
                for c in range(2):
                    p = shift + (width - 1) - LANES * c - lane
                    got = jnp.zeros((SUBS, LANES), jnp.float32)
                    for s in range(4):
                        tile = (b_ref if s < 2 else f_ref)[rows(2 * l + g), cols(s % 2)]
                        picked = jnp.take_along_axis(tile, p % LANES, axis=1, mode="promise_in_bounds")
                        got = jnp.where(p // LANES == s, picked, got)
                    swapped = jnp.where(sub % 2 == 0, pltpu.roll(got, SUBS - 1, 0), pltpu.roll(got, 1, 0))
                    if g == 1:
                        swapped = jnp.where(sub == 2, -got, jnp.where(sub == 3, got, swapped))
                    north[c, rows(2 * l + g + 1), :] = swapped

    packs = [jnp.zeros((SUBS, LANES), jnp.float32)] * 5
    for l in range(LEVELS):
        for q in range(QN):
            tile = []
            for c in range(2):
                at = SUBS + 16 * l + 2 * q
                tile.append(jnp.where(sub < 4, north[c, pl.ds(at, SUBS), :], south[c, pl.ds(at - 6, SUBS), :]))
                insert(packs, quarter, l, q, c, tile[c])
            for c in range(2):
                ref = (u2_ref, v2_ref, w_ref)[q - FIELDS] if q >= FIELDS else r_ref
                index = LEVELS * q + l if q < FIELDS else l
                ref[index, c, rows(SOUTH), :] = tile[c]
                if q == FIELDS:
                    mirrored = -pltpu.roll(jnp.where(lane == 0, tile[1 - c], tile[c]), LANES - 1, 1)
                    tile_n = jnp.where(top & (sub == 0), mirrored, tile[c])
                else:
                    tile_n = tile[c]
                ref[index, c, rows(tiles + OWN), :] = tile_n
    finish(packs, lane)

    for g in range(5):
        k_ref[g, rows(tiles), :] = packs[g]
    p_ref[rows(tiles), :], q_ref[rows(tiles), :] = outgoing(packs, lane, lon_even)


def seam(r, r_mirror, h, h_mirror, w, sign):
    return w * r_mirror * (sign * (0.5 + h_mirror) - h)


def seam_mirror(r, r_top, h_top, h, w, sign):
    return w * (sign * (0.5 + h_top) * r_top - h * r - h_top * (r - r_top))


def step_kernel(r_ref, u2_ref, v2_ref, w_ref, o_ref, r1):
    lane, sub = iota(1), iota(0)
    _, top = lat_place()
    tiles = o_ref.shape[2] // SUBS
    end = OWN + tiles

    def update(l, t, load):
        u = [u2_ref[l, c, rows(t), :] for c in range(2)]
        u_west = [pltpu.roll(jnp.where(lane == LANES - 1, u[1 - c], u[c]), 1, 1) for c in range(2)]
        v = [v2_ref[l, c, rows(t), :] for c in range(2)]
        v_south = [v2_ref[l, c, rows(t, -1), :] for c in range(2)]
        w = [w_ref[l, c, rows(t), :] for c in range(2)]
        out = []
        for f in range(FIELDS):
            r = [load(f, c, rows(t)) for c in range(2)]
            for c in range(2):
                ahead = pltpu.roll(jnp.where(lane == 0, r[1 - c], r[c]), LANES - 1, 1)
                behind = pltpu.roll(jnp.where(lane == LANES - 1, r[1 - c], r[c]), 1, 1)
                along = u[c] * (ahead - r[c]) + u_west[c] * (r[c] - behind)
                up = v[c] * (load(f, c, rows(t, 1)) - r[c])
                down = v_south[c] * (r[c] - load(f, c, rows(t, -1)))
                out.append((f, c, w[c] * (r[c] + along + up + down)))
        return out

    @pl.loop(0, LEVELS)
    def _(l):
        def first(f, c, at):
            return r_ref[LEVELS * f + l, c, at, :]

        def second(f, c, at):
            return r1[f, c, at, :]

        @pl.loop(SOUTH, end + 1, unroll=UNROLL1)
        def _(t):
            for f, c, value in update(l, t, first):
                r1[f, c, rows(t), :] = value

        def at_top(f, c, load):
            v, v_mirror = v2_ref[l, c, rows(end - 1), :], v2_ref[l, c, rows(end - 1, 2), :]
            r, r_mirror = load(f, c, rows(end - 1)), load(f, c, rows(end - 1, 1))
            add = seam(r, r_mirror, v, v_mirror, w_ref[l, c, rows(end - 1), :], sign_of(f))
            return jnp.where(sub == SUBS - 1, add, 0.0)

        @pl.when(top)
        def _():
            for f in range(FIELDS):
                for c in range(2):
                    v_top, v_mirror = v2_ref[l, c, rows(end, -1), :], v2_ref[l, c, rows(end, 1), :]
                    r, r_top = first(f, c, rows(end)), first(f, c, rows(end, -1))
                    add = seam_mirror(r, r_top, v_top, v_mirror, w_ref[l, c, rows(end), :], sign_of(f))
                    r1[f, c, rows(end), :] += jnp.where(sub == 0, add, 0.0)
                    r1[f, c, rows(end - 1), :] += at_top(f, c, first)

        @pl.loop(OWN, end, unroll=UNROLL2)
        def _(t):
            for f, c, value in update(l, t, second):
                o_ref[f, l, rows(t - OWN), cols(c)] = value

        @pl.when(top)
        def _():
            for f in range(FIELDS):
                for c in range(2):
                    o_ref[f, l, rows(tiles - 1), cols(c)] += at_top(f, c, second)


def edge_kernel(k_ref, p_ref, q_ref, i_ref, o_ref, z, z1, buf, sems):
    lane, sub = iota(1), iota(0)
    _, top = lat_place()
    lon_even = lax.axis_index("lon") % 2 == 0
    tiles = i_ref.shape[2] // SUBS
    end = OWN + tiles
    pair = lane // 2 % 8

    def join(t):
        p, q = p_ref[rows(t), :], q_ref[rows(t), :]
        from_west, from_east = jnp.where(lon_even, q, p), jnp.where(lon_even, p, q)
        out = []
        for g in range(5):
            back = (LANES - 2 * g) % LANES
            west, east = (pltpu.roll(x, back, 1) if back else x for x in (from_west, from_east))
            out.append(jnp.where(pair == 1, west, jnp.where(pair == 6, east, k_ref[g, rows(t), :])))
        return out

    @pl.loop(0, tiles, unroll=True)
    def _(t):
        for g, value in enumerate(join(t)):
            z[g, rows(t + OWN), :] = value

    for g, value in enumerate(join(tiles)):
        z[g, rows(SOUTH), :] = value
        if g == 2:
            value = jnp.where(top & (sub == 0), -pltpu.roll(value, LANES - 1, 1), value)
        z[g, rows(end), :] = value

    def update(t, load, mirrored):
        u, v, v_south, w = z[2, rows(t), :], z[3, rows(t), :], z[3, rows(t, -1), :], z[4, rows(t), :]
        u_west = pltpu.roll(u, 1, 1)
        out = []
        for h in range(2):
            r, r_north, r_south = load(h, rows(t)), load(h, rows(t, 1)), load(h, rows(t, -1))
            along = u * (pltpu.roll(r, LANES - 1, 1) - r) + u_west * (r - pltpu.roll(r, 1, 1))
            value = w * (r + along + v * (r_north - r) + v_south * (r - r_south))
            add = seam(r, r_north, v, z[3, rows(t, 2), :], w, sign_of(2 * h))
            value += jnp.where(top & (t == end - 1) & (sub == SUBS - 1), add, 0.0)
            if mirrored:
                add = seam_mirror(r, r_south, v_south, z[3, rows(t, 1), :], w, sign_of(2 * h))
                value += jnp.where(top & (t == end) & (sub == 0), add, 0.0)
            out.append(value)
        return out

    @pl.loop(SOUTH, end + 1, unroll=True)
    def _(t):
        for h, value in enumerate(update(t, lambda h, at: z[h, at, :], True)):
            z1[h, rows(t), :] = value

    def send(t):
        at = rows(t)
        return pltpu.make_async_copy(buf.at[:, :, at, :], o_ref.at[:, :, at, :], sems.at[t])

    @pl.loop(0, tiles, unroll=UNROLL2)
    def _(t):
        value = update(t + OWN, lambda h, at: z1[h, at, :], False)
        for f in range(FIELDS):
            for l in range(LEVELS):
                seg = 16 * (LEVELS * (f % 2) + l)
                west = pltpu.roll(value[f // 2], LANES - 4 - seg, 1)
                east = pltpu.roll(value[f // 2], (LANES + 116 - seg) % LANES, 1)
                buf[f, l, rows(t), cols(0)] = jnp.where(lane < 2, west, i_ref[f, l, rows(t), cols(0)])
                buf[f, l, rows(t), cols(1)] = jnp.where(lane >= LANES - 2, east, i_ref[f, l, rows(t), cols(1)])
        send(t).start()

    @pl.loop(0, tiles)
    def _(t):
        send(t).wait()


def per_device(state_adjoint, east_velocity, north_velocity, ocean_mask, partner):
    nlon, nlat = lax.axis_size("lon"), lax.axis_size("lat")
    fields, levels, height, width = state_adjoint.shape
    axes = ("lon", "lat")
    f32 = jnp.float32

    def device(lon, lat):
        return lon % nlon * nlat + lat

    def both(a, b):
        return [(a, b), (b, a)]

    fold = [(device(nlon - 1 - i, nlat - 1), device(i, nlat - 1)) for i in range(nlon)]
    fold_next = [(device(nlon - i, nlat - 1), device(i, nlat - 1)) for i in range(nlon)]
    within = [e for i in range(nlon) for j in range(0, nlat, 2) for e in both(device(i, j), device(i, j + 1))]
    across = [e for i in range(nlon) for j in range(1, nlat - 1, 2) for e in both(device(i, j), device(i, j + 1))]
    even = [e for i in range(0, nlon, 2) for j in range(nlat) for e in both(device(i, j), device(i + 1, j))]
    odd = [e for i in range(1, nlon, 2) for j in range(nlat) for e in both(device(i, j), device(i + 1, j))]

    def held(x):
        return pltpu.with_memory_space_constraint(x, pltpu.VMEM)

    def call(kernel, name, args, outs, scratch=(), scalars=0, aliases=None, micros=1):
        return pl.pallas_call(
            kernel,
            out_shape=tuple(pltpu.VMEM(shape, f32) for shape in outs),
            in_specs=[pl.BlockSpec(memory_space=pltpu.SMEM)] * scalars + [VMEM] * (len(args) - scalars),
            out_specs=(VMEM,) * len(outs),
            scratch_shapes=[pltpu.VMEM(shape, f32) for shape in scratch],
            input_output_aliases=aliases or {},
            cost_estimate=pl.CostEstimate(flops=0, bytes_accessed=micros * 3_000_000, transcendentals=0),
            compiler_params=pltpu.CompilerParams(vmem_limit_bytes=SCOPED),
            name=name,
        )(*args[:scalars], *(held(x) for x in args[scalars:]))

    inputs = (state_adjoint, east_velocity, north_velocity, ocean_mask)
    message = (16 * levels, width)
    to_a, to_b, *inputs = pl.pallas_call(
        row_kernel,
        out_shape=(pltpu.VMEM(message, f32), pltpu.VMEM(message, f32), *(pltpu.VMEM(x.shape, x.dtype) for x in inputs)),
        in_specs=[pl.BlockSpec(memory_space=pltpu.HBM)] * 4,
        out_specs=(VMEM,) * 6,
        scratch_shapes=[pltpu.SemaphoreType.DMA((3 + fields,))],
        compiler_params=pltpu.CompilerParams(vmem_limit_bytes=SCOPED),
        name="pack_rows",
    )(*(pltpu.with_memory_space_constraint(x, pltpu.HBM) for x in inputs))
    from_a = lax.ppermute(to_a, axes, within)
    from_b = lax.ppermute(to_b, axes, across + fold)
    from_f = lax.ppermute(to_b, axes, fold_next)

    tall = height + 4 * SUBS
    ext = [(fields * levels, 2, tall, LANES)] + [(levels, 2, tall, LANES)] * 3
    pack = (height + SUBS, LANES)
    laid = call(prepare_kernel, "prepare", inputs, (*ext, (5,) + pack, pack, pack))
    *laid, packs, to_p, to_q = call(
        halo_kernel,
        "place_rows",
        (partner, from_a, from_b, from_f, *laid),
        (*ext, (5,) + pack, pack, pack),
        [(2, message[0] + 2 * SUBS, LANES)] * 2,
        scalars=1,
        aliases={4 + i: i for i in range(7)},
    )
    from_p = lax.ppermute(to_p, axes, even)
    from_q = lax.ppermute(to_q, axes, odd)

    (inner,) = call(step_kernel, "both_steps", laid, (state_adjoint.shape,), [(fields, 2, tall, LANES)], micros=3)
    return pl.pallas_call(
        edge_kernel,
        out_shape=jax.ShapeDtypeStruct(state_adjoint.shape, f32),
        in_specs=[VMEM] * 4,
        out_specs=pl.BlockSpec(memory_space=pl.ANY),
        scratch_shapes=[
            pltpu.VMEM((5, tall, LANES), f32),
            pltpu.VMEM((2, tall, LANES), f32),
            pltpu.VMEM(state_adjoint.shape, f32),
            pltpu.SemaphoreType.DMA((height // SUBS,)),
        ],
        compiler_params=pltpu.CompilerParams(vmem_limit_bytes=SCOPED),
        name="edge_columns",
    )(*(held(x) for x in (packs, from_p, from_q, inner)))


def solution(mesh):
    placed = (
        P(None, None, "lat", "lon"),
        P(None, "lat", "lon"),
        P(None, "lat", "lon"),
        P(None, "lat", "lon"),
        P("lon"),
    )
    return jax.shard_map(
        per_device,
        mesh=mesh,
        in_specs=placed,
        out_specs=P(None, None, "lat", "lon"),
        check_vma=False,
    )
```

time: 110 us -> 19.5 us (0.18)
  the two profiles are of different devices: /device:TPU:10 before, /device:TPU:25 now
where the time goes in v2:
time: 19.5 us; the launch traced here: 19.3 us
  starting transfers between devices  9.4 us (48%)
  Pallas kernels  8.64 us (44%)
  waiting for transfers between devices  1.2 us (6%)
    ppermute x1, starting transfers between devices, per_device(): from_b = lax.ppermute(to_b, axes, across + fold)  5.55 us
    pallas_call x3, Pallas kernels, call(): pl.pallas_call(kernel, out_shape=tuple((pltpu.VMEM(shape, f32) for shape...  5.37 us
    ppermute x1, starting transfers between devices, per_device(): from_p = lax.ppermute(to_p, axes, even)  2.44 us
    pallas_call x1, Pallas kernels, per_device(): pl.pallas_call(edge_kernel, out_shape=jax.ShapeDtypeStruct(state_adjoint....  1.7 us
    pallas_call x1, Pallas kernels, per_device(): pl.pallas_call(row_kernel, out_shape=(pltpu.VMEM(message, f32), pltpu.VME...  1.57 us
    ppermute x1, waiting for transfers between devices, per_device(): from_q = lax.ppermute(to_q, axes, odd)  0.78 us
    ppermute x1, starting transfers between devices, per_device(): from_a = lax.ppermute(to_a, axes, within)  0.74 us
    ppermute x1, starting transfers between devices, per_device(): from_f = lax.ppermute(to_b, axes, fold_next)  0.65 us
  transfers between devices with their start and end apart: 5, of which 2 were waited for; matrix products, arithmetic and copies ran while one was open for 0% of the time, Pallas kernels for 21%

profile of v2, /device:TPU:25, one launch (start us, length us, event | category | flops | bytes accessed | tf_op | source)
XLA Modules:
  0.0 19.3 jit_solution(13674798112943547181)
XLA Ops:
  0.0 0.0 copy-start
  0.0 1.6 %pack_rows.1 = (f32[64,256]{1,0:T(8,128)S(1)}, f32[64,256]{1,0:T(8,128)S(1)}, f32[4,4,64,256]{3,2,1,0:T(8,128)S(1)}, f32[4,64,256]{2,1,0:T(8,128)S(1)}, f32[4,64...) custom-call(f32[4,4,64,256]{3,2,1,0:T(8,128)} %s_in.1, f32[4,64,256]{2,1,0:T(8,128)} %u_in.1, f32[4,64,256]{2,1,0:T(8,128)} %v_in.1, ...), custom_call_target="tpu_custom_call" | custom-call | tf_op jit(solution)/shard_map/pack_rows/pallas_call | solution.py:363
  1.6 0.7 %collective-permute-start = (f32[64,256]{1,0:T(8,128)S(1)}, f32[64,256]{1,0:T(8,128)S(1)}, u32[]{:S(2)}, u32[]{:S(2)}) collective-permute-start(f32[64,256]{1,0:T(8,128)S(1)} %get-tuple-element.25), channel_id=1, source_target_pairs={{0,1},{1,0},{2,3},{3,2},{4,5},{5,4},{6,7},{7,6},{8,9},{9,8},{10,11... | collective-permute-start | bytes 196616 | tf_op jit(solution)/shard_map/ppermute | solution.py:372
  2.3 0.7 %collective-permute-start.2 = (f32[64,256]{1,0:T(8,128)S(1)}, f32[64,256]{1,0:T(8,128)S(1)}, u32[]{:S(2)}, u32[]{:S(2)}) collective-permute-start(f32[64,256]{1,0:T(8,128)S(1)} %get-tuple-element.26), channel_id=1, source_target_pairs={{7,7},{31,15},{23,23},{15,31}} | collective-permute-start | bytes 196616 | tf_op jit(solution)/shard_map/ppermute | solution.py:374
  3.0 5.5 %collective-permute-start.1 = (f32[64,256]{1,0:T(8,128)S(1)}, f32[64,256]{1,0:T(8,128)S(1)}, u32[]{:S(2)}, u32[]{:S(2)}) collective-permute-start(f32[64,256]{1,0:T(8,128)S(1)} %get-tuple-element.26), channel_id=1, source_target_pairs={{1,2},{2,1},{3,4},{4,3},{5,6},{6,5},{9,10},{10,9},{11,12},{12,11},... | collective-permute-start | bytes 196616 | tf_op jit(solution)/shard_map/ppermute | solution.py:373
  8.5 1.2 %prepare.1 = (f32[16,2,96,128]{3,2,1,0:T(8,128)S(1)}, f32[4,2,96,128]{3,2,1,0:T(8,128)S(1)}, f32[4,2,96,128]{3,2,1,0:T(8,128)S(1)}, f32[4,2,96,128]{3,2,1,0:T(8,...) custom-call(f32[4,4,64,256]{3,2,1,0:T(8,128)S(1)} %get-tuple-element.27.s_ref, ...), custom_call_target="tpu_custom_call" | custom-call | bytes 3000000 | tf_op jit(solution)/shard_map/prepare/pallas_call | solution.py:349
  9.7 0.0 collective-permute-done.a_ref
  9.7 0.0 collective-permute-done.2.f_ref
  9.8 0.4 %collective-permute-done.1.b_ref = f32[64,256]{1,0:T(8,128)S(1)} collective-permute-done((f32[64,256]{1,0:T(8,128)S(1)}, f32[64,256]{1,0:T(8,128)S(1)}, u32[]{:S(2)}, u32[]{:S(2)}) %collective-permute-start.1) | collective-permute-done | bytes 65568 | tf_op jit(solution)/shard_map/ppermute | solution.py:373
  10.2 0.0 copy-done
  10.2 1.3 %place_rows.1 = (f32[16,2,96,128]{3,2,1,0:T(8,128)S(1)}, f32[4,2,96,128]{3,2,1,0:T(8,128)S(1)}, f32[4,2,96,128]{3,2,1,0:T(8,128)S(1)}, f32[4,2,96,128]{3,2,1,0:T...) custom-call(s32[256]{0:T(256)S(1)} %copy-done, ...), custom_call_target="tpu_custom_call", output_to_operand_aliasing={{0}: (4, {}), {1}: (5, {}), {2}: (6, {}), {3}: (7, {}), {4}... | custom-call | bytes 3000000 | tf_op jit(solution)/shard_map/place_rows/pallas_call | solution.py:349
  11.5 2.4 %collective-permute-start.3 = (f32[72,128]{1,0:T(8,128)S(1)}, f32[72,128]{1,0:T(8,128)S(1)}, u32[]{:S(2)}, u32[]{:S(2)}) collective-permute-start(f32[72,128]{1,0:T(8,128)S(1)} %get-tuple-element.39), channel_id=1, source_target_pairs={{0,8},{8,0},{1,9},{9,1},{2,10},{10,2},{3,11},{11,3},{4,12},{12,4},... | collective-permute-start | bytes 110600 | tf_op jit(solution)/shard_map/ppermute | solution.py:389
  13.9 0.0 collective-permute-start.4
  13.9 2.9 %both_steps.1.i_ref = f32[4,4,64,256]{3,2,1,0:T(8,128)S(1)} custom-call(f32[16,2,96,128]{3,2,1,0:T(8,128)S(1)} %get-tuple-element.41.r_ref, f32[4,2,96,128]{3,2,1,0:T(8,128)S(1)} %get-tuple-element.42.u2_ref, f32[4,2,96,128]{3,2,1,0:T(8,128)S(1)} %get-tuple-element.43.v2_ref, f32[4,2,96,128]{3,2,1,0:T(8,128)S(1)} %get-tuple-element.44.w_ref), custom_call_target="tpu_custom_call" | custom-call | bytes 9000000 | tf_op jit(solution)/shard_map/both_steps/pallas_call | solution.py:349
  16.8 0.0 collective-permute-done.3.p_ref
  16.8 0.8 %collective-permute-done.4.q_ref = f32[72,128]{1,0:T(8,128)S(1)} collective-permute-done((f32[72,128]{1,0:T(8,128)S(1)}, f32[72,128]{1,0:T(8,128)S(1)}, u32[]{:S(2)}, u32[]{:S(2)}) %collective-permute-start.4) | collective-permute-done | bytes 36896 | tf_op jit(solution)/shard_map/ppermute | solution.py:390
  17.6 1.7 %edge_columns.1 = f32[4,4,64,256]{3,2,1,0:T(8,128)} custom-call(f32[5,72,128]{2,1,0:T(8,128)S(1)} %get-tuple-element.38.k_ref, f32[72,128]{1,0:T(8,128)S(1)} %collective-permute-done.3.p_ref, f32[72,128]{1,0:T(8,128)S(1)} %collective-permute-done.4.q_ref, f32[4,4,64,256]{3,2,1,0:T(8,128)S(1)} %both_steps.1.i_ref), custom_call_target="tpu_custom_call" | custom-call | tf_op jit(solution)/shard_map/edge_columns/pallas_call | solution.py:393
Async XLA Ops:
  0.0 10.2 %copy-start = (s32[256]{0:T(256)S(1)}, s32[256]{0:T(256)}, u32[]{:S(2)}) copy-start(s32[256]{0:T(256)} %c_ref.1) | copy-start | bytes 3076
  1.6 8.2 %collective-permute-start = (f32[64,256]{1,0:T(8,128)S(1)}, f32[64,256]{1,0:T(8,128)S(1)}, u32[]{:S(2)}, u32[]{:S(2)}) collective-permute-start(f32[64,256]{1,0:T(8,128)S(1)} %get-tuple-element.25), channel_id=1, source_target_pairs={{0,1},{1,0},{2,3},{3,2},{4,5},{5,4},{6,7},{7,6},{8,9},{9,8},{10,11... | collective-permute-start | bytes 196616 | tf_op jit(solution)/shard_map/ppermute | solution.py:372
  2.3 7.4 %collective-permute-start.2 = (f32[64,256]{1,0:T(8,128)S(1)}, f32[64,256]{1,0:T(8,128)S(1)}, u32[]{:S(2)}, u32[]{:S(2)}) collective-permute-start(f32[64,256]{1,0:T(8,128)S(1)} %get-tuple-element.26), channel_id=1, source_target_pairs={{7,7},{31,15},{23,23},{15,31}} | collective-permute-start | bytes 196616 | tf_op jit(solution)/shard_map/ppermute | solution.py:374
  3.0 7.2 %collective-permute-start.1 = (f32[64,256]{1,0:T(8,128)S(1)}, f32[64,256]{1,0:T(8,128)S(1)}, u32[]{:S(2)}, u32[]{:S(2)}) collective-permute-start(f32[64,256]{1,0:T(8,128)S(1)} %get-tuple-element.26), channel_id=1, source_target_pairs={{1,2},{2,1},{3,4},{4,3},{5,6},{6,5},{9,10},{10,9},{11,12},{12,11},... | collective-permute-start | bytes 196616 | tf_op jit(solution)/shard_map/ppermute | solution.py:373
  11.5 5.4 %collective-permute-start.3 = (f32[72,128]{1,0:T(8,128)S(1)}, f32[72,128]{1,0:T(8,128)S(1)}, u32[]{:S(2)}, u32[]{:S(2)}) collective-permute-start(f32[72,128]{1,0:T(8,128)S(1)} %get-tuple-element.39), channel_id=1, source_target_pairs={{0,8},{8,0},{1,9},{9,1},{2,10},{10,2},{3,11},{11,3},{4,12},{12,4},... | collective-permute-start | bytes 110600 | tf_op jit(solution)/shard_map/ppermute | solution.py:389
  13.9 3.7 %collective-permute-start.4 = (f32[72,128]{1,0:T(8,128)S(1)}, f32[72,128]{1,0:T(8,128)S(1)}, u32[]{:S(2)}, u32[]{:S(2)}) collective-permute-start(f32[72,128]{1,0:T(8,128)S(1)} %get-tuple-element.40), channel_id=1, source_target_pairs={{8,16},{16,8},{9,17},{17,9},{10,18},{18,10},{11,19},{19,11},{12,20... | collective-permute-start | bytes 110600 | tf_op jit(solution)/shard_map/ppermute | solution.py:390

commit v3 on v2

--- a/solution.py
+++ b/solution.py
@@ -11,7 +11,7 @@
 SOUTH, OWN = 1, 2
 VMEM = pl.BlockSpec(memory_space=pltpu.VMEM)
 SCOPED = 4 << 20
-UNROLL1, UNROLL2 = 5, 4
+UNROLL1, UNROLL2 = 10, 8
 
 
 def iota(dim):
@@ -39,27 +39,26 @@
 
 
 def row_kernel(s_in, u_in, v_in, m_in, a_ref, b_ref, s_ref, u_ref, v_ref, m_ref, sems):
+    lat_even, _ = lat_place()
+    sub = iota(0)
     copies = []
-    for i, (src, dst) in enumerate(((u_in, u_ref), (v_in, v_ref), (m_in, m_ref))):
-        copies.append(pltpu.make_async_copy(src, dst, sems.at[i]))
-    for f in range(FIELDS):
-        copies.append(pltpu.make_async_copy(s_in.at[f], s_ref.at[f], sems.at[3 + f]))
+    for i, (src, dst) in enumerate(((s_in, s_ref), (u_in, u_ref), (v_in, v_ref), (m_in, m_ref))):
+        lead = (slice(None),) * (len(src.shape) - 2)
+        for k, t in enumerate((0, src.shape[-2] // SUBS - 1)):
+            copies.append(pltpu.make_async_copy(src.at[lead + (rows(t), slice(None))], dst.at[k], sems.at[i, k]))
     for copy in copies:
         copy.start()
     for copy in copies:
         copy.wait()
-    lat_even, _ = lat_place()
-    sub = iota(0)
-    last = s_ref.shape[2] // SUBS - 1
 
     @pl.loop(0, LEVELS)
     def _(l):
         for c in range(2):
             both = []
-            for t in (0, last):
-                w = m_ref[l, rows(t), cols(c)].astype(jnp.float32)
-                values = [s_ref[f, l, rows(t), cols(c)] * w for f in range(FIELDS)]
-                both.append(values + [0.5 * u_ref[l, rows(t), cols(c)], 0.5 * v_ref[l, rows(t), cols(c)], w, w])
+            for k in range(2):
+                w = m_ref[k, l, :, cols(c)].astype(jnp.float32)
+                values = [s_ref[k, f, l, :, cols(c)] * w for f in range(FIELDS)]
+                both.append(values + [0.5 * u_ref[k, l, :, cols(c)], 0.5 * v_ref[k, l, :, cols(c)], w, w])
             for g in range(2):
                 low, high = both[0][4 * g], pltpu.roll(both[1][4 * g], 2, 0)
                 for k in range(1, 4):
@@ -137,13 +136,13 @@
     @pl.when(top)
     def _():
         ncol = lax.axis_size("lon") * width
-        shift = jnp.clip(lax.rem(c_ref[0] + lon * width + 1, ncol), 0, width - 1)
+        source = [lax.rem(c_ref[pl.ds(c, SUBS, stride=0), :] + (lon + 1) * width, ncol) for c in range(2)]
 
         @pl.loop(0, LEVELS)
         def _(l):
             for g in range(2):
                 for c in range(2):
-                    p = shift + (width - 1) - LANES * c - lane
+                    p = source[c]
                     got = jnp.zeros((SUBS, LANES), jnp.float32)
                     for s in range(4):
                         tile = (b_ref if s < 2 else f_ref)[rows(2 * l + g), cols(s % 2)]
@@ -345,33 +344,35 @@
     def held(x):
         return pltpu.with_memory_space_constraint(x, pltpu.VMEM)
 
-    def call(kernel, name, args, outs, scratch=(), scalars=0, aliases=None, micros=1):
+    def call(kernel, name, args, outs, scratch=(), aliases=None, micros=1):
         return pl.pallas_call(
             kernel,
             out_shape=tuple(pltpu.VMEM(shape, f32) for shape in outs),
-            in_specs=[pl.BlockSpec(memory_space=pltpu.SMEM)] * scalars + [VMEM] * (len(args) - scalars),
+            in_specs=[VMEM] * len(args),
             out_specs=(VMEM,) * len(outs),
             scratch_shapes=[pltpu.VMEM(shape, f32) for shape in scratch],
             input_output_aliases=aliases or {},
             cost_estimate=pl.CostEstimate(flops=0, bytes_accessed=micros * 3_000_000, transcendentals=0),
             compiler_params=pltpu.CompilerParams(vmem_limit_bytes=SCOPED),
             name=name,
-        )(*args[:scalars], *(held(x) for x in args[scalars:]))
+        )(*(held(x) for x in args))
 
     inputs = (state_adjoint, east_velocity, north_velocity, ocean_mask)
     message = (16 * levels, width)
-    to_a, to_b, *inputs = pl.pallas_call(
+    to_a, to_b = pl.pallas_call(
         row_kernel,
-        out_shape=(pltpu.VMEM(message, f32), pltpu.VMEM(message, f32), *(pltpu.VMEM(x.shape, x.dtype) for x in inputs)),
+        out_shape=(pltpu.VMEM(message, f32), pltpu.VMEM(message, f32)),
         in_specs=[pl.BlockSpec(memory_space=pltpu.HBM)] * 4,
-        out_specs=(VMEM,) * 6,
-        scratch_shapes=[pltpu.SemaphoreType.DMA((3 + fields,))],
+        out_specs=(VMEM,) * 2,
+        scratch_shapes=[pltpu.VMEM((2,) + x.shape[:-2] + (SUBS, width), x.dtype) for x in inputs]
+        + [pltpu.SemaphoreType.DMA((4, 2))],
         compiler_params=pltpu.CompilerParams(vmem_limit_bytes=SCOPED),
         name="pack_rows",
     )(*(pltpu.with_memory_space_constraint(x, pltpu.HBM) for x in inputs))
     from_a = lax.ppermute(to_a, axes, within)
     from_b = lax.ppermute(to_b, axes, across + fold)
-    from_f = lax.ppermute(to_b, axes, fold_next)
+    to_f, _ = lax.optimization_barrier((to_b, from_a))
+    from_f = lax.ppermute(to_f, axes, fold_next)
 
     tall = height + 4 * SUBS
     ext = [(fields * levels, 2, tall, LANES)] + [(levels, 2, tall, LANES)] * 3
@@ -380,10 +381,9 @@
     *laid, packs, to_p, to_q = call(
         halo_kernel,
         "place_rows",
-        (partner, from_a, from_b, from_f, *laid),
+        (partner.reshape(2, LANES), from_a, from_b, from_f, *laid),
         (*ext, (5,) + pack, pack, pack),
         [(2, message[0] + 2 * SUBS, LANES)] * 2,
-        scalars=1,
         aliases={4 + i: i for i in range(7)},
     )
     from_p = lax.ppermute(to_p, axes, even)

time: 19.5 us -> 17.7 us (0.908)
  Pallas kernels: 8.64 us -> 7.05 us
  starting transfers between devices: 9.4 us -> 8.82 us
  waiting for transfers between devices: 1.2 us -> 1.49 us
    ppermute x1, starting transfers between devices: 5.55 us -> 4.06 us  [per_device(): from_b = lax.ppermute(to_b, axes, across + fold)]
    pallas_call x3, Pallas kernels: 5.37 us -> 4.12 us  [call(): pl.pallas_call(kernel, out_shape=tuple((pltpu.VMEM(shape, f32) for shape...]
    ppermute x1, starting transfers between devices: 2.44 us -> 3.33 us  [per_device(): from_p = lax.ppermute(to_p, axes, even)]
    ppermute x1, waiting for transfers between devices: 0.78 us -> 1.48 us  [per_device(): from_q = lax.ppermute(to_q, axes, odd)]
    ppermute x1, waiting for transfers between devices: 0.41 us -> 0.01 us  [per_device(): from_b = lax.ppermute(to_b, axes, across + fold)]
    pallas_call x1, Pallas kernels: 1.57 us -> 1.24 us  [per_device(): pl.pallas_call(row_kernel, out_shape=(pltpu.VMEM(message, f32), pltpu.VME...]
  transfers between devices with their start and end apart: 5 -> 5, of which waited for: 2 -> 1; matrix products, arithmetic and copies ran while one was open for 0% -> 0% of each run, Pallas kernels for 21% -> 19%
where the time goes in v3:
time: 17.7 us; the launch traced here: 17.5 us
  starting transfers between devices  8.82 us (50%)
  Pallas kernels  7.05 us (40%)
  waiting for transfers between devices  1.49 us (8%)
    pallas_call x3, Pallas kernels, call(): pl.pallas_call(kernel, out_shape=tuple((pltpu.VMEM(shape, f32) for shape...  4.12 us
    ppermute x1, starting transfers between devices, per_device(): from_b = lax.ppermute(to_b, axes, across + fold)  4.06 us
    ppermute x1, starting transfers between devices, per_device(): from_p = lax.ppermute(to_p, axes, even)  3.33 us
    pallas_call x1, Pallas kernels, per_device(): pl.pallas_call(edge_kernel, out_shape=jax.ShapeDtypeStruct(state_adjoint....  1.69 us
    ppermute x1, waiting for transfers between devices, per_device(): from_q = lax.ppermute(to_q, axes, odd)  1.48 us
    pallas_call x1, Pallas kernels, per_device(): pl.pallas_call(row_kernel, out_shape=(pltpu.VMEM(message, f32), pltpu.VME...  1.24 us
    ppermute x1, starting transfers between devices, per_device(): from_a = lax.ppermute(to_a, axes, within)  0.74 us
    ppermute x1, starting transfers between devices, per_device(): from_f = lax.ppermute(to_f, axes, fold_next)  0.66 us
  transfers between devices with their start and end apart: 5, of which 1 were waited for; matrix products, arithmetic and copies ran while one was open for 0% of the time, Pallas kernels for 19%

profile of v3, /device:TPU:25, one launch (start us, length us, event | category | flops | bytes accessed | tf_op | source)
XLA Modules:
  0.0 17.5 jit_solution(3125654692677996838)
XLA Ops:
  0.0 0.0 copy-start.3
  0.0 0.0 copy-start.2
  0.0 0.0 copy-start.1
  0.0 0.0 copy-start
  0.0 0.0 copy-start.4
  0.0 1.2 %pack_rows.1 = (f32[64,256]{1,0:T(8,128)S(1)}, f32[64,256]{1,0:T(8,128)S(1)}) custom-call(f32[4,4,64,256]{3,2,1,0:T(8,128)} %s_ref.1, f32[4,64,256]{2,1,0:T(8,128)} %u_ref.1, f32[4,64,256]{2,1,0:T(8,128)} %v_ref.1, s32[4,64,256]{2,1,0:T(8,128)} %m_ref.1), custom_call_target="tpu_custom_call" | custom-call | tf_op jit(solution)/shard_map/pack_rows/pallas_call | solution.py:362
  1.3 0.7 %collective-permute-start = (f32[64,256]{1,0:T(8,128)S(1)}, f32[64,256]{1,0:T(8,128)S(1)}, u32[]{:S(2)}, u32[]{:S(2)}) collective-permute-start(f32[64,256]{1,0:T(8,128)S(1)} %get-tuple-element.22), channel_id=1, source_target_pairs={{0,1},{1,0},{2,3},{3,2},{4,5},{5,4},{6,7},{7,6},{8,9},{9,8},{10,11... | collective-permute-start | bytes 196616 | tf_op jit(solution)/shard_map/ppermute | solution.py:372
  2.0 4.1 %collective-permute-start.1 = (f32[64,256]{1,0:T(8,128)S(1)}, f32[64,256]{1,0:T(8,128)S(1)}, u32[]{:S(2)}, u32[]{:S(2)}) collective-permute-start(f32[64,256]{1,0:T(8,128)S(1)} %get-tuple-element.24), channel_id=1, source_target_pairs={{1,2},{2,1},{3,4},{4,3},{5,6},{6,5},{9,10},{10,9},{11,12},{12,11},... | collective-permute-start | bytes 196616 | tf_op jit(solution)/shard_map/ppermute | solution.py:373
  6.1 0.0 collective-permute-done.a_ref
  6.1 0.7 %collective-permute-start.2 = (f32[64,256]{1,0:T(8,128)S(1)}, f32[64,256]{1,0:T(8,128)S(1)}, u32[]{:S(2)}, u32[]{:S(2)}) collective-permute-start(f32[64,256]{1,0:T(8,128)S(1)} %get-tuple-element.24), channel_id=1, source_target_pairs={{7,7},{31,15},{23,23},{15,31}} | collective-permute-start | bytes 196616 | tf_op jit(solution)/shard_map/ppermute | solution.py:375
  6.8 0.0 copy-done.3
  6.8 0.0 copy-done.2
  6.8 0.0 copy-done.1
  6.8 0.0 copy-done
  6.8 1.2 %prepare.1 = (f32[16,2,96,128]{3,2,1,0:T(8,128)S(1)}, f32[4,2,96,128]{3,2,1,0:T(8,128)S(1)}, f32[4,2,96,128]{3,2,1,0:T(8,128)S(1)}, f32[4,2,96,128]{3,2,1,0:T(8,...) custom-call(f32[4,4,64,256]{3,2,1,0:T(8,128)S(1)} %copy-done, ...), custom_call_target="tpu_custom_call" | custom-call | bytes 3000000 | tf_op jit(solution)/shard_map/prepare/pallas_call | solution.py:348
  8.0 0.0 collective-permute-done.1.b_ref
  8.0 0.0 collective-permute-done.2.f_ref
  8.0 0.0 copy-done.4
  8.0 0.7 %place_rows.1 = (f32[16,2,96,128]{3,2,1,0:T(8,128)S(1)}, f32[4,2,96,128]{3,2,1,0:T(8,128)S(1)}, f32[4,2,96,128]{3,2,1,0:T(8,128)S(1)}, f32[4,2,96,128]{3,2,1,0:T...) custom-call(s32[2,128]{1,0:T(2,128)S(1)} %bitcast.1, ...), custom_call_target="tpu_custom_call", output_to_operand_aliasing={{0}: (4, {}), {1}: (5, {}), {2}: (6, {}), {3}: (7, {}), {4}... | custom-call | bytes 3000000 | tf_op jit(solution)/shard_map/place_rows/pallas_call | solution.py:348
  8.8 3.3 %collective-permute-start.3 = (f32[72,128]{1,0:T(8,128)S(1)}, f32[72,128]{1,0:T(8,128)S(1)}, u32[]{:S(2)}, u32[]{:S(2)}) collective-permute-start(f32[72,128]{1,0:T(8,128)S(1)} %get-tuple-element.33), channel_id=1, source_target_pairs={{0,8},{8,0},{1,9},{9,1},{2,10},{10,2},{3,11},{11,3},{4,12},{12,4},... | collective-permute-start | bytes 110600 | tf_op jit(solution)/shard_map/ppermute | solution.py:389
  12.1 0.0 collective-permute-start.4
  12.1 2.2 %both_steps.1.i_ref = f32[4,4,64,256]{3,2,1,0:T(8,128)S(1)} custom-call(f32[16,2,96,128]{3,2,1,0:T(8,128)S(1)} %get-tuple-element.35.r_ref, f32[4,2,96,128]{3,2,1,0:T(8,128)S(1)} %get-tuple-element.36.u2_ref, f32[4,2,96,128]{3,2,1,0:T(8,128)S(1)} %get-tuple-element.37.v2_ref, f32[4,2,96,128]{3,2,1,0:T(8,128)S(1)} %get-tuple-element.38.w_ref), custom_call_target="tpu_custom_call" | custom-call | bytes 9000000 | tf_op jit(solution)/shard_map/both_steps/pallas_call | solution.py:348
  14.3 0.0 collective-permute-done.3.p_ref
  14.3 1.5 %collective-permute-done.4.q_ref = f32[72,128]{1,0:T(8,128)S(1)} collective-permute-done((f32[72,128]{1,0:T(8,128)S(1)}, f32[72,128]{1,0:T(8,128)S(1)}, u32[]{:S(2)}, u32[]{:S(2)}) %collective-permute-start.4) | collective-permute-done | bytes 36896 | tf_op jit(solution)/shard_map/ppermute | solution.py:390
  15.8 1.7 %edge_columns.1 = f32[4,4,64,256]{3,2,1,0:T(8,128)} custom-call(f32[5,72,128]{2,1,0:T(8,128)S(1)} %get-tuple-element.32.k_ref, f32[72,128]{1,0:T(8,128)S(1)} %collective-permute-done.3.p_ref, f32[72,128]{1,0:T(8,128)S(1)} %collective-permute-done.4.q_ref, f32[4,4,64,256]{3,2,1,0:T(8,128)S(1)} %both_steps.1.i_ref), custom_call_target="tpu_custom_call" | custom-call | tf_op jit(solution)/shard_map/edge_columns/pallas_call | solution.py:393
Async XLA Ops:
  0.0 6.8 %copy-start.3 = (s32[4,64,256]{2,1,0:T(8,128)S(1)}, s32[4,64,256]{2,1,0:T(8,128)}, u32[]{:S(2)}) copy-start(s32[4,64,256]{2,1,0:T(8,128)} %m_ref.1) | copy-start | bytes 786436
  0.0 6.8 %copy-start.2 = (f32[4,64,256]{2,1,0:T(8,128)S(1)}, f32[4,64,256]{2,1,0:T(8,128)}, u32[]{:S(2)}) copy-start(f32[4,64,256]{2,1,0:T(8,128)} %v_ref.1) | copy-start | bytes 786436
  0.0 6.8 %copy-start.1 = (f32[4,64,256]{2,1,0:T(8,128)S(1)}, f32[4,64,256]{2,1,0:T(8,128)}, u32[]{:S(2)}) copy-start(f32[4,64,256]{2,1,0:T(8,128)} %u_ref.1) | copy-start | bytes 786436
  0.0 6.8 %copy-start = (f32[4,4,64,256]{3,2,1,0:T(8,128)S(1)}, f32[4,4,64,256]{3,2,1,0:T(8,128)}, u32[]{:S(2)}) copy-start(f32[4,4,64,256]{3,2,1,0:T(8,128)} %s_ref.1) | copy-start | bytes 3145732
  0.0 8.0 %copy-start.4 = (s32[256]{0:T(256)S(1)}, s32[256]{0:T(256)}, u32[]{:S(2)}) copy-start(s32[256]{0:T(256)} %param.9) | copy-start | bytes 3076
  1.3 4.8 %collective-permute-start = (f32[64,256]{1,0:T(8,128)S(1)}, f32[64,256]{1,0:T(8,128)S(1)}, u32[]{:S(2)}, u32[]{:S(2)}) collective-permute-start(f32[64,256]{1,0:T(8,128)S(1)} %get-tuple-element.22), channel_id=1, source_target_pairs={{0,1},{1,0},{2,3},{3,2},{4,5},{5,4},{6,7},{7,6},{8,9},{9,8},{10,11... | collective-permute-start | bytes 196616 | tf_op jit(solution)/shard_map/ppermute | solution.py:372
  2.0 6.0 %collective-permute-start.1 = (f32[64,256]{1,0:T(8,128)S(1)}, f32[64,256]{1,0:T(8,128)S(1)}, u32[]{:S(2)}, u32[]{:S(2)}) collective-permute-start(f32[64,256]{1,0:T(8,128)S(1)} %get-tuple-element.24), channel_id=1, source_target_pairs={{1,2},{2,1},{3,4},{4,3},{5,6},{6,5},{9,10},{10,9},{11,12},{12,11},... | collective-permute-start | bytes 196616 | tf_op jit(solution)/shard_map/ppermute | solution.py:373
  6.1 1.9 %collective-permute-start.2 = (f32[64,256]{1,0:T(8,128)S(1)}, f32[64,256]{1,0:T(8,128)S(1)}, u32[]{:S(2)}, u32[]{:S(2)}) collective-permute-start(f32[64,256]{1,0:T(8,128)S(1)} %get-tuple-element.24), channel_id=1, source_target_pairs={{7,7},{31,15},{23,23},{15,31}} | collective-permute-start | bytes 196616 | tf_op jit(solution)/shard_map/ppermute | solution.py:375
  8.8 5.6 %collective-permute-start.3 = (f32[72,128]{1,0:T(8,128)S(1)}, f32[72,128]{1,0:T(8,128)S(1)}, u32[]{:S(2)}, u32[]{:S(2)}) collective-permute-start(f32[72,128]{1,0:T(8,128)S(1)} %get-tuple-element.33), channel_id=1, source_target_pairs={{0,8},{8,0},{1,9},{9,1},{2,10},{10,2},{3,11},{11,3},{4,12},{12,4},... | collective-permute-start | bytes 110600 | tf_op jit(solution)/shard_map/ppermute | solution.py:389
  12.1 3.7 %collective-permute-start.4 = (f32[72,128]{1,0:T(8,128)S(1)}, f32[72,128]{1,0:T(8,128)S(1)}, u32[]{:S(2)}, u32[]{:S(2)}) collective-permute-start(f32[72,128]{1,0:T(8,128)S(1)} %get-tuple-element.34), channel_id=1, source_target_pairs={{8,16},{16,8},{9,17},{17,9},{10,18},{18,10},{11,19},{19,11},{12,20... | collective-permute-start | bytes 110600 | tf_op jit(solution)/shard_map/ppermute | solution.py:390

commit v4 on v3

--- a/solution.py
+++ b/solution.py
@@ -114,16 +114,20 @@
         p_ref[src, :], q_ref[src, :] = outgoing(packs, lane, lon_even)
 
 
+def partner_columns(c_ref, width):
+    ncol = lax.axis_size("lon") * width
+    lon = lax.axis_index("lon")
+    return [lax.rem(c_ref[pl.ds(c, SUBS, stride=0), :] + (lon + 1) * width, ncol) for c in range(2)]
+
+
 def halo_kernel(
-    c_ref, a_ref, b_ref, f_ref, r_in, u2_in, v2_in, w_in, k_in, p_in, q_in,
+    a_ref, b_ref, r_in, u2_in, v2_in, w_in, k_in, p_in, q_in,
     r_ref, u2_ref, v2_ref, w_ref, k_ref, p_ref, q_ref, north, south,
 ):
     lane, sub = iota(1), iota(0)
     quarter = lane // 4
     lat_even, top = lat_place()
-    lon = lax.axis_index("lon")
-    lon_even = lon % 2 == 0
-    width = a_ref.shape[1]
+    lon_even = lax.axis_index("lon") % 2 == 0
     tiles = k_ref.shape[1] // SUBS - 1
 
     @pl.loop(0, 2 * LEVELS)
@@ -133,49 +137,74 @@
             north[c, rows(i + 1), :] = jnp.where(lat_even, a, b)
             south[c, rows(i + 1), :] = jnp.where(lat_even, b, a)
 
+    packs = [jnp.zeros((SUBS, LANES), jnp.float32)] * 5
+    for l in range(LEVELS):
+        for q in range(QN):
+            ref = (u2_ref, v2_ref, w_ref)[q - FIELDS] if q >= FIELDS else r_ref
+            index = LEVELS * q + l if q < FIELDS else l
+            at = SUBS + 16 * l + 2 * q
+            tile = []
+            for c in range(2):
+                tile.append(jnp.where(sub < 4, north[c, pl.ds(at, SUBS), :], south[c, pl.ds(at - 6, SUBS), :]))
+                ref[index, c, rows(SOUTH), :] = tile[c]
+                ref[index, c, rows(tiles + OWN), :] = tile[c]
+            last = pltpu.roll(tile[1], 1, 1)
+            insert(packs, quarter, l, q, 0, jnp.where(top & (sub < 2), last, tile[0]))
+            insert(packs, quarter, l, q, 1, tile[1])
+    finish(packs, lane)
+    for g in range(5):
+        k_ref[g, rows(tiles), :] = packs[g]
+    p_ref[rows(tiles), :], q_ref[rows(tiles), :] = outgoing(packs, lane, lon_even)
+
+
+def mirror_kernel(
+    c_ref, b_ref, f_ref, r_in, u2_in, v2_in, w_in, k_in, r_ref, u2_ref, v2_ref, w_ref, k_ref, mirrored
+):
+    lane, sub = iota(1), iota(0)
+    quarter = lane // 4
+    _, top = lat_place()
+    width = b_ref.shape[1]
+    tiles = k_ref.shape[1] // SUBS - 1
+
     @pl.when(top)
     def _():
-        ncol = lax.axis_size("lon") * width
-        source = [lax.rem(c_ref[pl.ds(c, SUBS, stride=0), :] + (lon + 1) * width, ncol) for c in range(2)]
+        source = partner_columns(c_ref, width)
+        before = jnp.broadcast_to(source[0][:, :1] + 1, (SUBS, LANES))
+        after = jnp.broadcast_to(jnp.maximum(source[1][:, LANES - 1 :] - 1, 0), (SUBS, LANES))
 
         @pl.loop(0, LEVELS)
         def _(l):
             for g in range(2):
-                for c in range(2):
-                    p = source[c]
+                raw = [(b_ref if s < 2 else f_ref)[rows(2 * l + g), cols(s % 2)] for s in range(4)]
+                for c, p in enumerate((*source, before, after)):
                     got = jnp.zeros((SUBS, LANES), jnp.float32)
                     for s in range(4):
-                        tile = (b_ref if s < 2 else f_ref)[rows(2 * l + g), cols(s % 2)]
-                        picked = jnp.take_along_axis(tile, p % LANES, axis=1, mode="promise_in_bounds")
+                        picked = jnp.take_along_axis(raw[s], p % LANES, axis=1, mode="promise_in_bounds")
                         got = jnp.where(p // LANES == s, picked, got)
                     swapped = jnp.where(sub % 2 == 0, pltpu.roll(got, SUBS - 1, 0), pltpu.roll(got, 1, 0))
                     if g == 1:
                         swapped = jnp.where(sub == 2, -got, jnp.where(sub == 3, got, swapped))
-                    north[c, rows(2 * l + g + 1), :] = swapped
-
-    packs = [jnp.zeros((SUBS, LANES), jnp.float32)] * 5
-    for l in range(LEVELS):
-        for q in range(QN):
-            tile = []
-            for c in range(2):
-                at = SUBS + 16 * l + 2 * q
-                tile.append(jnp.where(sub < 4, north[c, pl.ds(at, SUBS), :], south[c, pl.ds(at - 6, SUBS), :]))
-                insert(packs, quarter, l, q, c, tile[c])
-            for c in range(2):
+                    mirrored[c, rows(2 * l + g), :] = swapped
+
+        packs = [jnp.zeros((SUBS, LANES), jnp.float32)] * 5
+        for l in range(LEVELS):
+            for q in range(QN):
                 ref = (u2_ref, v2_ref, w_ref)[q - FIELDS] if q >= FIELDS else r_ref
                 index = LEVELS * q + l if q < FIELDS else l
-                ref[index, c, rows(SOUTH), :] = tile[c]
-                if q == FIELDS:
-                    mirrored = -pltpu.roll(jnp.where(lane == 0, tile[1 - c], tile[c]), LANES - 1, 1)
-                    tile_n = jnp.where(top & (sub == 0), mirrored, tile[c])
-                else:
-                    tile_n = tile[c]
-                ref[index, c, rows(tiles + OWN), :] = tile_n
-    finish(packs, lane)
-
-    for g in range(5):
-        k_ref[g, rows(tiles), :] = packs[g]
-    p_ref[rows(tiles), :], q_ref[rows(tiles), :] = outgoing(packs, lane, lon_even)
+                seg = LEVELS * (q % 2) + l if q < FIELDS else l
+                pack = q // 2 if q < FIELDS else q - 2
+                tile = [mirrored[c, pl.ds(16 * l + 2 * q, SUBS), :] for c in range(4)]
+                for c in range(2):
+                    insert(packs, quarter, l, q, c, tile[c])
+                    north = tile[c]
+                    if q == FIELDS:
+                        north = -pltpu.roll(jnp.where(lane == 0, tile[1 - c], tile[c]), LANES - 1, 1)
+                    ref[index, c, rows(tiles + OWN), :] = north
+                packs[pack] = jnp.where(lane == 16 * seg + 3, tile[2], packs[pack])
+                packs[pack] = jnp.where(lane == 16 * seg + 12, tile[3], packs[pack])
+        finish(packs, lane)
+        for g in range(5):
+            k_ref[g, rows(tiles), :] = jnp.where(sub < 2, packs[g], k_in[g, rows(tiles), :])
 
 
 def seam(r, r_mirror, h, h_mirror, w, sign):
@@ -251,7 +280,7 @@
                     o_ref[f, l, rows(tiles - 1), cols(c)] += at_top(f, c, second)
 
 
-def edge_kernel(k_ref, p_ref, q_ref, i_ref, o_ref, z, z1, buf, sems):
+def edge_kernel(c_ref, k_ref, q_ref, p_ref, i_ref, o_ref, z, z1, buf, sems):
     lane, sub = iota(1), iota(0)
     _, top = lat_place()
     lon_even = lax.axis_index("lon") % 2 == 0
@@ -274,8 +303,15 @@
         for g, value in enumerate(join(t)):
             z[g, rows(t + OWN), :] = value
 
+    at_seam = partner_columns(c_ref, i_ref.shape[3])[1][:, LANES - 1 :] == 0
+    p, q = p_ref[rows(tiles), :], q_ref[rows(tiles), :]
     for g, value in enumerate(join(tiles)):
         z[g, rows(SOUTH), :] = value
+        crossed = pltpu.roll(jnp.where(lon_even, p, q), (LANES - 2 * g) % LANES, 1) if g else jnp.where(lon_even, p, q)
+        if g != 3:
+            crossed = pltpu.roll(crossed, SUBS - 1, 0)
+        kept = jnp.where((pair == 6) & at_seam, crossed, k_ref[g, rows(tiles), :])
+        value = jnp.where(top & (sub < 2), kept, value)
         if g == 2:
             value = jnp.where(top & (sub == 0), -pltpu.roll(value, LANES - 1, 1), value)
         z[g, rows(end), :] = value
@@ -371,29 +407,37 @@
     )(*(pltpu.with_memory_space_constraint(x, pltpu.HBM) for x in inputs))
     from_a = lax.ppermute(to_a, axes, within)
     from_b = lax.ppermute(to_b, axes, across + fold)
-    to_f, _ = lax.optimization_barrier((to_b, from_a))
-    from_f = lax.ppermute(to_f, axes, fold_next)
+    from_f = lax.ppermute(to_b, axes, fold_next)
 
     tall = height + 4 * SUBS
     ext = [(fields * levels, 2, tall, LANES)] + [(levels, 2, tall, LANES)] * 3
     pack = (height + SUBS, LANES)
     laid = call(prepare_kernel, "prepare", inputs, (*ext, (5,) + pack, pack, pack))
-    *laid, packs, to_p, to_q = call(
+    *laid, to_p, to_q = call(
         halo_kernel,
         "place_rows",
-        (partner.reshape(2, LANES), from_a, from_b, from_f, *laid),
+        (from_a, from_b, *laid),
         (*ext, (5,) + pack, pack, pack),
         [(2, message[0] + 2 * SUBS, LANES)] * 2,
-        aliases={4 + i: i for i in range(7)},
+        aliases={2 + i: i for i in range(7)},
     )
     from_p = lax.ppermute(to_p, axes, even)
     from_q = lax.ppermute(to_q, axes, odd)
 
+    pairs = partner.reshape(2, LANES)
+    *laid, packs = call(
+        mirror_kernel,
+        "mirror_rows",
+        (pairs, from_b, from_f, *laid),
+        (*ext, (5,) + pack),
+        [(4, message[0] + SUBS, LANES)],
+        aliases={3 + i: i for i in range(5)},
+    )
     (inner,) = call(step_kernel, "both_steps", laid, (state_adjoint.shape,), [(fields, 2, tall, LANES)], micros=3)
     return pl.pallas_call(
         edge_kernel,
         out_shape=jax.ShapeDtypeStruct(state_adjoint.shape, f32),
-        in_specs=[VMEM] * 4,
+        in_specs=[VMEM] * 5,
         out_specs=pl.BlockSpec(memory_space=pl.ANY),
         scratch_shapes=[
             pltpu.VMEM((5, tall, LANES), f32),
@@ -403,7 +447,7 @@
         ],
         compiler_params=pltpu.CompilerParams(vmem_limit_bytes=SCOPED),
         name="edge_columns",
-    )(*(held(x) for x in (packs, from_p, from_q, inner)))
+    )(*(held(x) for x in (pairs, packs, from_q, from_p, inner)))
 
 
 def solution(mesh):

time: 17.7 us -> 16.4 us (0.927)
  the two profiles are of different devices: /device:TPU:25 before, /device:TPU:27 now
where the time goes in v4:
time: 16.4 us; the launch traced here: 16.2 us
  starting transfers between devices  8.42 us (51%)
  Pallas kernels  7.61 us (46%)
    pallas_call x4, Pallas kernels, call(): pl.pallas_call(kernel, out_shape=tuple((pltpu.VMEM(shape, f32) for shape...  4.67 us
    ppermute x1, starting transfers between devices, per_device(): from_b = lax.ppermute(to_b, axes, across + fold)  3.11 us
    ppermute x1, starting transfers between devices, per_device(): from_f = lax.ppermute(to_b, axes, fold_next)  2.13 us
    ppermute x1, starting transfers between devices, per_device(): from_p = lax.ppermute(to_p, axes, even)  1.89 us
    pallas_call x1, Pallas kernels, per_device(): pl.pallas_call(edge_kernel, out_shape=jax.ShapeDtypeStruct(state_adjoint....  1.7 us
    pallas_call x1, Pallas kernels, per_device(): pl.pallas_call(row_kernel, out_shape=(pltpu.VMEM(message, f32), pltpu.VME...  1.24 us
    ppermute x1, starting transfers between devices, per_device(): from_a = lax.ppermute(to_a, axes, within)  0.74 us
    ppermute x1, starting transfers between devices, per_device(): from_q = lax.ppermute(to_q, axes, odd)  0.55 us
  transfers between devices with their start and end apart: 5, of which 0 were waited for; matrix products, arithmetic and copies ran while one was open for 0% of the time, Pallas kernels for 29%

profile of v4, /device:TPU:27, one launch (start us, length us, event | category | flops | bytes accessed | tf_op | source)
XLA Modules:
  0.0 16.2 jit_solution(10754907072064065048)
XLA Ops:
  0.0 0.0 copy-start.3
  0.0 0.0 copy-start.2
  0.0 0.0 copy-start.1
  0.0 0.0 copy-start
  0.0 1.2 %pack_rows.1 = (f32[64,256]{1,0:T(8,128)S(1)}, f32[64,256]{1,0:T(8,128)S(1)}) custom-call(f32[4,4,64,256]{3,2,1,0:T(8,128)} %s_ref.1, f32[4,64,256]{2,1,0:T(8,128)} %u_ref.1, f32[4,64,256]{2,1,0:T(8,128)} %v_ref.1, s32[4,64,256]{2,1,0:T(8,128)} %m_ref.1), custom_call_target="tpu_custom_call" | custom-call | tf_op jit(solution)/shard_map/pack_rows/pallas_call | solution.py:398
  1.3 0.7 %collective-permute-start.2 = (f32[64,256]{1,0:T(8,128)S(1)}, f32[64,256]{1,0:T(8,128)S(1)}, u32[]{:S(2)}, u32[]{:S(2)}) collective-permute-start(f32[64,256]{1,0:T(8,128)S(1)} %get-tuple-element.27), channel_id=1, source_target_pairs={{0,1},{1,0},{2,3},{3,2},{4,5},{5,4},{6,7},{7,6},{8,9},{9,8},{10,11... | collective-permute-start | bytes 196616 | tf_op jit(solution)/shard_map/ppermute | solution.py:408
  2.0 3.1 %collective-permute-start = (f32[64,256]{1,0:T(8,128)S(1)}, f32[64,256]{1,0:T(8,128)S(1)}, u32[]{:S(2)}, u32[]{:S(2)}) collective-permute-start(f32[64,256]{1,0:T(8,128)S(1)} %get-tuple-element.26), channel_id=1, source_target_pairs={{1,2},{2,1},{3,4},{4,3},{5,6},{6,5},{9,10},{10,9},{11,12},{12,11},... | collective-permute-start | bytes 196616 | tf_op jit(solution)/shard_map/ppermute | solution.py:409
  5.1 2.1 %collective-permute-start.1 = (f32[64,256]{1,0:T(8,128)S(1)}, f32[64,256]{1,0:T(8,128)S(1)}, u32[]{:S(2)}, u32[]{:S(2)}) collective-permute-start(f32[64,256]{1,0:T(8,128)S(1)} %get-tuple-element.26), channel_id=1, source_target_pairs={{7,7},{31,15},{23,23},{15,31}} | collective-permute-start | bytes 196616 | tf_op jit(solution)/shard_map/ppermute | solution.py:410
  7.3 0.0 copy-done.3
  7.3 0.0 copy-done.2
  7.3 0.0 copy-done.1
  7.3 0.0 copy-done
  7.3 1.2 %prepare.1 = (f32[16,2,96,128]{3,2,1,0:T(8,128)S(1)}, f32[4,2,96,128]{3,2,1,0:T(8,128)S(1)}, f32[4,2,96,128]{3,2,1,0:T(8,128)S(1)}, f32[4,2,96,128]{3,2,1,0:T(8,...) custom-call(f32[4,4,64,256]{3,2,1,0:T(8,128)S(1)} %copy-done, ...), custom_call_target="tpu_custom_call" | custom-call | bytes 3000000 | tf_op jit(solution)/shard_map/prepare/pallas_call | solution.py:384
  8.5 0.0 collective-permute-done.2.a_ref
  8.5 0.0 collective-permute-done.b_ref
  8.6 0.0 copy-start.4
  8.6 0.4 %place_rows.1 = (f32[16,2,96,128]{3,2,1,0:T(8,128)S(1)}, f32[4,2,96,128]{3,2,1,0:T(8,128)S(1)}, f32[4,2,96,128]{3,2,1,0:T(8,128)S(1)}, f32[4,2,96,128]{3,2,1,0:T...) custom-call(f32[64,256]{1,0:T(8,128)S(1)} %collective-permute-done.2, ...), custom_call_target="tpu_custom_call", output_to_operand_aliasing={{0}: (2, {}), {1}: (3, {}), {2}: (4, {}), {3}: (5, {}), {4}... | custom-call | bytes 3000000 | tf_op jit(solution)/shard_map/place_rows/pallas_call | solution.py:384
  8.9 0.5 %collective-permute-start.3 = (f32[72,128]{1,0:T(8,128)S(1)}, f32[72,128]{1,0:T(8,128)S(1)}, u32[]{:S(2)}, u32[]{:S(2)}) collective-permute-start(f32[72,128]{1,0:T(8,128)S(1)} %get-tuple-element.41), channel_id=1, source_target_pairs={{8,16},{16,8},{9,17},{17,9},{10,18},{18,10},{11,19},{19,11},{12,20... | collective-permute-start | bytes 110600 | tf_op jit(solution)/shard_map/ppermute | solution.py:425
  9.5 1.9 %collective-permute-start.4 = (f32[72,128]{1,0:T(8,128)S(1)}, f32[72,128]{1,0:T(8,128)S(1)}, u32[]{:S(2)}, u32[]{:S(2)}) collective-permute-start(f32[72,128]{1,0:T(8,128)S(1)} %get-tuple-element.42), channel_id=1, source_target_pairs={{0,8},{8,0},{1,9},{9,1},{2,10},{10,2},{3,11},{11,3},{4,12},{12,4},... | collective-permute-start | bytes 110600 | tf_op jit(solution)/shard_map/ppermute | solution.py:424
  11.4 0.0 collective-permute-done.1.f_ref
  11.4 0.0 copy-done.4
  11.4 0.9 %mirror_rows.1 = (f32[16,2,96,128]{3,2,1,0:T(8,128)S(1)}, f32[4,2,96,128]{3,2,1,0:T(8,128)S(1)}, f32[4,2,96,128]{3,2,1,0:T(8,128)S(1)}, f32[4,2,96,128]{3,2,1,0:T(8,128)S(1)}, f32[5,72,128]{2,1,0:T(8,128)S(1)}) custom-call(s32[2,128]{1,0:T(2,128)S(1)} %bitcast.1, ...), custom_call_target="tpu_custom_call", output_to_operand_aliasing={{0}: (3, {}), {1}: (4, {}), {2}: (5, {}), {3}: (6, {}), {4}... | custom-call | bytes 3000000 | tf_op jit(solution)/shard_map/mirror_rows/pallas_call | solution.py:384
  12.2 2.2 %both_steps.1.i_ref = f32[4,4,64,256]{3,2,1,0:T(8,128)S(1)} custom-call(f32[16,2,96,128]{3,2,1,0:T(8,128)S(1)} %get-tuple-element.43.r_ref, f32[4,2,96,128]{3,2,1,0:T(8,128)S(1)} %get-tuple-element.44.u2_ref, f32[4,2,96,128]{3,2,1,0:T(8,128)S(1)} %get-tuple-element.45.v2_ref, f32[4,2,96,128]{3,2,1,0:T(8,128)S(1)} %get-tuple-element.46.w_ref), custom_call_target="tpu_custom_call" | custom-call | bytes 9000000 | tf_op jit(solution)/shard_map/both_steps/pallas_call | solution.py:384
  14.5 0.0 collective-permute-done.3.q_ref
  14.5 0.0 collective-permute-done.4.p_ref
  14.5 1.7 %edge_columns.1 = f32[4,4,64,256]{3,2,1,0:T(8,128)} custom-call(s32[2,128]{1,0:T(2,128)S(1)} %bitcast.2, f32[5,72,128]{2,1,0:T(8,128)S(1)} %get-tuple-element.40.k_ref, f32[72,128]{1,0:T(8,128)S(1)} %collective-permute-done.3.q_ref, f32[72,128]{1,0:T(8,128)S(1)} %collective-permute-done.4.p_ref, f32[4,4,64,256]{3,2,1,0:T(8,128)S(1)} %both_steps.1.i_ref), custom_call_target="tpu_custom_call" | custom-call | tf_op jit(solution)/shard_map/edge_columns/pallas_call | solution.py:437
Async XLA Ops:
  0.0 7.3 %copy-start.3 = (s32[4,64,256]{2,1,0:T(8,128)S(1)}, s32[4,64,256]{2,1,0:T(8,128)}, u32[]{:S(2)}) copy-start(s32[4,64,256]{2,1,0:T(8,128)} %m_ref.1) | copy-start | bytes 786436
  0.0 7.3 %copy-start.2 = (f32[4,64,256]{2,1,0:T(8,128)S(1)}, f32[4,64,256]{2,1,0:T(8,128)}, u32[]{:S(2)}) copy-start(f32[4,64,256]{2,1,0:T(8,128)} %v_ref.1) | copy-start | bytes 786436
  0.0 7.3 %copy-start.1 = (f32[4,64,256]{2,1,0:T(8,128)S(1)}, f32[4,64,256]{2,1,0:T(8,128)}, u32[]{:S(2)}) copy-start(f32[4,64,256]{2,1,0:T(8,128)} %u_ref.1) | copy-start | bytes 786436
  0.0 7.3 %copy-start = (f32[4,4,64,256]{3,2,1,0:T(8,128)S(1)}, f32[4,4,64,256]{3,2,1,0:T(8,128)}, u32[]{:S(2)}) copy-start(f32[4,4,64,256]{3,2,1,0:T(8,128)} %s_ref.1) | copy-start | bytes 3145732
  1.3 7.3 %collective-permute-start.2 = (f32[64,256]{1,0:T(8,128)S(1)}, f32[64,256]{1,0:T(8,128)S(1)}, u32[]{:S(2)}, u32[]{:S(2)}) collective-permute-start(f32[64,256]{1,0:T(8,128)S(1)} %get-tuple-element.27), channel_id=1, source_target_pairs={{0,1},{1,0},{2,3},{3,2},{4,5},{5,4},{6,7},{7,6},{8,9},{9,8},{10,11... | collective-permute-start | bytes 196616 | tf_op jit(solution)/shard_map/ppermute | solution.py:408
  2.0 6.5 %collective-permute-start = (f32[64,256]{1,0:T(8,128)S(1)}, f32[64,256]{1,0:T(8,128)S(1)}, u32[]{:S(2)}, u32[]{:S(2)}) collective-permute-start(f32[64,256]{1,0:T(8,128)S(1)} %get-tuple-element.26), channel_id=1, source_target_pairs={{1,2},{2,1},{3,4},{4,3},{5,6},{6,5},{9,10},{10,9},{11,12},{12,11},... | collective-permute-start | bytes 196616 | tf_op jit(solution)/shard_map/ppermute | solution.py:409
  5.1 6.3 %collective-permute-start.1 = (f32[64,256]{1,0:T(8,128)S(1)}, f32[64,256]{1,0:T(8,128)S(1)}, u32[]{:S(2)}, u32[]{:S(2)}) collective-permute-start(f32[64,256]{1,0:T(8,128)S(1)} %get-tuple-element.26), channel_id=1, source_target_pairs={{7,7},{31,15},{23,23},{15,31}} | collective-permute-start | bytes 196616 | tf_op jit(solution)/shard_map/ppermute | solution.py:410
  8.6 2.8 %copy-start.4 = (s32[256]{0:T(256)S(1)}, s32[256]{0:T(256)}, u32[]{:S(2)}) copy-start(s32[256]{0:T(256)} %param.9) | copy-start | bytes 3076
  8.9 5.5 %collective-permute-start.3 = (f32[72,128]{1,0:T(8,128)S(1)}, f32[72,128]{1,0:T(8,128)S(1)}, u32[]{:S(2)}, u32[]{:S(2)}) collective-permute-start(f32[72,128]{1,0:T(8,128)S(1)} %get-tuple-element.41), channel_id=1, source_target_pairs={{8,16},{16,8},{9,17},{17,9},{10,18},{18,10},{11,19},{19,11},{12,20... | collective-permute-start | bytes 110600 | tf_op jit(solution)/shard_map/ppermute | solution.py:425
  9.5 5.0 %collective-permute-start.4 = (f32[72,128]{1,0:T(8,128)S(1)}, f32[72,128]{1,0:T(8,128)S(1)}, u32[]{:S(2)}, u32[]{:S(2)}) collective-permute-start(f32[72,128]{1,0:T(8,128)S(1)} %get-tuple-element.42), channel_id=1, source_target_pairs={{0,8},{8,0},{1,9},{9,1},{2,10},{10,2},{3,11},{11,3},{4,12},{12,4},... | collective-permute-start | bytes 110600 | tf_op jit(solution)/shard_map/ppermute | solution.py:424

commit v5 on v4

--- a/solution.py
+++ b/solution.py
@@ -80,13 +80,16 @@
         packs[g] = jnp.where(lane < LANES // 2, packs[g], pltpu.roll(packs[g], LANES // 2, 1))
 
 
-def outgoing(packs, lane, lon_even):
+def outgoing(packs, lane, lon_even, seam_rows=None):
     east = jnp.zeros((SUBS, LANES), jnp.float32)
     west = jnp.zeros((SUBS, LANES), jnp.float32)
     pair = lane // 2 % 8
     for g, tile in enumerate(packs):
         east = jnp.where(pair == 1 + g, pltpu.roll(tile, LANES - 8 + 2 * g, 1), east)
-        west = jnp.where(pair == (6 + g) % 8, pltpu.roll(tile, 8 + 2 * g, 1), west)
+        first = pltpu.roll(tile, 8 + 2 * g, 1)
+        if seam_rows is not None:
+            first = jnp.where(seam_rows, pltpu.roll(tile, 1 + 2 * g, 1), first)
+        west = jnp.where(pair == (6 + g) % 8, first, west)
     return jnp.where(lon_even, east, west), jnp.where(lon_even, west, east)
 
 
@@ -148,13 +151,12 @@
                 tile.append(jnp.where(sub < 4, north[c, pl.ds(at, SUBS), :], south[c, pl.ds(at - 6, SUBS), :]))
                 ref[index, c, rows(SOUTH), :] = tile[c]
                 ref[index, c, rows(tiles + OWN), :] = tile[c]
-            last = pltpu.roll(tile[1], 1, 1)
-            insert(packs, quarter, l, q, 0, jnp.where(top & (sub < 2), last, tile[0]))
-            insert(packs, quarter, l, q, 1, tile[1])
+            for c in range(2):
+                insert(packs, quarter, l, q, c, tile[c])
     finish(packs, lane)
     for g in range(5):
         k_ref[g, rows(tiles), :] = packs[g]
-    p_ref[rows(tiles), :], q_ref[rows(tiles), :] = outgoing(packs, lane, lon_even)
+    p_ref[rows(tiles), :], q_ref[rows(tiles), :] = outgoing(packs, lane, lon_even, top & (sub < 2))
 
 
 def mirror_kernel(
@@ -172,7 +174,7 @@
         before = jnp.broadcast_to(source[0][:, :1] + 1, (SUBS, LANES))
         after = jnp.broadcast_to(jnp.maximum(source[1][:, LANES - 1 :] - 1, 0), (SUBS, LANES))
 
-        @pl.loop(0, LEVELS)
+        @pl.loop(0, LEVELS, unroll=True)
         def _(l):
             for g in range(2):
                 raw = [(b_ref if s < 2 else f_ref)[rows(2 * l + g), cols(s % 2)] for s in range(4)]
@@ -344,13 +346,13 @@
     @pl.loop(0, tiles, unroll=UNROLL2)
     def _(t):
         value = update(t + OWN, lambda h, at: z1[h, at, :], False)
+        value = [jnp.where(pair == 1, pltpu.roll(x, LANES - 8, 1), x) for x in value]
         for f in range(FIELDS):
             for l in range(LEVELS):
                 seg = 16 * (LEVELS * (f % 2) + l)
-                west = pltpu.roll(value[f // 2], LANES - 4 - seg, 1)
-                east = pltpu.roll(value[f // 2], (LANES + 116 - seg) % LANES, 1)
-                buf[f, l, rows(t), cols(0)] = jnp.where(lane < 2, west, i_ref[f, l, rows(t), cols(0)])
-                buf[f, l, rows(t), cols(1)] = jnp.where(lane >= LANES - 2, east, i_ref[f, l, rows(t), cols(1)])
+                sides = pltpu.roll(value[f // 2], LANES - 4 - seg, 1)
+                buf[f, l, rows(t), cols(0)] = jnp.where(lane < 2, sides, i_ref[f, l, rows(t), cols(0)])
+                buf[f, l, rows(t), cols(1)] = jnp.where(lane >= LANES - 2, sides, i_ref[f, l, rows(t), cols(1)])
         send(t).start()
 
     @pl.loop(0, tiles)

time: 16.4 us -> 15.8 us (0.963)
  the two profiles are of different devices: /device:TPU:27 before, /device:TPU:25 now
where the time goes in v5:
time: 15.8 us; the launch traced here: 15.7 us
  starting transfers between devices  8.21 us (52%)
  Pallas kernels  7.01 us (44%)
  waiting for transfers between devices  0.31 us (2%)
    pallas_call x4, Pallas kernels, call(): pl.pallas_call(kernel, out_shape=tuple((pltpu.VMEM(shape, f32) for shape...  4.22 us
    ppermute x1, starting transfers between devices, per_device(): from_b = lax.ppermute(to_b, axes, across + fold)  4.06 us
    ppermute x1, starting transfers between devices, per_device(): from_q = lax.ppermute(to_q, axes, odd)  2.74 us
    pallas_call x1, Pallas kernels, per_device(): pl.pallas_call(edge_kernel, out_shape=jax.ShapeDtypeStruct(state_adjoint....  1.54 us
    pallas_call x1, Pallas kernels, per_device(): pl.pallas_call(row_kernel, out_shape=(pltpu.VMEM(message, f32), pltpu.VME...  1.24 us
    ppermute x1, starting transfers between devices, per_device(): from_a = lax.ppermute(to_a, axes, within)  0.74 us
    ppermute x1, starting transfers between devices, per_device(): from_f = lax.ppermute(to_b, axes, fold_next)  0.66 us
  transfers between devices with their start and end apart: 5, of which 1 were waited for; matrix products, arithmetic and copies ran while one was open for 0% of the time, Pallas kernels for 27%

profile of v5, /device:TPU:25, one launch (start us, length us, event | category | flops | bytes accessed | tf_op | source)
XLA Modules:
  0.0 15.7 jit_solution(8661724859939175283)
XLA Ops:
  0.0 0.0 copy-start.3
  0.0 0.0 copy-start.2
  0.0 0.0 copy-start.1
  0.0 0.0 copy-start
  0.0 1.2 %pack_rows.1 = (f32[64,256]{1,0:T(8,128)S(1)}, f32[64,256]{1,0:T(8,128)S(1)}) custom-call(f32[4,4,64,256]{3,2,1,0:T(8,128)} %s_ref.1, f32[4,64,256]{2,1,0:T(8,128)} %u_ref.1, f32[4,64,256]{2,1,0:T(8,128)} %v_ref.1, s32[4,64,256]{2,1,0:T(8,128)} %m_ref.1), custom_call_target="tpu_custom_call" | custom-call | tf_op jit(solution)/shard_map/pack_rows/pallas_call | solution.py:400
  1.3 0.7 %collective-permute-start.2 = (f32[64,256]{1,0:T(8,128)S(1)}, f32[64,256]{1,0:T(8,128)S(1)}, u32[]{:S(2)}, u32[]{:S(2)}) collective-permute-start(f32[64,256]{1,0:T(8,128)S(1)} %get-tuple-element.27), channel_id=1, source_target_pairs={{0,1},{1,0},{2,3},{3,2},{4,5},{5,4},{6,7},{7,6},{8,9},{9,8},{10,11... | collective-permute-start | bytes 196616 | tf_op jit(solution)/shard_map/ppermute | solution.py:410
  2.0 4.1 %collective-permute-start = (f32[64,256]{1,0:T(8,128)S(1)}, f32[64,256]{1,0:T(8,128)S(1)}, u32[]{:S(2)}, u32[]{:S(2)}) collective-permute-start(f32[64,256]{1,0:T(8,128)S(1)} %get-tuple-element.26), channel_id=1, source_target_pairs={{1,2},{2,1},{3,4},{4,3},{5,6},{6,5},{9,10},{10,9},{11,12},{12,11},... | collective-permute-start | bytes 196616 | tf_op jit(solution)/shard_map/ppermute | solution.py:411
  6.1 0.7 %collective-permute-start.1 = (f32[64,256]{1,0:T(8,128)S(1)}, f32[64,256]{1,0:T(8,128)S(1)}, u32[]{:S(2)}, u32[]{:S(2)}) collective-permute-start(f32[64,256]{1,0:T(8,128)S(1)} %get-tuple-element.26), channel_id=1, source_target_pairs={{7,7},{31,15},{23,23},{15,31}} | collective-permute-start | bytes 196616 | tf_op jit(solution)/shard_map/ppermute | solution.py:412
  6.8 0.0 copy-done.3
  6.8 0.0 copy-done.2
  6.8 0.0 copy-done.1
  6.8 0.0 copy-done
  6.8 1.2 %prepare.1 = (f32[16,2,96,128]{3,2,1,0:T(8,128)S(1)}, f32[4,2,96,128]{3,2,1,0:T(8,128)S(1)}, f32[4,2,96,128]{3,2,1,0:T(8,128)S(1)}, f32[4,2,96,128]{3,2,1,0:T(8,...) custom-call(f32[4,4,64,256]{3,2,1,0:T(8,128)S(1)} %copy-done, ...), custom_call_target="tpu_custom_call" | custom-call | bytes 3000000 | tf_op jit(solution)/shard_map/prepare/pallas_call | solution.py:386
  8.0 0.0 collective-permute-done.2.a_ref
  8.0 0.0 collective-permute-done.b_ref
  8.0 0.0 copy-start.4
  8.1 0.3 %place_rows.1 = (f32[16,2,96,128]{3,2,1,0:T(8,128)S(1)}, f32[4,2,96,128]{3,2,1,0:T(8,128)S(1)}, f32[4,2,96,128]{3,2,1,0:T(8,128)S(1)}, f32[4,2,96,128]{3,2,1,0:T...) custom-call(f32[64,256]{1,0:T(8,128)S(1)} %collective-permute-done.2, ...), custom_call_target="tpu_custom_call", output_to_operand_aliasing={{0}: (2, {}), {1}: (3, {}), {2}: (4, {}), {3}: (5, {}), {4}... | custom-call | bytes 3000000 | tf_op jit(solution)/shard_map/place_rows/pallas_call | solution.py:386
  8.4 2.7 %collective-permute-start.3 = (f32[72,128]{1,0:T(8,128)S(1)}, f32[72,128]{1,0:T(8,128)S(1)}, u32[]{:S(2)}, u32[]{:S(2)}) collective-permute-start(f32[72,128]{1,0:T(8,128)S(1)} %get-tuple-element.41), channel_id=1, source_target_pairs={{8,16},{16,8},{9,17},{17,9},{10,18},{18,10},{11,19},{19,11},{12,20... | collective-permute-start | bytes 110600 | tf_op jit(solution)/shard_map/ppermute | solution.py:427
  11.1 0.0 collective-permute-start.4
  11.1 0.0 collective-permute-done.1.f_ref
  11.1 0.0 copy-done.4
  11.1 0.5 %mirror_rows.1 = (f32[16,2,96,128]{3,2,1,0:T(8,128)S(1)}, f32[4,2,96,128]{3,2,1,0:T(8,128)S(1)}, f32[4,2,96,128]{3,2,1,0:T(8,128)S(1)}, f32[4,2,96,128]{3,2,1,0:T(8,128)S(1)}, f32[5,72,128]{2,1,0:T(8,128)S(1)}) custom-call(s32[2,128]{1,0:T(2,128)S(1)} %bitcast.1, ...), custom_call_target="tpu_custom_call", output_to_operand_aliasing={{0}: (3, {}), {1}: (4, {}), {2}: (5, {}), {3}: (6, {}), {4}... | custom-call | bytes 3000000 | tf_op jit(solution)/shard_map/mirror_rows/pallas_call | solution.py:386
  11.6 2.2 %both_steps.1.i_ref = f32[4,4,64,256]{3,2,1,0:T(8,128)S(1)} custom-call(f32[16,2,96,128]{3,2,1,0:T(8,128)S(1)} %get-tuple-element.43.r_ref, f32[4,2,96,128]{3,2,1,0:T(8,128)S(1)} %get-tuple-element.44.u2_ref, f32[4,2,96,128]{3,2,1,0:T(8,128)S(1)} %get-tuple-element.45.v2_ref, f32[4,2,96,128]{3,2,1,0:T(8,128)S(1)} %get-tuple-element.46.w_ref), custom_call_target="tpu_custom_call" | custom-call | bytes 9000000 | tf_op jit(solution)/shard_map/both_steps/pallas_call | solution.py:386
  13.8 0.0 collective-permute-done.3.q_ref
  13.8 0.3 %collective-permute-done.4.p_ref = f32[72,128]{1,0:T(8,128)S(1)} collective-permute-done((f32[72,128]{1,0:T(8,128)S(1)}, f32[72,128]{1,0:T(8,128)S(1)}, u32[]{:S(2)}, u32[]{:S(2)}) %collective-permute-start.4) | collective-permute-done | bytes 36896 | tf_op jit(solution)/shard_map/ppermute | solution.py:426
  14.1 1.5 %edge_columns.1 = f32[4,4,64,256]{3,2,1,0:T(8,128)} custom-call(s32[2,128]{1,0:T(2,128)S(1)} %bitcast.2, f32[5,72,128]{2,1,0:T(8,128)S(1)} %get-tuple-element.40.k_ref, f32[72,128]{1,0:T(8,128)S(1)} %collective-permute-done.3.q_ref, f32[72,128]{1,0:T(8,128)S(1)} %collective-permute-done.4.p_ref, f32[4,4,64,256]{3,2,1,0:T(8,128)S(1)} %both_steps.1.i_ref), custom_call_target="tpu_custom_call" | custom-call | tf_op jit(solution)/shard_map/edge_columns/pallas_call | solution.py:439
Async XLA Ops:
  0.0 6.8 %copy-start.3 = (s32[4,64,256]{2,1,0:T(8,128)S(1)}, s32[4,64,256]{2,1,0:T(8,128)}, u32[]{:S(2)}) copy-start(s32[4,64,256]{2,1,0:T(8,128)} %m_ref.1) | copy-start | bytes 786436
  0.0 6.8 %copy-start.2 = (f32[4,64,256]{2,1,0:T(8,128)S(1)}, f32[4,64,256]{2,1,0:T(8,128)}, u32[]{:S(2)}) copy-start(f32[4,64,256]{2,1,0:T(8,128)} %v_ref.1) | copy-start | bytes 786436
  0.0 6.8 %copy-start.1 = (f32[4,64,256]{2,1,0:T(8,128)S(1)}, f32[4,64,256]{2,1,0:T(8,128)}, u32[]{:S(2)}) copy-start(f32[4,64,256]{2,1,0:T(8,128)} %u_ref.1) | copy-start | bytes 786436
  0.0 6.8 %copy-start = (f32[4,4,64,256]{3,2,1,0:T(8,128)S(1)}, f32[4,4,64,256]{3,2,1,0:T(8,128)}, u32[]{:S(2)}) copy-start(f32[4,4,64,256]{3,2,1,0:T(8,128)} %s_ref.1) | copy-start | bytes 3145732
  1.3 6.8 %collective-permute-start.2 = (f32[64,256]{1,0:T(8,128)S(1)}, f32[64,256]{1,0:T(8,128)S(1)}, u32[]{:S(2)}, u32[]{:S(2)}) collective-permute-start(f32[64,256]{1,0:T(8,128)S(1)} %get-tuple-element.27), channel_id=1, source_target_pairs={{0,1},{1,0},{2,3},{3,2},{4,5},{5,4},{6,7},{7,6},{8,9},{9,8},{10,11... | collective-permute-start | bytes 196616 | tf_op jit(solution)/shard_map/ppermute | solution.py:410
  2.0 6.0 %collective-permute-start = (f32[64,256]{1,0:T(8,128)S(1)}, f32[64,256]{1,0:T(8,128)S(1)}, u32[]{:S(2)}, u32[]{:S(2)}) collective-permute-start(f32[64,256]{1,0:T(8,128)S(1)} %get-tuple-element.26), channel_id=1, source_target_pairs={{1,2},{2,1},{3,4},{4,3},{5,6},{6,5},{9,10},{10,9},{11,12},{12,11},... | collective-permute-start | bytes 196616 | tf_op jit(solution)/shard_map/ppermute | solution.py:411
  6.1 5.0 %collective-permute-start.1 = (f32[64,256]{1,0:T(8,128)S(1)}, f32[64,256]{1,0:T(8,128)S(1)}, u32[]{:S(2)}, u32[]{:S(2)}) collective-permute-start(f32[64,256]{1,0:T(8,128)S(1)} %get-tuple-element.26), channel_id=1, source_target_pairs={{7,7},{31,15},{23,23},{15,31}} | collective-permute-start | bytes 196616 | tf_op jit(solution)/shard_map/ppermute | solution.py:412
  8.0 3.1 %copy-start.4 = (s32[256]{0:T(256)S(1)}, s32[256]{0:T(256)}, u32[]{:S(2)}) copy-start(s32[256]{0:T(256)} %param.9) | copy-start | bytes 3076
  8.4 5.4 %collective-permute-start.3 = (f32[72,128]{1,0:T(8,128)S(1)}, f32[72,128]{1,0:T(8,128)S(1)}, u32[]{:S(2)}, u32[]{:S(2)}) collective-permute-start(f32[72,128]{1,0:T(8,128)S(1)} %get-tuple-element.41), channel_id=1, source_target_pairs={{8,16},{16,8},{9,17},{17,9},{10,18},{18,10},{11,19},{19,11},{12,20... | collective-permute-start | bytes 110600 | tf_op jit(solution)/shard_map/ppermute | solution.py:427
  11.1 3.0 %collective-permute-start.4 = (f32[72,128]{1,0:T(8,128)S(1)}, f32[72,128]{1,0:T(8,128)S(1)}, u32[]{:S(2)}, u32[]{:S(2)}) collective-permute-start(f32[72,128]{1,0:T(8,128)S(1)} %get-tuple-element.42), channel_id=1, source_target_pairs={{0,8},{8,0},{1,9},{9,1},{2,10},{10,2},{3,11},{11,3},{4,12},{12,4},... | collective-permute-start | bytes 110600 | tf_op jit(solution)/shard_map/ppermute | solution.py:426

commit v6 on v5

--- a/solution.py
+++ b/solution.py
@@ -51,28 +51,49 @@
     for copy in copies:
         copy.wait()
 
-    @pl.loop(0, LEVELS)
-    def _(l):
-        for c in range(2):
-            both = []
-            for k in range(2):
-                w = m_ref[k, l, :, cols(c)].astype(jnp.float32)
-                values = [s_ref[k, f, l, :, cols(c)] * w for f in range(FIELDS)]
-                both.append(values + [0.5 * u_ref[k, l, :, cols(c)], 0.5 * v_ref[k, l, :, cols(c)], w, w])
-            for g in range(2):
-                low, high = both[0][4 * g], pltpu.roll(both[1][4 * g], 2, 0)
-                for k in range(1, 4):
-                    low = jnp.where(sub // 2 == k, pltpu.roll(both[0][4 * g + k], 2 * k, 0), low)
-                    high = jnp.where(sub // 2 == k, pltpu.roll(both[1][4 * g + k], (2 * k + 2) % SUBS, 0), high)
-                a_ref[rows(2 * l + g), cols(c)] = jnp.where(lat_even, high, low)
-                b_ref[rows(2 * l + g), cols(c)] = jnp.where(lat_even, low, high)
-
-
-def insert(packs, quarter, l, q, side, tile):
+    def put(t, c, values, where):
+        low = high = jnp.zeros((SUBS, LANES), jnp.float32)
+        for (south, north), (first, count) in zip(values, where):
+            here = (sub >= first) & (sub < first + count)
+            low = jnp.where(here, pltpu.roll(south, first, 0) if first else south, low)
+            high = jnp.where(here, pltpu.roll(north, (first + count) % SUBS, 0) if (first + count) % SUBS else north, high)
+        a_ref[rows(t), cols(c)] = jnp.where(lat_even, high, low)
+        b_ref[rows(t), cols(c)] = jnp.where(lat_even, low, high)
+
+    for c in range(2):
+
+        @pl.loop(0, LEVELS)
+        def _(l):
+            w = [m_ref[k, l, :, cols(c)].astype(jnp.float32) for k in range(2)]
+            values = [[s_ref[k, f, l, :, cols(c)] * w[k] for k in range(2)] for f in range(FIELDS)]
+            put(l, c, values, [(2 * f, 2) for f in range(FIELDS)])
+
+        u, v, w = (
+            [[ref[k, l, :, cols(c)].astype(jnp.float32) for k in range(2)] for l in range(LEVELS)]
+            for ref in (u_ref, v_ref, m_ref)
+        )
+        put(LEVELS, c, [[0.5 * x for x in pair] for pair in v], [(2 * l, 2) for l in range(LEVELS)])
+        values = [[0.5 * x for x in pair] for pair in u] + w
+        put(LEVELS + 1, c, values, [(l, 1) for l in range(2 * LEVELS)])
+
+
+def place_in_message(l, q):
+    if q < FIELDS:
+        return SUBS * l + 2 * q, 2
+    if q == FIELDS + 1:
+        return SUBS * LEVELS + 2 * l, 2
+    return SUBS * (LEVELS + 1) + l + (LEVELS if q > FIELDS else 0), 1
+
+
+def insert(packs, lane, l, q, tile):
     seg = LEVELS * (q % 2) + l if q < FIELDS else l
     g = q // 2 if q < FIELDS else q - 2
-    moved = pltpu.roll(tile, (16 * seg + (12 if side else 4)) % LANES, 1)
-    packs[g] = jnp.where(quarter == 4 * seg + 1 + side, moved, packs[g])
+    sides = pltpu.roll(jnp.where(lane < LANES // 2, tile[0], tile[1]), (16 * seg + 8) % LANES, 1)
+    packs[g] = jnp.where((lane + 4) // 8 == 2 * seg + 1, sides, packs[g])
+
+
+def arrange(pack, lane):
+    return jnp.where(lane // 4 % 4 == 1, pltpu.roll(pack, LANES - 4, 1), pltpu.roll(pack, 4, 1))
 
 
 def finish(packs, lane):
@@ -85,17 +106,16 @@
     west = jnp.zeros((SUBS, LANES), jnp.float32)
     pair = lane // 2 % 8
     for g, tile in enumerate(packs):
-        east = jnp.where(pair == 1 + g, pltpu.roll(tile, LANES - 8 + 2 * g, 1), east)
-        first = pltpu.roll(tile, 8 + 2 * g, 1)
+        east = jnp.where(pair == 1 + g, pltpu.roll(tile, (LANES - 4 + 2 * g) % LANES, 1) if g != 2 else tile, east)
+        first = pltpu.roll(tile, 4 + 2 * g, 1)
         if seam_rows is not None:
-            first = jnp.where(seam_rows, pltpu.roll(tile, 1 + 2 * g, 1), first)
+            first = jnp.where(seam_rows, pltpu.roll(tile, 5 + 2 * g, 1), first)
         west = jnp.where(pair == (6 + g) % 8, first, west)
     return jnp.where(lon_even, east, west), jnp.where(lon_even, west, east)
 
 
 def prepare_kernel(s_ref, u_ref, v_ref, m_ref, r_ref, u2_ref, v2_ref, w_ref, k_ref, p_ref, q_ref):
     lane = iota(1)
-    quarter = lane // 4
     lon_even = lax.axis_index("lon") % 2 == 0
 
     @pl.loop(0, s_ref.shape[2] // SUBS, unroll=2)
@@ -103,17 +123,21 @@
         src, dst = rows(t), rows(t + OWN)
         packs = [jnp.zeros((SUBS, LANES), jnp.float32)] * 5
         for l in range(LEVELS):
-            for c in range(2):
-                w = m_ref[l, src, cols(c)].astype(jnp.float32)
-                values = [s_ref[f, l, src, cols(c)] * w for f in range(FIELDS)]
-                values += [0.5 * u_ref[l, src, cols(c)], 0.5 * v_ref[l, src, cols(c)], w]
-                for q, value in enumerate(values):
-                    ref = (u2_ref, v2_ref, w_ref)[q - FIELDS] if q >= FIELDS else r_ref
-                    ref[LEVELS * q + l if q < FIELDS else l, c, dst, :] = value
-                    insert(packs, quarter, l, q, c, value)
+            w = [m_ref[l, src, cols(c)].astype(jnp.float32) for c in range(2)]
+            for q in range(QN):
+                if q < FIELDS:
+                    ref, index, tile = r_ref, LEVELS * q + l, [s_ref[q, l, src, cols(c)] * w[c] for c in range(2)]
+                elif q < FIELDS + 2:
+                    ref, index, x_ref = (u2_ref, v2_ref)[q - FIELDS], l, (u_ref, v_ref)[q - FIELDS]
+                    tile = [0.5 * x_ref[l, src, cols(c)] for c in range(2)]
+                else:
+                    ref, index, tile = w_ref, l, w
+                for c in range(2):
+                    ref[index, c, dst, :] = tile[c]
+                insert(packs, lane, l, q, tile)
         finish(packs, lane)
         for g in range(5):
-            k_ref[g, src, :] = packs[g]
+            k_ref[g, src, :] = arrange(packs[g], lane)
         p_ref[src, :], q_ref[src, :] = outgoing(packs, lane, lon_even)
 
 
@@ -128,12 +152,11 @@
     r_ref, u2_ref, v2_ref, w_ref, k_ref, p_ref, q_ref, north, south,
 ):
     lane, sub = iota(1), iota(0)
-    quarter = lane // 4
     lat_even, top = lat_place()
     lon_even = lax.axis_index("lon") % 2 == 0
     tiles = k_ref.shape[1] // SUBS - 1
 
-    @pl.loop(0, 2 * LEVELS)
+    @pl.loop(0, LEVELS + 2, unroll=True)
     def _(i):
         for c in range(2):
             a, b = a_ref[rows(i), cols(c)], b_ref[rows(i), cols(c)]
@@ -145,17 +168,17 @@
         for q in range(QN):
             ref = (u2_ref, v2_ref, w_ref)[q - FIELDS] if q >= FIELDS else r_ref
             index = LEVELS * q + l if q < FIELDS else l
-            at = SUBS + 16 * l + 2 * q
+            first, count = place_in_message(l, q)
+            at, at_south = pl.ds(SUBS + first, SUBS), pl.ds(first + count, SUBS)
             tile = []
             for c in range(2):
-                tile.append(jnp.where(sub < 4, north[c, pl.ds(at, SUBS), :], south[c, pl.ds(at - 6, SUBS), :]))
+                tile.append(jnp.where(sub < 4, north[c, at, :], south[c, at_south, :]))
                 ref[index, c, rows(SOUTH), :] = tile[c]
                 ref[index, c, rows(tiles + OWN), :] = tile[c]
-            for c in range(2):
-                insert(packs, quarter, l, q, c, tile[c])
+            insert(packs, lane, l, q, tile)
     finish(packs, lane)
     for g in range(5):
-        k_ref[g, rows(tiles), :] = packs[g]
+        k_ref[g, rows(tiles), :] = arrange(packs[g], lane)
     p_ref[rows(tiles), :], q_ref[rows(tiles), :] = outgoing(packs, lane, lon_even, top & (sub < 2))
 
 
@@ -163,7 +186,6 @@
     c_ref, b_ref, f_ref, r_in, u2_in, v2_in, w_in, k_in, r_ref, u2_ref, v2_ref, w_ref, k_ref, mirrored
 ):
     lane, sub = iota(1), iota(0)
-    quarter = lane // 4
     _, top = lat_place()
     width = b_ref.shape[1]
     tiles = k_ref.shape[1] // SUBS - 1
@@ -174,39 +196,40 @@
         before = jnp.broadcast_to(source[0][:, :1] + 1, (SUBS, LANES))
         after = jnp.broadcast_to(jnp.maximum(source[1][:, LANES - 1 :] - 1, 0), (SUBS, LANES))
 
-        @pl.loop(0, LEVELS, unroll=True)
-        def _(l):
-            for g in range(2):
-                raw = [(b_ref if s < 2 else f_ref)[rows(2 * l + g), cols(s % 2)] for s in range(4)]
-                for c, p in enumerate((*source, before, after)):
-                    got = jnp.zeros((SUBS, LANES), jnp.float32)
-                    for s in range(4):
-                        picked = jnp.take_along_axis(raw[s], p % LANES, axis=1, mode="promise_in_bounds")
-                        got = jnp.where(p // LANES == s, picked, got)
-                    swapped = jnp.where(sub % 2 == 0, pltpu.roll(got, SUBS - 1, 0), pltpu.roll(got, 1, 0))
-                    if g == 1:
-                        swapped = jnp.where(sub == 2, -got, jnp.where(sub == 3, got, swapped))
-                    mirrored[c, rows(2 * l + g), :] = swapped
-
-        packs = [jnp.zeros((SUBS, LANES), jnp.float32)] * 5
+        for t in range(LEVELS + 2):
+            raw = [(b_ref if s < 2 else f_ref)[rows(t), cols(s % 2)] for s in range(4)]
+            for c, p in enumerate((*source, before, after)):
+                got = jnp.zeros((SUBS, LANES), jnp.float32)
+                for s in range(4):
+                    picked = jnp.take_along_axis(raw[s], p % LANES, axis=1, mode="promise_in_bounds")
+                    got = jnp.where(p // LANES == s, picked, got)
+                if t < LEVELS:
+                    got = jnp.where(sub % 2 == 0, pltpu.roll(got, SUBS - 1, 0), pltpu.roll(got, 1, 0))
+                elif t == LEVELS:
+                    got = jnp.where(sub % 2 == 0, -got, got)
+                mirrored[c, rows(t), :] = got
+
+        packs, halo = ([jnp.zeros((SUBS, LANES), jnp.float32)] * 5 for _ in range(2))
         for l in range(LEVELS):
             for q in range(QN):
                 ref = (u2_ref, v2_ref, w_ref)[q - FIELDS] if q >= FIELDS else r_ref
                 index = LEVELS * q + l if q < FIELDS else l
                 seg = LEVELS * (q % 2) + l if q < FIELDS else l
                 pack = q // 2 if q < FIELDS else q - 2
-                tile = [mirrored[c, pl.ds(16 * l + 2 * q, SUBS), :] for c in range(4)]
+                tile = [mirrored[c, pl.ds(place_in_message(l, q)[0], SUBS), :] for c in range(4)]
+                insert(packs, lane, l, q, tile)
                 for c in range(2):
-                    insert(packs, quarter, l, q, c, tile[c])
                     north = tile[c]
                     if q == FIELDS:
                         north = -pltpu.roll(jnp.where(lane == 0, tile[1 - c], tile[c]), LANES - 1, 1)
                     ref[index, c, rows(tiles + OWN), :] = north
-                packs[pack] = jnp.where(lane == 16 * seg + 3, tile[2], packs[pack])
-                packs[pack] = jnp.where(lane == 16 * seg + 12, tile[3], packs[pack])
+                halo[pack] = jnp.where(lane == 16 * seg + 3, tile[2], halo[pack])
+                halo[pack] = jnp.where(lane == 16 * seg + 12, tile[3], halo[pack])
         finish(packs, lane)
+        finish(halo, lane)
         for g in range(5):
-            k_ref[g, rows(tiles), :] = jnp.where(sub < 2, packs[g], k_in[g, rows(tiles), :])
+            value = jnp.where((lane % 16 == 3) | (lane % 16 == 12), halo[g], arrange(packs[g], lane))
+            k_ref[g, rows(tiles), :] = jnp.where(sub < 2, value, k_in[g, rows(tiles), :])
 
 
 def seam(r, r_mirror, h, h_mirror, w, sign):
@@ -310,7 +333,7 @@
     for g, value in enumerate(join(tiles)):
         z[g, rows(SOUTH), :] = value
         crossed = pltpu.roll(jnp.where(lon_even, p, q), (LANES - 2 * g) % LANES, 1) if g else jnp.where(lon_even, p, q)
-        if g != 3:
+        if g < 2:
             crossed = pltpu.roll(crossed, SUBS - 1, 0)
         kept = jnp.where((pair == 6) & at_seam, crossed, k_ref[g, rows(tiles), :])
         value = jnp.where(top & (sub < 2), kept, value)
@@ -396,7 +419,7 @@
         )(*(held(x) for x in args))
 
     inputs = (state_adjoint, east_velocity, north_velocity, ocean_mask)
-    message = (16 * levels, width)
+    message = (SUBS * (levels + 2), width)
     to_a, to_b = pl.pallas_call(
         row_kernel,
         out_shape=(pltpu.VMEM(message, f32), pltpu.VMEM(message, f32)),

time: 15.8 us -> 15.6 us (0.987)
  Pallas kernels: 7.01 us -> 6.79 us
    pallas_call x4, Pallas kernels: 4.22 us -> 3.97 us  [call(): pl.pallas_call(kernel, out_shape=tuple((pltpu.VMEM(shape, f32) for shape...]
  transfers between devices with their start and end apart: 5 -> 5, of which waited for: 1 -> 1; matrix products, arithmetic and copies ran while one was open for 0% -> 0% of each run, Pallas kernels for 27% -> 26%
where the time goes in v6:
time: 15.6 us; the launch traced here: 15.5 us
  starting transfers between devices  8.22 us (53%)
  Pallas kernels  6.79 us (44%)
  waiting for transfers between devices  0.29 us (2%)
    ppermute x1, starting transfers between devices, per_device(): from_b = lax.ppermute(to_b, axes, across + fold)  4.06 us
    pallas_call x4, Pallas kernels, call(): pl.pallas_call(kernel, out_shape=tuple((pltpu.VMEM(shape, f32) for shape...  3.97 us
    ppermute x1, starting transfers between devices, per_device(): from_q = lax.ppermute(to_q, axes, odd)  2.75 us
    pallas_call x1, Pallas kernels, per_device(): pl.pallas_call(edge_kernel, out_shape=jax.ShapeDtypeStruct(state_adjoint....  1.54 us
    pallas_call x1, Pallas kernels, per_device(): pl.pallas_call(row_kernel, out_shape=(pltpu.VMEM(message, f32), pltpu.VME...  1.28 us
    ppermute x1, starting transfers between devices, per_device(): from_a = lax.ppermute(to_a, axes, within)  0.74 us
    ppermute x1, starting transfers between devices, per_device(): from_f = lax.ppermute(to_b, axes, fold_next)  0.66 us
  transfers between devices with their start and end apart: 5, of which 1 were waited for; matrix products, arithmetic and copies ran while one was open for 0% of the time, Pallas kernels for 26%

profile of v6, /device:TPU:25, one launch (start us, length us, event | category | flops | bytes accessed | tf_op | source)
XLA Modules:
  0.0 15.5 jit_solution(10053701530976562391)
XLA Ops:
  0.0 0.0 copy-start.3
  0.0 0.0 copy-start.2
  0.0 0.0 copy-start.1
  0.0 0.0 copy-start
  0.0 1.3 %pack_rows.1 = (f32[48,256]{1,0:T(8,128)S(1)}, f32[48,256]{1,0:T(8,128)S(1)}) custom-call(f32[4,4,64,256]{3,2,1,0:T(8,128)} %s_ref.1, f32[4,64,256]{2,1,0:T(8,128)} %u_ref.1, f32[4,64,256]{2,1,0:T(8,128)} %v_ref.1, s32[4,64,256]{2,1,0:T(8,128)} %m_ref.1), custom_call_target="tpu_custom_call" | custom-call | tf_op jit(solution)/shard_map/pack_rows/pallas_call | solution.py:423
  1.3 0.7 %collective-permute-start.2 = (f32[48,256]{1,0:T(8,128)S(1)}, f32[48,256]{1,0:T(8,128)S(1)}, u32[]{:S(2)}, u32[]{:S(2)}) collective-permute-start(f32[48,256]{1,0:T(8,128)S(1)} %get-tuple-element.27), channel_id=1, source_target_pairs={{0,1},{1,0},{2,3},{3,2},{4,5},{5,4},{6,7},{7,6},{8,9},{9,8},{10,11... | collective-permute-start | bytes 147464 | tf_op jit(solution)/shard_map/ppermute | solution.py:433
  2.0 4.1 %collective-permute-start = (f32[48,256]{1,0:T(8,128)S(1)}, f32[48,256]{1,0:T(8,128)S(1)}, u32[]{:S(2)}, u32[]{:S(2)}) collective-permute-start(f32[48,256]{1,0:T(8,128)S(1)} %get-tuple-element.26), channel_id=1, source_target_pairs={{1,2},{2,1},{3,4},{4,3},{5,6},{6,5},{9,10},{10,9},{11,12},{12,11},... | collective-permute-start | bytes 147464 | tf_op jit(solution)/shard_map/ppermute | solution.py:434
  6.1 0.7 %collective-permute-start.1 = (f32[48,256]{1,0:T(8,128)S(1)}, f32[48,256]{1,0:T(8,128)S(1)}, u32[]{:S(2)}, u32[]{:S(2)}) collective-permute-start(f32[48,256]{1,0:T(8,128)S(1)} %get-tuple-element.26), channel_id=1, source_target_pairs={{7,7},{31,15},{23,23},{15,31}} | collective-permute-start | bytes 147464 | tf_op jit(solution)/shard_map/ppermute | solution.py:435
  6.8 0.0 copy-done.3
  6.8 0.0 copy-done.2
  6.8 0.0 copy-done.1
  6.8 0.0 copy-done
  6.8 1.1 %prepare.1 = (f32[16,2,96,128]{3,2,1,0:T(8,128)S(1)}, f32[4,2,96,128]{3,2,1,0:T(8,128)S(1)}, f32[4,2,96,128]{3,2,1,0:T(8,128)S(1)}, f32[4,2,96,128]{3,2,1,0:T(8,...) custom-call(f32[4,4,64,256]{3,2,1,0:T(8,128)S(1)} %copy-done, ...), custom_call_target="tpu_custom_call" | custom-call | bytes 3000000 | tf_op jit(solution)/shard_map/prepare/pallas_call | solution.py:409
  7.9 0.0 copy-start.4
  7.9 0.0 collective-permute-done.2.a_ref
  7.9 0.0 collective-permute-done.b_ref
  8.0 0.2 %place_rows.1 = (f32[16,2,96,128]{3,2,1,0:T(8,128)S(1)}, f32[4,2,96,128]{3,2,1,0:T(8,128)S(1)}, f32[4,2,96,128]{3,2,1,0:T(8,128)S(1)}, f32[4,2,96,128]{3,2,1,0:T...) custom-call(f32[48,256]{1,0:T(8,128)S(1)} %collective-permute-done.2, ...), custom_call_target="tpu_custom_call", output_to_operand_aliasing={{0}: (2, {}), {1}: (3, {}), {2}: (4, {}), {3}: (5, {}), {4}... | custom-call | bytes 3000000 | tf_op jit(solution)/shard_map/place_rows/pallas_call | solution.py:409
  8.2 2.7 %collective-permute-start.3 = (f32[72,128]{1,0:T(8,128)S(1)}, f32[72,128]{1,0:T(8,128)S(1)}, u32[]{:S(2)}, u32[]{:S(2)}) collective-permute-start(f32[72,128]{1,0:T(8,128)S(1)} %get-tuple-element.41), channel_id=1, source_target_pairs={{8,16},{16,8},{9,17},{17,9},{10,18},{18,10},{11,19},{19,11},{12,20... | collective-permute-start | bytes 110600 | tf_op jit(solution)/shard_map/ppermute | solution.py:450
  11.0 0.0 collective-permute-start.4
  11.0 0.0 collective-permute-done.1.f_ref
  11.0 0.0 copy-done.4
  11.0 0.4 %mirror_rows.1 = (f32[16,2,96,128]{3,2,1,0:T(8,128)S(1)}, f32[4,2,96,128]{3,2,1,0:T(8,128)S(1)}, f32[4,2,96,128]{3,2,1,0:T(8,128)S(1)}, f32[4,2,96,128]{3,2,1,0:T(8,128)S(1)}, f32[5,72,128]{2,1,0:T(8,128)S(1)}) custom-call(s32[2,128]{1,0:T(2,128)S(1)} %bitcast.1, ...), custom_call_target="tpu_custom_call", output_to_operand_aliasing={{0}: (3, {}), {1}: (4, {}), {2}: (5, {}), {3}: (6, {}), {4}... | custom-call | bytes 3000000 | tf_op jit(solution)/shard_map/mirror_rows/pallas_call | solution.py:409
  11.4 2.2 %both_steps.1.i_ref = f32[4,4,64,256]{3,2,1,0:T(8,128)S(1)} custom-call(f32[16,2,96,128]{3,2,1,0:T(8,128)S(1)} %get-tuple-element.43.r_ref, f32[4,2,96,128]{3,2,1,0:T(8,128)S(1)} %get-tuple-element.44.u2_ref, f32[4,2,96,128]{3,2,1,0:T(8,128)S(1)} %get-tuple-element.45.v2_ref, f32[4,2,96,128]{3,2,1,0:T(8,128)S(1)} %get-tuple-element.46.w_ref), custom_call_target="tpu_custom_call" | custom-call | bytes 9000000 | tf_op jit(solution)/shard_map/both_steps/pallas_call | solution.py:409
  13.6 0.0 collective-permute-done.3.q_ref
  13.6 0.3 %collective-permute-done.4.p_ref = f32[72,128]{1,0:T(8,128)S(1)} collective-permute-done((f32[72,128]{1,0:T(8,128)S(1)}, f32[72,128]{1,0:T(8,128)S(1)}, u32[]{:S(2)}, u32[]{:S(2)}) %collective-permute-start.4) | collective-permute-done | bytes 36896 | tf_op jit(solution)/shard_map/ppermute | solution.py:449
  13.9 1.5 %edge_columns.1 = f32[4,4,64,256]{3,2,1,0:T(8,128)} custom-call(s32[2,128]{1,0:T(2,128)S(1)} %bitcast.2, f32[5,72,128]{2,1,0:T(8,128)S(1)} %get-tuple-element.40.k_ref, f32[72,128]{1,0:T(8,128)S(1)} %collective-permute-done.3.q_ref, f32[72,128]{1,0:T(8,128)S(1)} %collective-permute-done.4.p_ref, f32[4,4,64,256]{3,2,1,0:T(8,128)S(1)} %both_steps.1.i_ref), custom_call_target="tpu_custom_call" | custom-call | tf_op jit(solution)/shard_map/edge_columns/pallas_call | solution.py:462
Async XLA Ops:
  0.0 6.8 %copy-start.3 = (s32[4,64,256]{2,1,0:T(8,128)S(1)}, s32[4,64,256]{2,1,0:T(8,128)}, u32[]{:S(2)}) copy-start(s32[4,64,256]{2,1,0:T(8,128)} %m_ref.1) | copy-start | bytes 786436
  0.0 6.8 %copy-start.2 = (f32[4,64,256]{2,1,0:T(8,128)S(1)}, f32[4,64,256]{2,1,0:T(8,128)}, u32[]{:S(2)}) copy-start(f32[4,64,256]{2,1,0:T(8,128)} %v_ref.1) | copy-start | bytes 786436
  0.0 6.8 %copy-start.1 = (f32[4,64,256]{2,1,0:T(8,128)S(1)}, f32[4,64,256]{2,1,0:T(8,128)}, u32[]{:S(2)}) copy-start(f32[4,64,256]{2,1,0:T(8,128)} %u_ref.1) | copy-start | bytes 786436
  0.0 6.8 %copy-start = (f32[4,4,64,256]{3,2,1,0:T(8,128)S(1)}, f32[4,4,64,256]{3,2,1,0:T(8,128)}, u32[]{:S(2)}) copy-start(f32[4,4,64,256]{3,2,1,0:T(8,128)} %s_ref.1) | copy-start | bytes 3145732
  1.3 6.6 %collective-permute-start.2 = (f32[48,256]{1,0:T(8,128)S(1)}, f32[48,256]{1,0:T(8,128)S(1)}, u32[]{:S(2)}, u32[]{:S(2)}) collective-permute-start(f32[48,256]{1,0:T(8,128)S(1)} %get-tuple-element.27), channel_id=1, source_target_pairs={{0,1},{1,0},{2,3},{3,2},{4,5},{5,4},{6,7},{7,6},{8,9},{9,8},{10,11... | collective-permute-start | bytes 147464 | tf_op jit(solution)/shard_map/ppermute | solution.py:433
  2.0 5.9 %collective-permute-start = (f32[48,256]{1,0:T(8,128)S(1)}, f32[48,256]{1,0:T(8,128)S(1)}, u32[]{:S(2)}, u32[]{:S(2)}) collective-permute-start(f32[48,256]{1,0:T(8,128)S(1)} %get-tuple-element.26), channel_id=1, source_target_pairs={{1,2},{2,1},{3,4},{4,3},{5,6},{6,5},{9,10},{10,9},{11,12},{12,11},... | collective-permute-start | bytes 147464 | tf_op jit(solution)/shard_map/ppermute | solution.py:434
  6.1 4.8 %collective-permute-start.1 = (f32[48,256]{1,0:T(8,128)S(1)}, f32[48,256]{1,0:T(8,128)S(1)}, u32[]{:S(2)}, u32[]{:S(2)}) collective-permute-start(f32[48,256]{1,0:T(8,128)S(1)} %get-tuple-element.26), channel_id=1, source_target_pairs={{7,7},{31,15},{23,23},{15,31}} | collective-permute-start | bytes 147464 | tf_op jit(solution)/shard_map/ppermute | solution.py:435
  7.9 3.0 %copy-start.4 = (s32[256]{0:T(256)S(1)}, s32[256]{0:T(256)}, u32[]{:S(2)}) copy-start(s32[256]{0:T(256)} %param.9) | copy-start | bytes 3076
  8.2 5.4 %collective-permute-start.3 = (f32[72,128]{1,0:T(8,128)S(1)}, f32[72,128]{1,0:T(8,128)S(1)}, u32[]{:S(2)}, u32[]{:S(2)}) collective-permute-start(f32[72,128]{1,0:T(8,128)S(1)} %get-tuple-element.41), channel_id=1, source_target_pairs={{8,16},{16,8},{9,17},{17,9},{10,18},{18,10},{11,19},{19,11},{12,20... | collective-permute-start | bytes 110600 | tf_op jit(solution)/shard_map/ppermute | solution.py:450
  11.0 3.0 %collective-permute-start.4 = (f32[72,128]{1,0:T(8,128)S(1)}, f32[72,128]{1,0:T(8,128)S(1)}, u32[]{:S(2)}, u32[]{:S(2)}) collective-permute-start(f32[72,128]{1,0:T(8,128)S(1)} %get-tuple-element.42), channel_id=1, source_target_pairs={{0,8},{8,0},{1,9},{9,1},{2,10},{10,2},{3,11},{11,3},{4,12},{12,4},... | collective-permute-start | bytes 110600 | tf_op jit(solution)/shard_map/ppermute | solution.py:449

commit v7 on v6

--- a/solution.py
+++ b/solution.py
@@ -11,7 +11,7 @@
 SOUTH, OWN = 1, 2
 VMEM = pl.BlockSpec(memory_space=pltpu.VMEM)
 SCOPED = 4 << 20
-UNROLL1, UNROLL2 = 10, 8
+UNROLL = 8
 
 
 def iota(dim):
@@ -101,16 +101,25 @@
         packs[g] = jnp.where(lane < LANES // 2, packs[g], pltpu.roll(packs[g], LANES // 2, 1))
 
 
-def outgoing(packs, lane, lon_even, seam_rows=None):
-    east = jnp.zeros((SUBS, LANES), jnp.float32)
-    west = jnp.zeros((SUBS, LANES), jnp.float32)
-    pair = lane // 2 % 8
-    for g, tile in enumerate(packs):
-        east = jnp.where(pair == 1 + g, pltpu.roll(tile, (LANES - 4 + 2 * g) % LANES, 1) if g != 2 else tile, east)
-        first = pltpu.roll(tile, 4 + 2 * g, 1)
+def turn(tile, by):
+    by %= LANES
+    return pltpu.roll(tile, by, 1) if by else tile
+
+
+def slots(lane):
+    slot = lane % 8
+    return [(slot // 2 == g, 2 * g) for g in range(3)] + [(slot == 6, 6), (slot == 7, 7)]
+
+
+def outgoing(packs, lane, lon_even, half, seam_rows=None):
+    east = west = jnp.zeros((SUBS, LANES), jnp.float32)
+    for g, (here, first) in enumerate(slots(lane)):
+        to = first + 8 * half
+        west_part = turn(packs[g], to - 8)
         if seam_rows is not None:
-            first = jnp.where(seam_rows, pltpu.roll(tile, 5 + 2 * g, 1), first)
-        west = jnp.where(pair == (6 + g) % 8, first, west)
+            west_part = jnp.where(seam_rows, turn(packs[g], to - 7), west_part)
+        west = jnp.where(here, west_part, west)
+        east = jnp.where(here, turn(packs[g], to - (6 if g < 3 else 7)), east)
     return jnp.where(lon_even, east, west), jnp.where(lon_even, west, east)
 
 
@@ -118,27 +127,31 @@
     lane = iota(1)
     lon_even = lax.axis_index("lon") % 2 == 0
 
-    @pl.loop(0, s_ref.shape[2] // SUBS, unroll=2)
-    def _(t):
-        src, dst = rows(t), rows(t + OWN)
-        packs = [jnp.zeros((SUBS, LANES), jnp.float32)] * 5
-        for l in range(LEVELS):
-            w = [m_ref[l, src, cols(c)].astype(jnp.float32) for c in range(2)]
-            for q in range(QN):
-                if q < FIELDS:
-                    ref, index, tile = r_ref, LEVELS * q + l, [s_ref[q, l, src, cols(c)] * w[c] for c in range(2)]
-                elif q < FIELDS + 2:
-                    ref, index, x_ref = (u2_ref, v2_ref)[q - FIELDS], l, (u_ref, v_ref)[q - FIELDS]
-                    tile = [0.5 * x_ref[l, src, cols(c)] for c in range(2)]
-                else:
-                    ref, index, tile = w_ref, l, w
-                for c in range(2):
-                    ref[index, c, dst, :] = tile[c]
-                insert(packs, lane, l, q, tile)
-        finish(packs, lane)
-        for g in range(5):
-            k_ref[g, src, :] = arrange(packs[g], lane)
-        p_ref[src, :], q_ref[src, :] = outgoing(packs, lane, lon_even)
+    @pl.loop(0, s_ref.shape[2] // SUBS // 2)
+    def _(pair):
+        sent = []
+        for half in range(2):
+            src, dst = rows(2 * pair + half), rows(2 * pair + half + OWN)
+            packs = [jnp.zeros((SUBS, LANES), jnp.float32)] * 5
+            for l in range(LEVELS):
+                w = [m_ref[l, src, cols(c)].astype(jnp.float32) for c in range(2)]
+                for q in range(QN):
+                    if q < FIELDS:
+                        ref, index, tile = r_ref, LEVELS * q + l, [s_ref[q, l, src, cols(c)] * w[c] for c in range(2)]
+                    elif q < FIELDS + 2:
+                        ref, index, x_ref = (u2_ref, v2_ref)[q - FIELDS], l, (u_ref, v_ref)[q - FIELDS]
+                        tile = [0.5 * x_ref[l, src, cols(c)] for c in range(2)]
+                    else:
+                        ref, index, tile = w_ref, l, w
+                    for c in range(2):
+                        ref[index, c, dst, :] = tile[c]
+                    insert(packs, lane, l, q, tile)
+            finish(packs, lane)
+            for g in range(5):
+                k_ref[g, src, :] = arrange(packs[g], lane)
+            sent.append(outgoing(packs, lane, lon_even, half))
+        for ref, low, high in zip((p_ref, q_ref), *sent):
+            ref[rows(pair), :] = jnp.where(lane % 16 < 8, low, high)
 
 
 def partner_columns(c_ref, width):
@@ -179,7 +192,8 @@
     finish(packs, lane)
     for g in range(5):
         k_ref[g, rows(tiles), :] = arrange(packs[g], lane)
-    p_ref[rows(tiles), :], q_ref[rows(tiles), :] = outgoing(packs, lane, lon_even, top & (sub < 2))
+    to = rows(tiles // 2)
+    p_ref[to, :], q_ref[to, :] = outgoing(packs, lane, lon_even, 0, top & (sub < 2))
 
 
 def mirror_kernel(
@@ -240,29 +254,42 @@
     return w * (sign * (0.5 + h_top) * r_top - h * r - h_top * (r - r_top))
 
 
-def step_kernel(r_ref, u2_ref, v2_ref, w_ref, o_ref, r1):
+def step_kernel(r_ref, u2_ref, v2_ref, w_ref, o_ref, r1, uw):
     lane, sub = iota(1), iota(0)
     _, top = lat_place()
     tiles = o_ref.shape[2] // SUBS
     end = OWN + tiles
 
-    def update(l, t, load):
-        u = [u2_ref[l, c, rows(t), :] for c in range(2)]
-        u_west = [pltpu.roll(jnp.where(lane == LANES - 1, u[1 - c], u[c]), 1, 1) for c in range(2)]
-        v = [v2_ref[l, c, rows(t), :] for c in range(2)]
-        v_south = [v2_ref[l, c, rows(t, -1), :] for c in range(2)]
-        w = [w_ref[l, c, rows(t), :] for c in range(2)]
+    def update(l, look, load, first):
+        def of(ref, c):
+            return lambda at: ref[l, c, at, :]
+
+        u = [look(of(u2_ref, c), 0) for c in range(2)]
+        if first:
+            u_west = [pltpu.roll(jnp.where(lane == LANES - 1, u[1 - c], u[c]), 1, 1) for c in range(2)]
+        else:
+            u_west = [look(lambda at, c=c: uw[c, at, :], 0) for c in range(2)]
+        v = [look(of(v2_ref, c), 0) for c in range(2)]
+        v_south = [look(of(v2_ref, c), -1) for c in range(2)]
+        w = [look(of(w_ref, c), 0) for c in range(2)]
         out = []
         for f in range(FIELDS):
-            r = [load(f, c, rows(t)) for c in range(2)]
+            reads = [lambda at, c=c: load(f, c, at) for c in range(2)]
+            r = [look(read, 0) for read in reads]
             for c in range(2):
                 ahead = pltpu.roll(jnp.where(lane == 0, r[1 - c], r[c]), LANES - 1, 1)
                 behind = pltpu.roll(jnp.where(lane == LANES - 1, r[1 - c], r[c]), 1, 1)
                 along = u[c] * (ahead - r[c]) + u_west[c] * (r[c] - behind)
-                up = v[c] * (load(f, c, rows(t, 1)) - r[c])
-                down = v_south[c] * (r[c] - load(f, c, rows(t, -1)))
+                up = v[c] * (look(reads[c], 1) - r[c])
+                down = v_south[c] * (r[c] - look(reads[c], -1))
                 out.append((f, c, w[c] * (r[c] + along + up + down)))
-        return out
+        return out, u_west
+
+    def tile(t):
+        return lambda read, by: read(rows(t, by))
+
+    def outside(read, by):
+        return jnp.where(sub < SUBS // 2, read(rows(end, by)), read(rows(SOUTH, by)))
 
     @pl.loop(0, LEVELS)
     def _(l):
@@ -272,9 +299,16 @@
         def second(f, c, at):
             return r1[f, c, at, :]
 
-        @pl.loop(SOUTH, end + 1, unroll=UNROLL1)
+        for f, c, value in update(l, outside, first, True)[0]:
+            r1[f, c, rows(SOUTH), :] = value
+            r1[f, c, rows(end), :] = value
+
+        @pl.loop(OWN, end, unroll=UNROLL)
         def _(t):
-            for f, c, value in update(l, t, first):
+            values, u_west = update(l, tile(t), first, True)
+            for c in range(2):
+                uw[c, rows(t), :] = u_west[c]
+            for f, c, value in values:
                 r1[f, c, rows(t), :] = value
 
         def at_top(f, c, load):
@@ -293,9 +327,9 @@
                     r1[f, c, rows(end), :] += jnp.where(sub == 0, add, 0.0)
                     r1[f, c, rows(end - 1), :] += at_top(f, c, first)
 
-        @pl.loop(OWN, end, unroll=UNROLL2)
+        @pl.loop(OWN, end, unroll=UNROLL)
         def _(t):
-            for f, c, value in update(l, t, second):
+            for f, c, value in update(l, tile(t), second, False)[0]:
                 o_ref[f, l, rows(t - OWN), cols(c)] = value
 
         @pl.when(top)
@@ -314,25 +348,22 @@
     pair = lane // 2 % 8
 
     def join(t):
-        p, q = p_ref[rows(t), :], q_ref[rows(t), :]
+        p, q = p_ref[rows(t // 2), :], q_ref[rows(t // 2), :]
         from_west, from_east = jnp.where(lon_even, q, p), jnp.where(lon_even, p, q)
         out = []
-        for g in range(5):
-            back = (LANES - 2 * g) % LANES
-            west, east = (pltpu.roll(x, back, 1) if back else x for x in (from_west, from_east))
-            out.append(jnp.where(pair == 1, west, jnp.where(pair == 6, east, k_ref[g, rows(t), :])))
+        for g, (_, first) in enumerate(slots(lane)):
+            at = first + 8 * (t % 2)
+            west, east = turn(from_west, (2 if g < 3 else 3) - at), turn(from_east, 12 - at)
+            out.append((jnp.where(pair == 1, west, jnp.where(pair == 6, east, k_ref[g, rows(t), :])), east))
         return out
 
-    @pl.loop(0, tiles, unroll=True)
-    def _(t):
-        for g, value in enumerate(join(t)):
+    for t in range(tiles):
+        for g, (value, _) in enumerate(join(t)):
             z[g, rows(t + OWN), :] = value
 
     at_seam = partner_columns(c_ref, i_ref.shape[3])[1][:, LANES - 1 :] == 0
-    p, q = p_ref[rows(tiles), :], q_ref[rows(tiles), :]
-    for g, value in enumerate(join(tiles)):
+    for g, (value, crossed) in enumerate(join(tiles)):
         z[g, rows(SOUTH), :] = value
-        crossed = pltpu.roll(jnp.where(lon_even, p, q), (LANES - 2 * g) % LANES, 1) if g else jnp.where(lon_even, p, q)
         if g < 2:
             crossed = pltpu.roll(crossed, SUBS - 1, 0)
         kept = jnp.where((pair == 6) & at_seam, crossed, k_ref[g, rows(tiles), :])
@@ -366,7 +397,7 @@
         at = rows(t)
         return pltpu.make_async_copy(buf.at[:, :, at, :], o_ref.at[:, :, at, :], sems.at[t])
 
-    @pl.loop(0, tiles, unroll=UNROLL2)
+    @pl.loop(0, tiles, unroll=UNROLL)
     def _(t):
         value = update(t + OWN, lambda h, at: z1[h, at, :], False)
         value = [jnp.where(pair == 1, pltpu.roll(x, LANES - 8, 1), x) for x in value]
@@ -436,13 +467,13 @@
 
     tall = height + 4 * SUBS
     ext = [(fields * levels, 2, tall, LANES)] + [(levels, 2, tall, LANES)] * 3
-    pack = (height + SUBS, LANES)
-    laid = call(prepare_kernel, "prepare", inputs, (*ext, (5,) + pack, pack, pack))
+    pack, sides = (height + SUBS, LANES), (height // 2 + SUBS, LANES)
+    laid = call(prepare_kernel, "prepare", inputs, (*ext, (5,) + pack, sides, sides))
     *laid, to_p, to_q = call(
         halo_kernel,
         "place_rows",
         (from_a, from_b, *laid),
-        (*ext, (5,) + pack, pack, pack),
+        (*ext, (5,) + pack, sides, sides),
         [(2, message[0] + 2 * SUBS, LANES)] * 2,
         aliases={2 + i: i for i in range(7)},
     )
@@ -458,7 +489,7 @@
         [(4, message[0] + SUBS, LANES)],
         aliases={3 + i: i for i in range(5)},
     )
-    (inner,) = call(step_kernel, "both_steps", laid, (state_adjoint.shape,), [(fields, 2, tall, LANES)], micros=3)
+    (inner,) = call(step_kernel, "both_steps", laid, (state_adjoint.shape,), [(fields, 2, tall, LANES), (2, tall, LANES)], micros=3)
     return pl.pallas_call(
         edge_kernel,
         out_shape=jax.ShapeDtypeStruct(state_adjoint.shape, f32),

time: 15.6 us -> 15.4 us (0.987)
  Pallas kernels: 6.79 us -> 6.56 us
    pallas_call x4, Pallas kernels: 3.97 us -> 3.78 us  [call(): pl.pallas_call(kernel, out_shape=tuple((pltpu.VMEM(shape, f32) for shape...]
  transfers between devices with their start and end apart: 5 -> 5, of which waited for: 1 -> 1; matrix products, arithmetic and copies ran while one was open for 0% -> 0% of each run, Pallas kernels for 26% -> 25%
where the time goes in v7:
time: 15.4 us; the launch traced here: 15.1 us
  starting transfers between devices  8.22 us (53%)
  Pallas kernels  6.56 us (43%)
  waiting for transfers between devices  0.17 us (1%)
    ppermute x1, starting transfers between devices, per_device(): from_b = lax.ppermute(to_b, axes, across + fold)  4.06 us
    pallas_call x4, Pallas kernels, call(): pl.pallas_call(kernel, out_shape=tuple((pltpu.VMEM(shape, f32) for shape...  3.78 us
    ppermute x1, starting transfers between devices, per_device(): from_q = lax.ppermute(to_q, axes, odd)  2.75 us
    pallas_call x1, Pallas kernels, per_device(): pl.pallas_call(edge_kernel, out_shape=jax.ShapeDtypeStruct(state_adjoint....  1.51 us
    pallas_call x1, Pallas kernels, per_device(): pl.pallas_call(row_kernel, out_shape=(pltpu.VMEM(message, f32), pltpu.VME...  1.28 us
    ppermute x1, starting transfers between devices, per_device(): from_a = lax.ppermute(to_a, axes, within)  0.74 us
    ppermute x1, starting transfers between devices, per_device(): from_f = lax.ppermute(to_b, axes, fold_next)  0.66 us
  transfers between devices with their start and end apart: 5, of which 1 were waited for; matrix products, arithmetic and copies ran while one was open for 0% of the time, Pallas kernels for 25%

profile of v7, /device:TPU:25, one launch (start us, length us, event | category | flops | bytes accessed | tf_op | source)
XLA Modules:
  0.0 15.1 jit_solution(8994768756614016042)
XLA Ops:
  0.0 0.0 copy-start.3
  0.0 0.0 copy-start.2
  0.0 0.0 copy-start.1
  0.0 0.0 copy-start
  0.0 1.3 %pack_rows.1 = (f32[48,256]{1,0:T(8,128)S(1)}, f32[48,256]{1,0:T(8,128)S(1)}) custom-call(f32[4,4,64,256]{3,2,1,0:T(8,128)} %s_ref.1, f32[4,64,256]{2,1,0:T(8,128)} %u_ref.1, f32[4,64,256]{2,1,0:T(8,128)} %v_ref.1, s32[4,64,256]{2,1,0:T(8,128)} %m_ref.1), custom_call_target="tpu_custom_call" | custom-call | tf_op jit(solution)/shard_map/pack_rows/pallas_call | solution.py:454
  1.3 0.7 %collective-permute-start.2 = (f32[48,256]{1,0:T(8,128)S(1)}, f32[48,256]{1,0:T(8,128)S(1)}, u32[]{:S(2)}, u32[]{:S(2)}) collective-permute-start(f32[48,256]{1,0:T(8,128)S(1)} %get-tuple-element.27), channel_id=1, source_target_pairs={{0,1},{1,0},{2,3},{3,2},{4,5},{5,4},{6,7},{7,6},{8,9},{9,8},{10,11... | collective-permute-start | bytes 147464 | tf_op jit(solution)/shard_map/ppermute | solution.py:464
  2.0 4.1 %collective-permute-start = (f32[48,256]{1,0:T(8,128)S(1)}, f32[48,256]{1,0:T(8,128)S(1)}, u32[]{:S(2)}, u32[]{:S(2)}) collective-permute-start(f32[48,256]{1,0:T(8,128)S(1)} %get-tuple-element.26), channel_id=1, source_target_pairs={{1,2},{2,1},{3,4},{4,3},{5,6},{6,5},{9,10},{10,9},{11,12},{12,11},... | collective-permute-start | bytes 147464 | tf_op jit(solution)/shard_map/ppermute | solution.py:465
  6.1 0.7 %collective-permute-start.1 = (f32[48,256]{1,0:T(8,128)S(1)}, f32[48,256]{1,0:T(8,128)S(1)}, u32[]{:S(2)}, u32[]{:S(2)}) collective-permute-start(f32[48,256]{1,0:T(8,128)S(1)} %get-tuple-element.26), channel_id=1, source_target_pairs={{7,7},{31,15},{23,23},{15,31}} | collective-permute-start | bytes 147464 | tf_op jit(solution)/shard_map/ppermute | solution.py:466
  6.8 0.0 copy-done.3
  6.8 0.0 copy-done.2
  6.8 0.0 copy-done.1
  6.8 0.0 copy-done
  6.8 1.1 %prepare.1 = (f32[16,2,96,128]{3,2,1,0:T(8,128)S(1)}, f32[4,2,96,128]{3,2,1,0:T(8,128)S(1)}, f32[4,2,96,128]{3,2,1,0:T(8,128)S(1)}, f32[4,2,96,128]{3,2,1,0:T(8,...) custom-call(f32[4,4,64,256]{3,2,1,0:T(8,128)S(1)} %copy-done, ...), custom_call_target="tpu_custom_call" | custom-call | bytes 3000000 | tf_op jit(solution)/shard_map/prepare/pallas_call | solution.py:440
  7.9 0.0 copy-start.4
  7.9 0.0 collective-permute-done.2.a_ref
  8.0 0.0 collective-permute-done.b_ref
  8.0 0.2 %place_rows.1 = (f32[16,2,96,128]{3,2,1,0:T(8,128)S(1)}, f32[4,2,96,128]{3,2,1,0:T(8,128)S(1)}, f32[4,2,96,128]{3,2,1,0:T(8,128)S(1)}, f32[4,2,96,128]{3,2,1,0:T...) custom-call(f32[48,256]{1,0:T(8,128)S(1)} %collective-permute-done.2, ...), custom_call_target="tpu_custom_call", output_to_operand_aliasing={{0}: (2, {}), {1}: (3, {}), {2}: (4, {}), {3}: (5, {}), {4}... | custom-call | bytes 3000000 | tf_op jit(solution)/shard_map/place_rows/pallas_call | solution.py:440
  8.2 2.7 %collective-permute-start.3 = (f32[40,128]{1,0:T(8,128)S(1)}, f32[40,128]{1,0:T(8,128)S(1)}, u32[]{:S(2)}, u32[]{:S(2)}) collective-permute-start(f32[40,128]{1,0:T(8,128)S(1)} %get-tuple-element.41), channel_id=1, source_target_pairs={{8,16},{16,8},{9,17},{17,9},{10,18},{18,10},{11,19},{19,11},{12,20... | collective-permute-start | bytes 61448 | tf_op jit(solution)/shard_map/ppermute | solution.py:481
  11.0 0.0 collective-permute-start.4
  11.0 0.0 collective-permute-done.1.f_ref
  11.0 0.0 copy-done.4
  11.0 0.4 %mirror_rows.1 = (f32[16,2,96,128]{3,2,1,0:T(8,128)S(1)}, f32[4,2,96,128]{3,2,1,0:T(8,128)S(1)}, f32[4,2,96,128]{3,2,1,0:T(8,128)S(1)}, f32[4,2,96,128]{3,2,1,0:T(8,128)S(1)}, f32[5,72,128]{2,1,0:T(8,128)S(1)}) custom-call(s32[2,128]{1,0:T(2,128)S(1)} %bitcast.1, ...), custom_call_target="tpu_custom_call", output_to_operand_aliasing={{0}: (3, {}), {1}: (4, {}), {2}: (5, {}), {3}: (6, {}), {4}... | custom-call | bytes 3000000 | tf_op jit(solution)/shard_map/mirror_rows/pallas_call | solution.py:440
  11.4 2.0 %both_steps.1.i_ref = f32[4,4,64,256]{3,2,1,0:T(8,128)S(1)} custom-call(f32[16,2,96,128]{3,2,1,0:T(8,128)S(1)} %get-tuple-element.43.r_ref, f32[4,2,96,128]{3,2,1,0:T(8,128)S(1)} %get-tuple-element.44.u2_ref, f32[4,2,96,128]{3,2,1,0:T(8,128)S(1)} %get-tuple-element.45.v2_ref, f32[4,2,96,128]{3,2,1,0:T(8,128)S(1)} %get-tuple-element.46.w_ref), custom_call_target="tpu_custom_call" | custom-call | bytes 9000000 | tf_op jit(solution)/shard_map/both_steps/pallas_call | solution.py:440
  13.4 0.0 collective-permute-done.3.q_ref
  13.4 0.2 %collective-permute-done.4.p_ref = f32[40,128]{1,0:T(8,128)S(1)} collective-permute-done((f32[40,128]{1,0:T(8,128)S(1)}, f32[40,128]{1,0:T(8,128)S(1)}, u32[]{:S(2)}, u32[]{:S(2)}) %collective-permute-start.4) | collective-permute-done | bytes 20512 | tf_op jit(solution)/shard_map/ppermute | solution.py:480
  13.6 1.5 %edge_columns.1 = f32[4,4,64,256]{3,2,1,0:T(8,128)} custom-call(s32[2,128]{1,0:T(2,128)S(1)} %bitcast.2, f32[5,72,128]{2,1,0:T(8,128)S(1)} %get-tuple-element.40.k_ref, f32[40,128]{1,0:T(8,128)S(1)} %collective-permute-done.3.q_ref, f32[40,128]{1,0:T(8,128)S(1)} %collective-permute-done.4.p_ref, f32[4,4,64,256]{3,2,1,0:T(8,128)S(1)} %both_steps.1.i_ref), custom_call_target="tpu_custom_call" | custom-call | tf_op jit(solution)/shard_map/edge_columns/pallas_call | solution.py:493
Async XLA Ops:
  0.0 6.8 %copy-start.3 = (s32[4,64,256]{2,1,0:T(8,128)S(1)}, s32[4,64,256]{2,1,0:T(8,128)}, u32[]{:S(2)}) copy-start(s32[4,64,256]{2,1,0:T(8,128)} %m_ref.1) | copy-start | bytes 786436
  0.0 6.8 %copy-start.2 = (f32[4,64,256]{2,1,0:T(8,128)S(1)}, f32[4,64,256]{2,1,0:T(8,128)}, u32[]{:S(2)}) copy-start(f32[4,64,256]{2,1,0:T(8,128)} %v_ref.1) | copy-start | bytes 786436
  0.0 6.8 %copy-start.1 = (f32[4,64,256]{2,1,0:T(8,128)S(1)}, f32[4,64,256]{2,1,0:T(8,128)}, u32[]{:S(2)}) copy-start(f32[4,64,256]{2,1,0:T(8,128)} %u_ref.1) | copy-start | bytes 786436
  0.0 6.8 %copy-start = (f32[4,4,64,256]{3,2,1,0:T(8,128)S(1)}, f32[4,4,64,256]{3,2,1,0:T(8,128)}, u32[]{:S(2)}) copy-start(f32[4,4,64,256]{3,2,1,0:T(8,128)} %s_ref.1) | copy-start | bytes 3145732
  1.3 6.6 %collective-permute-start.2 = (f32[48,256]{1,0:T(8,128)S(1)}, f32[48,256]{1,0:T(8,128)S(1)}, u32[]{:S(2)}, u32[]{:S(2)}) collective-permute-start(f32[48,256]{1,0:T(8,128)S(1)} %get-tuple-element.27), channel_id=1, source_target_pairs={{0,1},{1,0},{2,3},{3,2},{4,5},{5,4},{6,7},{7,6},{8,9},{9,8},{10,11... | collective-permute-start | bytes 147464 | tf_op jit(solution)/shard_map/ppermute | solution.py:464
  2.0 5.9 %collective-permute-start = (f32[48,256]{1,0:T(8,128)S(1)}, f32[48,256]{1,0:T(8,128)S(1)}, u32[]{:S(2)}, u32[]{:S(2)}) collective-permute-start(f32[48,256]{1,0:T(8,128)S(1)} %get-tuple-element.26), channel_id=1, source_target_pairs={{1,2},{2,1},{3,4},{4,3},{5,6},{6,5},{9,10},{10,9},{11,12},{12,11},... | collective-permute-start | bytes 147464 | tf_op jit(solution)/shard_map/ppermute | solution.py:465
  6.1 4.8 %collective-permute-start.1 = (f32[48,256]{1,0:T(8,128)S(1)}, f32[48,256]{1,0:T(8,128)S(1)}, u32[]{:S(2)}, u32[]{:S(2)}) collective-permute-start(f32[48,256]{1,0:T(8,128)S(1)} %get-tuple-element.26), channel_id=1, source_target_pairs={{7,7},{31,15},{23,23},{15,31}} | collective-permute-start | bytes 147464 | tf_op jit(solution)/shard_map/ppermute | solution.py:466
  7.9 3.0 %copy-start.4 = (s32[256]{0:T(256)S(1)}, s32[256]{0:T(256)}, u32[]{:S(2)}) copy-start(s32[256]{0:T(256)} %param.9) | copy-start | bytes 3076
  8.2 5.2 %collective-permute-start.3 = (f32[40,128]{1,0:T(8,128)S(1)}, f32[40,128]{1,0:T(8,128)S(1)}, u32[]{:S(2)}, u32[]{:S(2)}) collective-permute-start(f32[40,128]{1,0:T(8,128)S(1)} %get-tuple-element.41), channel_id=1, source_target_pairs={{8,16},{16,8},{9,17},{17,9},{10,18},{18,10},{11,19},{19,11},{12,20... | collective-permute-start | bytes 61448 | tf_op jit(solution)/shard_map/ppermute | solution.py:481
  11.0 2.6 %collective-permute-start.4 = (f32[40,128]{1,0:T(8,128)S(1)}, f32[40,128]{1,0:T(8,128)S(1)}, u32[]{:S(2)}, u32[]{:S(2)}) collective-permute-start(f32[40,128]{1,0:T(8,128)S(1)} %get-tuple-element.42), channel_id=1, source_target_pairs={{0,8},{8,0},{1,9},{9,1},{2,10},{10,2},{3,11},{11,3},{4,12},{12,4},... | collective-permute-start | bytes 61448 | tf_op jit(solution)/shard_map/ppermute | solution.py:480

commit v8 on v7

--- a/solution.py
+++ b/solution.py
@@ -204,6 +204,10 @@
     width = b_ref.shape[1]
     tiles = k_ref.shape[1] // SUBS - 1
 
+    def pick(raw, which, p):
+        tile = jnp.where(which < 2, jnp.where(which < 1, raw[0], raw[1]), jnp.where(which < 3, raw[2], raw[3]))
+        return jnp.take_along_axis(tile, p % LANES, axis=1, mode="promise_in_bounds")
+
     @pl.when(top)
     def _():
         source = partner_columns(c_ref, width)
@@ -213,10 +217,10 @@
         for t in range(LEVELS + 2):
             raw = [(b_ref if s < 2 else f_ref)[rows(t), cols(s % 2)] for s in range(4)]
             for c, p in enumerate((*source, before, after)):
-                got = jnp.zeros((SUBS, LANES), jnp.float32)
-                for s in range(4):
-                    picked = jnp.take_along_axis(raw[s], p % LANES, axis=1, mode="promise_in_bounds")
-                    got = jnp.where(p // LANES == s, picked, got)
+                last = jnp.broadcast_to(p[:, :1] // LANES, (SUBS, LANES))
+                got = pick(raw, last, p)
+                if c < 2:
+                    got = jnp.where(p // LANES == last, got, pick(raw, last - 1, p))
                 if t < LEVELS:
                     got = jnp.where(sub % 2 == 0, pltpu.roll(got, SUBS - 1, 0), pltpu.roll(got, 1, 0))
                 elif t == LEVELS:
@@ -299,44 +303,32 @@
         def second(f, c, at):
             return r1[f, c, at, :]
 
+        def at_top(f, c, load):
+            v, v_mirror = v2_ref[l, c, rows(end - 1), :], v2_ref[l, c, rows(end - 1, 2), :]
+            r, r_mirror = load(f, c, rows(end - 1)), load(f, c, rows(end - 1, 1))
+            add = seam(r, r_mirror, v, v_mirror, w_ref[l, c, rows(end - 1), :], sign_of(f))
+            return jnp.where(top & (sub == SUBS - 1), add, 0.0)
+
+        def at_mirror(f, c):
+            v_top, v_mirror = v2_ref[l, c, rows(end, -1), :], v2_ref[l, c, rows(end, 1), :]
+            r, r_top = first(f, c, rows(end)), first(f, c, rows(end, -1))
+            add = seam_mirror(r, r_top, v_top, v_mirror, w_ref[l, c, rows(end), :], sign_of(f))
+            return jnp.where(top & (sub == 0), add, 0.0)
+
         for f, c, value in update(l, outside, first, True)[0]:
             r1[f, c, rows(SOUTH), :] = value
-            r1[f, c, rows(end), :] = value
-
-        @pl.loop(OWN, end, unroll=UNROLL)
-        def _(t):
+            r1[f, c, rows(end), :] = value + at_mirror(f, c)
+
+        for t in range(OWN, end):
             values, u_west = update(l, tile(t), first, True)
             for c in range(2):
                 uw[c, rows(t), :] = u_west[c]
             for f, c, value in values:
-                r1[f, c, rows(t), :] = value
-
-        def at_top(f, c, load):
-            v, v_mirror = v2_ref[l, c, rows(end - 1), :], v2_ref[l, c, rows(end - 1, 2), :]
-            r, r_mirror = load(f, c, rows(end - 1)), load(f, c, rows(end - 1, 1))
-            add = seam(r, r_mirror, v, v_mirror, w_ref[l, c, rows(end - 1), :], sign_of(f))
-            return jnp.where(sub == SUBS - 1, add, 0.0)
-
-        @pl.when(top)
-        def _():
-            for f in range(FIELDS):
-                for c in range(2):
-                    v_top, v_mirror = v2_ref[l, c, rows(end, -1), :], v2_ref[l, c, rows(end, 1), :]
-                    r, r_top = first(f, c, rows(end)), first(f, c, rows(end, -1))
-                    add = seam_mirror(r, r_top, v_top, v_mirror, w_ref[l, c, rows(end), :], sign_of(f))
-                    r1[f, c, rows(end), :] += jnp.where(sub == 0, add, 0.0)
-                    r1[f, c, rows(end - 1), :] += at_top(f, c, first)
-
-        @pl.loop(OWN, end, unroll=UNROLL)
-        def _(t):
+                r1[f, c, rows(t), :] = value + at_top(f, c, first) if t == end - 1 else value
+
+        for t in range(OWN, end):
             for f, c, value in update(l, tile(t), second, False)[0]:
-                o_ref[f, l, rows(t - OWN), cols(c)] = value
-
-        @pl.when(top)
-        def _():
-            for f in range(FIELDS):
-                for c in range(2):
-                    o_ref[f, l, rows(tiles - 1), cols(c)] += at_top(f, c, second)
+                o_ref[f, l, rows(t - OWN), cols(c)] = value + at_top(f, c, second) if t == end - 1 else value
 
 
 def edge_kernel(c_ref, k_ref, q_ref, p_ref, i_ref, o_ref, z, z1, buf, sems):

time: 15.4 us -> 15.3 us (level)
  waiting for transfers between devices: 0.17 us -> 0.61 us
  Pallas kernels: 6.56 us -> 6.13 us
    ppermute x1, waiting for transfers between devices: 0.16 us -> 0.6 us  [per_device(): from_p = lax.ppermute(to_p, axes, even)]
    pallas_call x4, Pallas kernels: 3.78 us -> 3.35 us  [call(): pl.pallas_call(kernel, out_shape=tuple((pltpu.VMEM(shape, f32) for shape...]
  transfers between devices with their start and end apart: 5 -> 5, of which waited for: 1 -> 1; matrix products, arithmetic and copies ran while one was open for 0% -> 0% of each run, Pallas kernels for 25% -> 22%
where the time goes in v8:
time: 15.3 us; the launch traced here: 15.1 us
  starting transfers between devices  8.22 us (54%)
  Pallas kernels  6.13 us (40%)
  waiting for transfers between devices  0.61 us (4%)
    ppermute x1, starting transfers between devices, per_device(): from_b = lax.ppermute(to_b, axes, across + fold)  4.06 us
    pallas_call x4, Pallas kernels, call(): pl.pallas_call(kernel, out_shape=tuple((pltpu.VMEM(shape, f32) for shape...  3.35 us
    ppermute x1, starting transfers between devices, per_device(): from_q = lax.ppermute(to_q, axes, odd)  2.75 us
    pallas_call x1, Pallas kernels, per_device(): pl.pallas_call(edge_kernel, out_shape=jax.ShapeDtypeStruct(state_adjoint....  1.51 us
    pallas_call x1, Pallas kernels, per_device(): pl.pallas_call(row_kernel, out_shape=(pltpu.VMEM(message, f32), pltpu.VME...  1.28 us
    ppermute x1, starting transfers between devices, per_device(): from_a = lax.ppermute(to_a, axes, within)  0.74 us
    ppermute x1, starting transfers between devices, per_device(): from_f = lax.ppermute(to_b, axes, fold_next)  0.66 us
    ppermute x1, waiting for transfers between devices, per_device(): from_p = lax.ppermute(to_p, axes, even)  0.6 us
  transfers between devices with their start and end apart: 5, of which 1 were waited for; matrix products, arithmetic and copies ran while one was open for 0% of the time, Pallas kernels for 22%

profile of v8, /device:TPU:25, one launch (start us, length us, event | category | flops | bytes accessed | tf_op | source)
XLA Modules:
  0.0 15.1 jit_solution(2032612051589881778)
XLA Ops:
  0.0 0.0 copy-start.3
  0.0 0.0 copy-start.2
  0.0 0.0 copy-start.1
  0.0 0.0 copy-start
  0.0 1.3 %pack_rows.1 = (f32[48,256]{1,0:T(8,128)S(1)}, f32[48,256]{1,0:T(8,128)S(1)}) custom-call(f32[4,4,64,256]{3,2,1,0:T(8,128)} %s_ref.1, f32[4,64,256]{2,1,0:T(8,128)} %u_ref.1, f32[4,64,256]{2,1,0:T(8,128)} %v_ref.1, s32[4,64,256]{2,1,0:T(8,128)} %m_ref.1), custom_call_target="tpu_custom_call" | custom-call | tf_op jit(solution)/shard_map/pack_rows/pallas_call | solution.py:446
  1.3 0.7 %collective-permute-start.2 = (f32[48,256]{1,0:T(8,128)S(1)}, f32[48,256]{1,0:T(8,128)S(1)}, u32[]{:S(2)}, u32[]{:S(2)}) collective-permute-start(f32[48,256]{1,0:T(8,128)S(1)} %get-tuple-element.27), channel_id=1, source_target_pairs={{0,1},{1,0},{2,3},{3,2},{4,5},{5,4},{6,7},{7,6},{8,9},{9,8},{10,11... | collective-permute-start | bytes 147464 | tf_op jit(solution)/shard_map/ppermute | solution.py:456
  2.0 4.1 %collective-permute-start = (f32[48,256]{1,0:T(8,128)S(1)}, f32[48,256]{1,0:T(8,128)S(1)}, u32[]{:S(2)}, u32[]{:S(2)}) collective-permute-start(f32[48,256]{1,0:T(8,128)S(1)} %get-tuple-element.26), channel_id=1, source_target_pairs={{1,2},{2,1},{3,4},{4,3},{5,6},{6,5},{9,10},{10,9},{11,12},{12,11},... | collective-permute-start | bytes 147464 | tf_op jit(solution)/shard_map/ppermute | solution.py:457
  6.1 0.7 %collective-permute-start.1 = (f32[48,256]{1,0:T(8,128)S(1)}, f32[48,256]{1,0:T(8,128)S(1)}, u32[]{:S(2)}, u32[]{:S(2)}) collective-permute-start(f32[48,256]{1,0:T(8,128)S(1)} %get-tuple-element.26), channel_id=1, source_target_pairs={{7,7},{31,15},{23,23},{15,31}} | collective-permute-start | bytes 147464 | tf_op jit(solution)/shard_map/ppermute | solution.py:458
  6.8 0.0 copy-done.3
  6.8 0.0 copy-done.2
  6.8 0.0 copy-done.1
  6.8 0.0 copy-done
  6.8 1.1 %prepare.1 = (f32[16,2,96,128]{3,2,1,0:T(8,128)S(1)}, f32[4,2,96,128]{3,2,1,0:T(8,128)S(1)}, f32[4,2,96,128]{3,2,1,0:T(8,128)S(1)}, f32[4,2,96,128]{3,2,1,0:T(8,...) custom-call(f32[4,4,64,256]{3,2,1,0:T(8,128)S(1)} %copy-done, ...), custom_call_target="tpu_custom_call" | custom-call | bytes 3000000 | tf_op jit(solution)/shard_map/prepare/pallas_call | solution.py:432
  7.9 0.0 copy-start.4
  7.9 0.0 collective-permute-done.2.a_ref
  8.0 0.0 collective-permute-done.b_ref
  8.0 0.2 %place_rows.1 = (f32[16,2,96,128]{3,2,1,0:T(8,128)S(1)}, f32[4,2,96,128]{3,2,1,0:T(8,128)S(1)}, f32[4,2,96,128]{3,2,1,0:T(8,128)S(1)}, f32[4,2,96,128]{3,2,1,0:T...) custom-call(f32[48,256]{1,0:T(8,128)S(1)} %collective-permute-done.2, ...), custom_call_target="tpu_custom_call", output_to_operand_aliasing={{0}: (2, {}), {1}: (3, {}), {2}: (4, {}), {3}: (5, {}), {4}... | custom-call | bytes 3000000 | tf_op jit(solution)/shard_map/place_rows/pallas_call | solution.py:432
  8.2 2.7 %collective-permute-start.3 = (f32[40,128]{1,0:T(8,128)S(1)}, f32[40,128]{1,0:T(8,128)S(1)}, u32[]{:S(2)}, u32[]{:S(2)}) collective-permute-start(f32[40,128]{1,0:T(8,128)S(1)} %get-tuple-element.41), channel_id=1, source_target_pairs={{8,16},{16,8},{9,17},{17,9},{10,18},{18,10},{11,19},{19,11},{12,20... | collective-permute-start | bytes 61448 | tf_op jit(solution)/shard_map/ppermute | solution.py:473
  11.0 0.0 collective-permute-start.4
  11.0 0.0 collective-permute-done.1.f_ref
  11.0 0.0 copy-done.4
  11.0 0.4 %mirror_rows.1 = (f32[16,2,96,128]{3,2,1,0:T(8,128)S(1)}, f32[4,2,96,128]{3,2,1,0:T(8,128)S(1)}, f32[4,2,96,128]{3,2,1,0:T(8,128)S(1)}, f32[4,2,96,128]{3,2,1,0:T(8,128)S(1)}, f32[5,72,128]{2,1,0:T(8,128)S(1)}) custom-call(s32[2,128]{1,0:T(2,128)S(1)} %bitcast.1, ...), custom_call_target="tpu_custom_call", output_to_operand_aliasing={{0}: (3, {}), {1}: (4, {}), {2}: (5, {}), {3}: (6, {}), {4}... | custom-call | bytes 3000000 | tf_op jit(solution)/shard_map/mirror_rows/pallas_call | solution.py:432
  11.4 1.6 %both_steps.1.i_ref = f32[4,4,64,256]{3,2,1,0:T(8,128)S(1)} custom-call(f32[16,2,96,128]{3,2,1,0:T(8,128)S(1)} %get-tuple-element.43.r_ref, f32[4,2,96,128]{3,2,1,0:T(8,128)S(1)} %get-tuple-element.44.u2_ref, f32[4,2,96,128]{3,2,1,0:T(8,128)S(1)} %get-tuple-element.45.v2_ref, f32[4,2,96,128]{3,2,1,0:T(8,128)S(1)} %get-tuple-element.46.w_ref), custom_call_target="tpu_custom_call" | custom-call | bytes 9000000 | tf_op jit(solution)/shard_map/both_steps/pallas_call | solution.py:432
  13.0 0.0 collective-permute-done.3.q_ref
  13.0 0.6 %collective-permute-done.4.p_ref = f32[40,128]{1,0:T(8,128)S(1)} collective-permute-done((f32[40,128]{1,0:T(8,128)S(1)}, f32[40,128]{1,0:T(8,128)S(1)}, u32[]{:S(2)}, u32[]{:S(2)}) %collective-permute-start.4) | collective-permute-done | bytes 20512 | tf_op jit(solution)/shard_map/ppermute | solution.py:472
  13.6 1.5 %edge_columns.1 = f32[4,4,64,256]{3,2,1,0:T(8,128)} custom-call(s32[2,128]{1,0:T(2,128)S(1)} %bitcast.2, f32[5,72,128]{2,1,0:T(8,128)S(1)} %get-tuple-element.40.k_ref, f32[40,128]{1,0:T(8,128)S(1)} %collective-permute-done.3.q_ref, f32[40,128]{1,0:T(8,128)S(1)} %collective-permute-done.4.p_ref, f32[4,4,64,256]{3,2,1,0:T(8,128)S(1)} %both_steps.1.i_ref), custom_call_target="tpu_custom_call" | custom-call | tf_op jit(solution)/shard_map/edge_columns/pallas_call | solution.py:485
Async XLA Ops:
  0.0 6.8 %copy-start.3 = (s32[4,64,256]{2,1,0:T(8,128)S(1)}, s32[4,64,256]{2,1,0:T(8,128)}, u32[]{:S(2)}) copy-start(s32[4,64,256]{2,1,0:T(8,128)} %m_ref.1) | copy-start | bytes 786436
  0.0 6.8 %copy-start.2 = (f32[4,64,256]{2,1,0:T(8,128)S(1)}, f32[4,64,256]{2,1,0:T(8,128)}, u32[]{:S(2)}) copy-start(f32[4,64,256]{2,1,0:T(8,128)} %v_ref.1) | copy-start | bytes 786436
  0.0 6.8 %copy-start.1 = (f32[4,64,256]{2,1,0:T(8,128)S(1)}, f32[4,64,256]{2,1,0:T(8,128)}, u32[]{:S(2)}) copy-start(f32[4,64,256]{2,1,0:T(8,128)} %u_ref.1) | copy-start | bytes 786436
  0.0 6.8 %copy-start = (f32[4,4,64,256]{3,2,1,0:T(8,128)S(1)}, f32[4,4,64,256]{3,2,1,0:T(8,128)}, u32[]{:S(2)}) copy-start(f32[4,4,64,256]{3,2,1,0:T(8,128)} %s_ref.1) | copy-start | bytes 3145732
  1.3 6.6 %collective-permute-start.2 = (f32[48,256]{1,0:T(8,128)S(1)}, f32[48,256]{1,0:T(8,128)S(1)}, u32[]{:S(2)}, u32[]{:S(2)}) collective-permute-start(f32[48,256]{1,0:T(8,128)S(1)} %get-tuple-element.27), channel_id=1, source_target_pairs={{0,1},{1,0},{2,3},{3,2},{4,5},{5,4},{6,7},{7,6},{8,9},{9,8},{10,11... | collective-permute-start | bytes 147464 | tf_op jit(solution)/shard_map/ppermute | solution.py:456
  2.0 5.9 %collective-permute-start = (f32[48,256]{1,0:T(8,128)S(1)}, f32[48,256]{1,0:T(8,128)S(1)}, u32[]{:S(2)}, u32[]{:S(2)}) collective-permute-start(f32[48,256]{1,0:T(8,128)S(1)} %get-tuple-element.26), channel_id=1, source_target_pairs={{1,2},{2,1},{3,4},{4,3},{5,6},{6,5},{9,10},{10,9},{11,12},{12,11},... | collective-permute-start | bytes 147464 | tf_op jit(solution)/shard_map/ppermute | solution.py:457
  6.1 4.8 %collective-permute-start.1 = (f32[48,256]{1,0:T(8,128)S(1)}, f32[48,256]{1,0:T(8,128)S(1)}, u32[]{:S(2)}, u32[]{:S(2)}) collective-permute-start(f32[48,256]{1,0:T(8,128)S(1)} %get-tuple-element.26), channel_id=1, source_target_pairs={{7,7},{31,15},{23,23},{15,31}} | collective-permute-start | bytes 147464 | tf_op jit(solution)/shard_map/ppermute | solution.py:458
  7.9 3.0 %copy-start.4 = (s32[256]{0:T(256)S(1)}, s32[256]{0:T(256)}, u32[]{:S(2)}) copy-start(s32[256]{0:T(256)} %param.9) | copy-start | bytes 3076
  8.2 4.8 %collective-permute-start.3 = (f32[40,128]{1,0:T(8,128)S(1)}, f32[40,128]{1,0:T(8,128)S(1)}, u32[]{:S(2)}, u32[]{:S(2)}) collective-permute-start(f32[40,128]{1,0:T(8,128)S(1)} %get-tuple-element.41), channel_id=1, source_target_pairs={{8,16},{16,8},{9,17},{17,9},{10,18},{18,10},{11,19},{19,11},{12,20... | collective-permute-start | bytes 61448 | tf_op jit(solution)/shard_map/ppermute | solution.py:473
  11.0 2.6 %collective-permute-start.4 = (f32[40,128]{1,0:T(8,128)S(1)}, f32[40,128]{1,0:T(8,128)S(1)}, u32[]{:S(2)}, u32[]{:S(2)}) collective-permute-start(f32[40,128]{1,0:T(8,128)S(1)} %get-tuple-element.42), channel_id=1, source_target_pairs={{0,8},{8,0},{1,9},{9,1},{2,10},{10,2},{3,11},{11,3},{4,12},{12,4},... | collective-permute-start | bytes 61448 | tf_op jit(solution)/shard_map/ppermute | solution.py:472

commit v9 on v8

--- a/solution.py
+++ b/solution.py
@@ -11,7 +11,6 @@
 SOUTH, OWN = 1, 2
 VMEM = pl.BlockSpec(memory_space=pltpu.VMEM)
 SCOPED = 4 << 20
-UNROLL = 8
 
 
 def iota(dim):
@@ -364,7 +363,7 @@
             value = jnp.where(top & (sub == 0), -pltpu.roll(value, LANES - 1, 1), value)
         z[g, rows(end), :] = value
 
-    def update(t, load, mirrored):
+    def update(t, load):
         u, v, v_south, w = z[2, rows(t), :], z[3, rows(t), :], z[3, rows(t, -1), :], z[4, rows(t), :]
         u_west = pltpu.roll(u, 1, 1)
         out = []
@@ -372,26 +371,25 @@
             r, r_north, r_south = load(h, rows(t)), load(h, rows(t, 1)), load(h, rows(t, -1))
             along = u * (pltpu.roll(r, LANES - 1, 1) - r) + u_west * (r - pltpu.roll(r, 1, 1))
             value = w * (r + along + v * (r_north - r) + v_south * (r - r_south))
-            add = seam(r, r_north, v, z[3, rows(t, 2), :], w, sign_of(2 * h))
-            value += jnp.where(top & (t == end - 1) & (sub == SUBS - 1), add, 0.0)
-            if mirrored:
+            if t == end - 1:
+                add = seam(r, r_north, v, z[3, rows(t, 2), :], w, sign_of(2 * h))
+                value += jnp.where(top & (sub == SUBS - 1), add, 0.0)
+            if t == end:
                 add = seam_mirror(r, r_south, v_south, z[3, rows(t, 1), :], w, sign_of(2 * h))
-                value += jnp.where(top & (t == end) & (sub == 0), add, 0.0)
+                value += jnp.where(top & (sub == 0), add, 0.0)
             out.append(value)
         return out
 
-    @pl.loop(SOUTH, end + 1, unroll=True)
-    def _(t):
-        for h, value in enumerate(update(t, lambda h, at: z[h, at, :], True)):
+    for t in range(SOUTH, end + 1):
+        for h, value in enumerate(update(t, lambda h, at: z[h, at, :])):
             z1[h, rows(t), :] = value
 
     def send(t):
         at = rows(t)
         return pltpu.make_async_copy(buf.at[:, :, at, :], o_ref.at[:, :, at, :], sems.at[t])
 
-    @pl.loop(0, tiles, unroll=UNROLL)
-    def _(t):
-        value = update(t + OWN, lambda h, at: z1[h, at, :], False)
+    for t in range(tiles):
+        value = update(t + OWN, lambda h, at: z1[h, at, :])
         value = [jnp.where(pair == 1, pltpu.roll(x, LANES - 8, 1), x) for x in value]
         for f in range(FIELDS):
             for l in range(LEVELS):

time: 15.3 us -> 15.3 us (level)
  no operation moved by 1% of the time
where the time goes in v9:
time: 15.3 us; the launch traced here: 15.1 us
  starting transfers between devices  8.22 us (54%)
  Pallas kernels  6.13 us (40%)
  waiting for transfers between devices  0.61 us (4%)
    ppermute x1, starting transfers between devices, per_device(): from_b = lax.ppermute(to_b, axes, across + fold)  4.06 us
    pallas_call x4, Pallas kernels, call(): pl.pallas_call(kernel, out_shape=tuple((pltpu.VMEM(shape, f32) for shape...  3.35 us
    ppermute x1, starting transfers between devices, per_device(): from_q = lax.ppermute(to_q, axes, odd)  2.75 us
    pallas_call x1, Pallas kernels, per_device(): pl.pallas_call(edge_kernel, out_shape=jax.ShapeDtypeStruct(state_adjoint....  1.51 us
    pallas_call x1, Pallas kernels, per_device(): pl.pallas_call(row_kernel, out_shape=(pltpu.VMEM(message, f32), pltpu.VME...  1.28 us
    ppermute x1, starting transfers between devices, per_device(): from_a = lax.ppermute(to_a, axes, within)  0.74 us
    ppermute x1, starting transfers between devices, per_device(): from_f = lax.ppermute(to_b, axes, fold_next)  0.66 us
    ppermute x1, waiting for transfers between devices, per_device(): from_p = lax.ppermute(to_p, axes, even)  0.6 us
  transfers between devices with their start and end apart: 5, of which 1 were waited for; matrix products, arithmetic and copies ran while one was open for 0% of the time, Pallas kernels for 22%

profile of v9, /device:TPU:25, one launch (start us, length us, event | category | flops | bytes accessed | tf_op | source)
XLA Modules:
  0.0 15.1 jit_solution(2032612051589881778)
XLA Ops:
  0.0 0.0 copy-start.3
  0.0 0.0 copy-start.2
  0.0 0.0 copy-start.1
  0.0 0.0 copy-start
  0.0 1.3 %pack_rows.1 = (f32[48,256]{1,0:T(8,128)S(1)}, f32[48,256]{1,0:T(8,128)S(1)}) custom-call(f32[4,4,64,256]{3,2,1,0:T(8,128)} %s_ref.1, f32[4,64,256]{2,1,0:T(8,128)} %u_ref.1, f32[4,64,256]{2,1,0:T(8,128)} %v_ref.1, s32[4,64,256]{2,1,0:T(8,128)} %m_ref.1), custom_call_target="tpu_custom_call" | custom-call | tf_op jit(solution)/shard_map/pack_rows/pallas_call | solution.py:444
  1.3 0.7 %collective-permute-start.2 = (f32[48,256]{1,0:T(8,128)S(1)}, f32[48,256]{1,0:T(8,128)S(1)}, u32[]{:S(2)}, u32[]{:S(2)}) collective-permute-start(f32[48,256]{1,0:T(8,128)S(1)} %get-tuple-element.27), channel_id=1, source_target_pairs={{0,1},{1,0},{2,3},{3,2},{4,5},{5,4},{6,7},{7,6},{8,9},{9,8},{10,11... | collective-permute-start | bytes 147464 | tf_op jit(solution)/shard_map/ppermute | solution.py:454
  2.0 4.1 %collective-permute-start = (f32[48,256]{1,0:T(8,128)S(1)}, f32[48,256]{1,0:T(8,128)S(1)}, u32[]{:S(2)}, u32[]{:S(2)}) collective-permute-start(f32[48,256]{1,0:T(8,128)S(1)} %get-tuple-element.26), channel_id=1, source_target_pairs={{1,2},{2,1},{3,4},{4,3},{5,6},{6,5},{9,10},{10,9},{11,12},{12,11},... | collective-permute-start | bytes 147464 | tf_op jit(solution)/shard_map/ppermute | solution.py:455
  6.1 0.7 %collective-permute-start.1 = (f32[48,256]{1,0:T(8,128)S(1)}, f32[48,256]{1,0:T(8,128)S(1)}, u32[]{:S(2)}, u32[]{:S(2)}) collective-permute-start(f32[48,256]{1,0:T(8,128)S(1)} %get-tuple-element.26), channel_id=1, source_target_pairs={{7,7},{31,15},{23,23},{15,31}} | collective-permute-start | bytes 147464 | tf_op jit(solution)/shard_map/ppermute | solution.py:456
  6.8 0.0 copy-done.3
  6.8 0.0 copy-done.2
  6.8 0.0 copy-done.1
  6.8 0.0 copy-done
  6.8 1.1 %prepare.1 = (f32[16,2,96,128]{3,2,1,0:T(8,128)S(1)}, f32[4,2,96,128]{3,2,1,0:T(8,128)S(1)}, f32[4,2,96,128]{3,2,1,0:T(8,128)S(1)}, f32[4,2,96,128]{3,2,1,0:T(8,...) custom-call(f32[4,4,64,256]{3,2,1,0:T(8,128)S(1)} %copy-done, ...), custom_call_target="tpu_custom_call" | custom-call | bytes 3000000 | tf_op jit(solution)/shard_map/prepare/pallas_call | solution.py:430
  7.9 0.0 copy-start.4
  7.9 0.0 collective-permute-done.2.a_ref
  8.0 0.0 collective-permute-done.b_ref
  8.0 0.2 %place_rows.1 = (f32[16,2,96,128]{3,2,1,0:T(8,128)S(1)}, f32[4,2,96,128]{3,2,1,0:T(8,128)S(1)}, f32[4,2,96,128]{3,2,1,0:T(8,128)S(1)}, f32[4,2,96,128]{3,2,1,0:T...) custom-call(f32[48,256]{1,0:T(8,128)S(1)} %collective-permute-done.2, ...), custom_call_target="tpu_custom_call", output_to_operand_aliasing={{0}: (2, {}), {1}: (3, {}), {2}: (4, {}), {3}: (5, {}), {4}... | custom-call | bytes 3000000 | tf_op jit(solution)/shard_map/place_rows/pallas_call | solution.py:430
  8.2 2.7 %collective-permute-start.3 = (f32[40,128]{1,0:T(8,128)S(1)}, f32[40,128]{1,0:T(8,128)S(1)}, u32[]{:S(2)}, u32[]{:S(2)}) collective-permute-start(f32[40,128]{1,0:T(8,128)S(1)} %get-tuple-element.41), channel_id=1, source_target_pairs={{8,16},{16,8},{9,17},{17,9},{10,18},{18,10},{11,19},{19,11},{12,20... | collective-permute-start | bytes 61448 | tf_op jit(solution)/shard_map/ppermute | solution.py:471
  11.0 0.0 collective-permute-start.4
  11.0 0.0 collective-permute-done.1.f_ref
  11.0 0.0 copy-done.4
  11.0 0.4 %mirror_rows.1 = (f32[16,2,96,128]{3,2,1,0:T(8,128)S(1)}, f32[4,2,96,128]{3,2,1,0:T(8,128)S(1)}, f32[4,2,96,128]{3,2,1,0:T(8,128)S(1)}, f32[4,2,96,128]{3,2,1,0:T(8,128)S(1)}, f32[5,72,128]{2,1,0:T(8,128)S(1)}) custom-call(s32[2,128]{1,0:T(2,128)S(1)} %bitcast.1, ...), custom_call_target="tpu_custom_call", output_to_operand_aliasing={{0}: (3, {}), {1}: (4, {}), {2}: (5, {}), {3}: (6, {}), {4}... | custom-call | bytes 3000000 | tf_op jit(solution)/shard_map/mirror_rows/pallas_call | solution.py:430
  11.4 1.6 %both_steps.1.i_ref = f32[4,4,64,256]{3,2,1,0:T(8,128)S(1)} custom-call(f32[16,2,96,128]{3,2,1,0:T(8,128)S(1)} %get-tuple-element.43.r_ref, f32[4,2,96,128]{3,2,1,0:T(8,128)S(1)} %get-tuple-element.44.u2_ref, f32[4,2,96,128]{3,2,1,0:T(8,128)S(1)} %get-tuple-element.45.v2_ref, f32[4,2,96,128]{3,2,1,0:T(8,128)S(1)} %get-tuple-element.46.w_ref), custom_call_target="tpu_custom_call" | custom-call | bytes 9000000 | tf_op jit(solution)/shard_map/both_steps/pallas_call | solution.py:430
  13.0 0.0 collective-permute-done.3.q_ref
  13.0 0.6 %collective-permute-done.4.p_ref = f32[40,128]{1,0:T(8,128)S(1)} collective-permute-done((f32[40,128]{1,0:T(8,128)S(1)}, f32[40,128]{1,0:T(8,128)S(1)}, u32[]{:S(2)}, u32[]{:S(2)}) %collective-permute-start.4) | collective-permute-done | bytes 20512 | tf_op jit(solution)/shard_map/ppermute | solution.py:470
  13.6 1.5 %edge_columns.1 = f32[4,4,64,256]{3,2,1,0:T(8,128)} custom-call(s32[2,128]{1,0:T(2,128)S(1)} %bitcast.2, f32[5,72,128]{2,1,0:T(8,128)S(1)} %get-tuple-element.40.k_ref, f32[40,128]{1,0:T(8,128)S(1)} %collective-permute-done.3.q_ref, f32[40,128]{1,0:T(8,128)S(1)} %collective-permute-done.4.p_ref, f32[4,4,64,256]{3,2,1,0:T(8,128)S(1)} %both_steps.1.i_ref), custom_call_target="tpu_custom_call" | custom-call | tf_op jit(solution)/shard_map/edge_columns/pallas_call | solution.py:483
Async XLA Ops:
  0.0 6.8 %copy-start.3 = (s32[4,64,256]{2,1,0:T(8,128)S(1)}, s32[4,64,256]{2,1,0:T(8,128)}, u32[]{:S(2)}) copy-start(s32[4,64,256]{2,1,0:T(8,128)} %m_ref.1) | copy-start | bytes 786436
  0.0 6.8 %copy-start.2 = (f32[4,64,256]{2,1,0:T(8,128)S(1)}, f32[4,64,256]{2,1,0:T(8,128)}, u32[]{:S(2)}) copy-start(f32[4,64,256]{2,1,0:T(8,128)} %v_ref.1) | copy-start | bytes 786436
  0.0 6.8 %copy-start.1 = (f32[4,64,256]{2,1,0:T(8,128)S(1)}, f32[4,64,256]{2,1,0:T(8,128)}, u32[]{:S(2)}) copy-start(f32[4,64,256]{2,1,0:T(8,128)} %u_ref.1) | copy-start | bytes 786436
  0.0 6.8 %copy-start = (f32[4,4,64,256]{3,2,1,0:T(8,128)S(1)}, f32[4,4,64,256]{3,2,1,0:T(8,128)}, u32[]{:S(2)}) copy-start(f32[4,4,64,256]{3,2,1,0:T(8,128)} %s_ref.1) | copy-start | bytes 3145732
  1.3 6.6 %collective-permute-start.2 = (f32[48,256]{1,0:T(8,128)S(1)}, f32[48,256]{1,0:T(8,128)S(1)}, u32[]{:S(2)}, u32[]{:S(2)}) collective-permute-start(f32[48,256]{1,0:T(8,128)S(1)} %get-tuple-element.27), channel_id=1, source_target_pairs={{0,1},{1,0},{2,3},{3,2},{4,5},{5,4},{6,7},{7,6},{8,9},{9,8},{10,11... | collective-permute-start | bytes 147464 | tf_op jit(solution)/shard_map/ppermute | solution.py:454
  2.0 5.9 %collective-permute-start = (f32[48,256]{1,0:T(8,128)S(1)}, f32[48,256]{1,0:T(8,128)S(1)}, u32[]{:S(2)}, u32[]{:S(2)}) collective-permute-start(f32[48,256]{1,0:T(8,128)S(1)} %get-tuple-element.26), channel_id=1, source_target_pairs={{1,2},{2,1},{3,4},{4,3},{5,6},{6,5},{9,10},{10,9},{11,12},{12,11},... | collective-permute-start | bytes 147464 | tf_op jit(solution)/shard_map/ppermute | solution.py:455
  6.1 4.8 %collective-permute-start.1 = (f32[48,256]{1,0:T(8,128)S(1)}, f32[48,256]{1,0:T(8,128)S(1)}, u32[]{:S(2)}, u32[]{:S(2)}) collective-permute-start(f32[48,256]{1,0:T(8,128)S(1)} %get-tuple-element.26), channel_id=1, source_target_pairs={{7,7},{31,15},{23,23},{15,31}} | collective-permute-start | bytes 147464 | tf_op jit(solution)/shard_map/ppermute | solution.py:456
  7.9 3.0 %copy-start.4 = (s32[256]{0:T(256)S(1)}, s32[256]{0:T(256)}, u32[]{:S(2)}) copy-start(s32[256]{0:T(256)} %param.9) | copy-start | bytes 3076
  8.2 4.8 %collective-permute-start.3 = (f32[40,128]{1,0:T(8,128)S(1)}, f32[40,128]{1,0:T(8,128)S(1)}, u32[]{:S(2)}, u32[]{:S(2)}) collective-permute-start(f32[40,128]{1,0:T(8,128)S(1)} %get-tuple-element.41), channel_id=1, source_target_pairs={{8,16},{16,8},{9,17},{17,9},{10,18},{18,10},{11,19},{19,11},{12,20... | collective-permute-start | bytes 61448 | tf_op jit(solution)/shard_map/ppermute | solution.py:471
  11.0 2.6 %collective-permute-start.4 = (f32[40,128]{1,0:T(8,128)S(1)}, f32[40,128]{1,0:T(8,128)S(1)}, u32[]{:S(2)}, u32[]{:S(2)}) collective-permute-start(f32[40,128]{1,0:T(8,128)S(1)} %get-tuple-element.42), channel_id=1, source_target_pairs={{0,8},{8,0},{1,9},{9,1},{2,10},{10,2},{3,11},{11,3},{4,12},{12,4},... | collective-permute-start | bytes 61448 | tf_op jit(solution)/shard_map/ppermute | solution.py:470
